TPU v7x, 32 devices: a whole 2x2x4 slice. The times are simulated.
32 devices in a mesh: seq: 4 (over y, core), tp: 8 (over z, x).
Axes of the slice: x: 2, y: 2, z: 4, core: 2. Of those that a mesh axis runs over, the one named last changes fastest.
Arguments:
- tokens: bfloat16 [2048, 8192], P('seq', 'tp'), may hold values from -6 to 6
- w_query: bfloat16 [8192, 6144], P(None, 'tp'), may hold values from -0.0625 to 0.0625
- w_key: bfloat16 [8192, 6144], P(None, 'tp'), may hold values from -0.0625 to 0.0625
- w_value: bfloat16 [8192, 6144], P(None, 'tp'), may hold values from -0.0625 to 0.0625
- w_out: bfloat16 [6144, 8192], P('tp'), may hold values from -0.109375 to 0.109375
- carry: float32 [48, 128, 128], P('tp'), may hold values from -40 to 40
Outputs:
- mixed: bfloat16 [2048, 8192], P('seq', 'tp')
All inputs are finite; a program needn't handle non-finite values.
Results may differ from a plain program's by a relative error of at most 0.0066.
Values may be sent and summed in bfloat16 or wider, within the bound.
No kernel may reach another device: no remote copies, remote signals or barrier semaphores. Data moves between devices by JAX's collectives and lax.ppermute only.
A program may use at most 192 MiB of HBM per device.

v0:
```python
import jax
import jax.numpy as jnp
from jax import lax
from jax.sharding import PartitionSpec as P

EPSILON = 1e-05


def entering(array, axis, combine, identity):
    count, place = (lax.axis_size(axis), lax.axis_index(axis))
    everything = lax.all_gather(array, axis)
    start = jnp.broadcast_to(jnp.asarray(identity, array.dtype), array.shape)

    def turn(k, before):
        reached = k < place
        new = combine(before, everything[k])
        return jnp.where(reached, new, before)

    return lax.fori_loop(0, count, turn, start)


def combine_states(earlier, latter_part):
    return earlier + latter_part


def local(tokens, w_query, w_key, w_value, w_out, carry):
    row_count = tokens.shape[0]
    head_count = carry.shape[0]
    head_size = carry.shape[1]
    proj_width = w_query.shape[1]
    segment = lax.all_gather(tokens, "tp", axis=1, tiled=True)
    query_sum = jnp.dot(segment, w_query, preferred_element_type=jnp.float32)
    key_sum = jnp.dot(segment, w_key, preferred_element_type=jnp.float32)
    value_sum = jnp.dot(segment, w_value, preferred_element_type=jnp.float32)
    query = query_sum.astype(jnp.bfloat16).reshape(row_count, head_count, head_size)
    keys_local = key_sum.astype(jnp.bfloat16).reshape(row_count, head_count, head_size)
    values_local = value_sum.astype(jnp.bfloat16).reshape(row_count, head_count, head_size)
    local_state = jnp.einsum(
        "thd,the->hde", keys_local, values_local, preferred_element_type=jnp.float32
    )
    earlier_sum = entering(local_state, "seq", combine_states, jnp.zeros_like(local_state))
    prior = carry + earlier_sum
    across = jnp.einsum(
        "thd,hde->the", query.astype(jnp.float32), prior, precision=lax.Precision.HIGHEST
    )
    causal = lax.broadcasted_iota(jnp.int32, (row_count, row_count), 0) >= lax.broadcasted_iota(
        jnp.int32, (row_count, row_count), 1
    )
    scores = jnp.einsum("thd,shd->hts", query, keys_local, preferred_element_type=jnp.float32)
    scores = jnp.where(causal[None], scores, 0.0).astype(jnp.bfloat16)
    within = jnp.einsum("hts,she->the", scores, values_local, preferred_element_type=jnp.float32)
    total = across + within
    normed = total * lax.rsqrt(jnp.mean(total * total, axis=-1, keepdims=True) + EPSILON)
    attended = normed.astype(jnp.bfloat16).reshape(row_count, proj_width)
    summed = lax.psum_scatter(
        lax.dot_general(
            w_out, attended, (((0,), (1,)), ((), ())), preferred_element_type=jnp.float32
        ),
        "tp",
        scatter_dimension=0,
        tiled=True,
    )
    return summed.T.astype(jnp.bfloat16)


def solution(mesh):
    placed = (
        P("seq", "tp"),
        P(None, "tp"),
        P(None, "tp"),
        P(None, "tp"),
        P("tp", None),
        P("tp", None, None),
    )
    return jax.shard_map(
        local, mesh=mesh, in_specs=placed, out_specs=P("seq", "tp"), check_vma=False
    )
```

profile of v0, /device:TPU:0, one launch (start us, length us, event | category | flops | bytes accessed | tf_op | source)
XLA Modules:
  0.0 496.5 jit_solution(3666014107982523729)
XLA Ops:
  6.5 0.0 all-gather.4.cloned.1.call-start
  6.5 0.7 all-gather.4.cloned.1.call-update
  7.3 0.0 all-gather.6.cloned.1.call-start
  7.3 129.9 %all-gather.4.cloned.1.call-done = bf16[512,8192]{1,0:T(8,128)(2,1)} async-done(((bf16[512,1024]{1,0:T(8,128)(2,1)}), bf16[512,8192]{1,0:T(8,128)(2,1)}) %all-gather.4.cloned.1.call-update) | async-done | bytes 8388624 | tf_op jit(solution)/shard_map/all_gather | solution.py:31
  137.2 12.7 %convolution_convert_fusion.2 = bf16[512,768]{1,0:T(8,128)(2,1)S(1)} fusion(bf16[512,8192]{1,0:T(8,128)(2,1)} %all-gather.4.cloned.1.call-done, bf16[8192,768]{1,0:T(8,128)(2,1)} %param.10), kind=kOutput, calls=%fused_computation.14 | convolution fusion | flops 6442844160 | bytes 21757952 | tf_op jit(solution)/shard_map/dot_general | solution.py:33
  149.9 0.3 copy.18
  150.2 12.7 %convolution_convert_fusion.1 = bf16[512,768]{1,0:T(8,128)(2,1)S(1)} fusion(bf16[512,8192]{1,0:T(8,128)(2,1)} %all-gather.4.cloned.1.call-done, bf16[8192,768]{1,0:T(8,128)(2,1)} %param.11), kind=kOutput, calls=%fused_computation.13 | convolution fusion | flops 6442844160 | bytes 21757952 | tf_op jit(solution)/shard_map/dot_general | solution.py:34
  162.9 0.3 copy.19
  163.2 1.1 fusion.9
  164.3 0.0 all-gather.6.cloned.1.call-update
  164.3 0.2 reduce-scatter.2.cloned.1.call-start
  164.6 0.8 iota_compare_fusion
  165.3 13.2 %convolution_convert_fusion = bf16[512,768]{1,0:T(8,128)(2,1)S(1)} fusion(bf16[512,8192]{1,0:T(8,128)(2,1)} %all-gather.4.cloned.1.call-done, bf16[8192,768]{1,0:T(8,128)(2,1)} %param.9), kind=kOutput, calls=%fused_computation.12 | convolution fusion | flops 6442844160 | bytes 21757952 | tf_op jit(solution)/shard_map/dot_general | solution.py:32
  178.6 0.3 copy.21
  178.9 0.0 copy-start
  178.9 4.2 fusion
  183.1 0.0 all-gather.6.cloned.1.call-done
  183.1 4.6 while.14
  183.1 1.1 add_select_fusion.2
  184.2 1.1 add_select_fusion.2
  185.4 1.1 add_select_fusion.2
  186.5 1.1 add_select_fusion.2
  187.7 0.0 copy-done
  187.7 2.4 fusion.5
  190.1 0.2 fusion.6
  190.3 14.8 %convolution_bitcast_fusion = f32[8192,512]{0,1:T(8,128)} fusion(bf16[512,768]{0,1:T(8,128)(2,1)S(1)} %bitcast.34, bf16[768,8192]{1,0:T(8,128)(2,1)} %param.12), kind=kOutput, calls=%fused_computation.1 | convolution fusion | flops 6442450944 | bytes 30146560 | tf_op jit(solution)/shard_map/dot_general | solution.py:56
  205.1 0.0 reduce-scatter.2.cloned.1.call-update
  205.1 282.1 %reduce-scatter.2.cloned.1.call-done = f32[1024,512]{0,1:T(8,128)} async-done(((f32[8192,512]{0,1:T(8,128)}), f32[1024,512]{0,1:T(8,128)}) %reduce-scatter.2.cloned.1.call-update) | async-done | bytes 2097168 | tf_op jit(solution)/shard_map/reduce_scatter | solution.py:55
  487.2 2.7 convert_bitcast_fusion
  (2 shorter events, 0.0 us)
Async XLA Ops:
  6.5 130.7 %all-gather.4.cloned.1.call-start = ((), (), s32[]{:S(2)}) async-start(), calls=%async_computation.1 | async-start | bytes 9437184 | tf_op jit(solution)/shard_map/all_gather | solution.py:31
  7.3 175.8 %all-gather.6.cloned.1.call-start = ((), (), s32[]{:S(2)}) async-start(), calls=%async_computation.3 | async-start | bytes 1966080 | tf_op jit(solution)/shard_map/all_gather | solution.py:11
  164.3 322.9 %reduce-scatter.2.cloned.1.call-start = ((), (), s32[]{:S(2)}) async-start(), calls=%async_computation.2 | async-start | bytes 18874368 | tf_op jit(solution)/shard_map/reduce_scatter | solution.py:55
  178.9 8.8 %copy-start = (f32[6,128,128]{2,1,0:T(8,128)S(1)}, f32[6,128,128]{2,1,0:T(8,128)}, u32[]{:S(2)}) copy-start(f32[6,128,128]{2,1,0:T(8,128)} %param.13) | copy-start | bytes 1179652
Sparse Core Ops, SparseCore 0:
  9.5 127.5 all-gather.3
  164.4 17.8 all-gather.5
  205.2 281.9 reduce-scatter.1
where the time goes:
time: 497 us; the launch traced here: 496 us
  waiting for transfers between devices  413 us (83%)
  matrix products  61.1 us (12%)
  between operations  13.2 us (3%)
  other arithmetic  8.24 us (2%)
    reduce_scatter x1, waiting for transfers between devices, local(): lax.psum_scatter(lax.dot_general(w_out, attended, (((0,), (1,)), ((), ())...  282 us
    all_gather x1, waiting for transfers between devices, local(): segment = lax.all_gather(tokens, 'tp', axis=1, tiled=True)  130 us
    dot_general x1, matrix products, local(): lax.dot_general(w_out, attended, (((0,), (1,)), ((), ())), preferred_elem...  14.8 us
    dot_general x1, matrix products, local(): query_sum = jnp.dot(segment, w_query, preferred_element_type=jnp.float32)  13.2 us
    dot_general x1, matrix products, local(): key_sum = jnp.dot(segment, w_key, preferred_element_type=jnp.float32)  12.7 us
    dot_general x1, matrix products, local(): value_sum = jnp.dot(segment, w_value, preferred_element_type=jnp.float32)  12.7 us
  transfers between devices with their start and end apart: 3, of which 2 were waited for; matrix products, arithmetic and copies ran while one was open for 4% of the time, Pallas kernels for 0%

commit v1 on v0

v1 whole, which is shorter than its diff:
```python
import functools

import jax
import jax.numpy as jnp
from jax import lax
from jax.experimental import pallas as pl
from jax.experimental.pallas import tpu as pltpu
from jax.sharding import PartitionSpec as P

EPSILON = 1e-05
BF16 = jnp.bfloat16
F32 = jnp.float32
PROJECT_BYTES = 34 << 20


def ring_order(count):
    columns = 1
    while columns * columns * 4 <= count:
        columns *= 2
    rows = count // columns
    if rows % 2 or columns < 2:
        return list(range(count))
    order = [row * columns for row in range(rows)]
    for step, row in enumerate(reversed(range(rows))):
        span = range(1, columns) if step % 2 == 0 else range(columns - 1, 0, -1)
        order += [row * columns + column for column in span]
    return order


def lookup(table, index):
    value = jnp.int32(table[0])
    for i, entry in enumerate(table[1:], 1):
        value = jnp.where(index == i, jnp.int32(entry), value)
    return value


def cut_at(array, start, size, axis):
    starts = [jnp.int32(0), jnp.int32(0)]
    sizes = list(array.shape)
    starts[axis], sizes[axis] = start, size
    return lax.dynamic_slice(array, starts, sizes, allow_negative_indices=False)


def dot(a, b):
    return jnp.dot(a, b, preferred_element_type=F32)


def dot_rows(a, b):
    return lax.dot_general(a, b, (((0,), (0,)), ((), ())), preferred_element_type=F32)


def dot_columns(a, b):
    return lax.dot_general(a, b, (((1,), (1,)), ((), ())), preferred_element_type=F32)


def kernel(body, inputs, outputs, aliases=None, scratch=(), vmem=16 << 20):
    return pl.pallas_call(
        body,
        in_specs=[pl.BlockSpec(memory_space=space) for _, space in inputs],
        out_specs=[pl.BlockSpec(memory_space=pltpu.VMEM) for _ in outputs],
        out_shape=[jax.ShapeDtypeStruct(shape, kind) for shape, kind in outputs],
        scratch_shapes=list(scratch),
        input_output_aliases=aliases or {},
        compiler_params=pltpu.CompilerParams(vmem_limit_bytes=vmem),
        cost_estimate=pl.CostEstimate(flops=0, bytes_accessed=1 << 20, transcendentals=0),
    )(*[array for array, _ in inputs])


def columns_of(j, block):
    return pl.ds(pl.multiple_of(j * block, block), block)


def project_body(pieces, has_sums, has_rows, block, place, next_place, has_columns, *refs):
    starts, xs, refs = refs[0], refs[1 : 1 + pieces], refs[1 + pieces :]
    weights, refs = refs[:3], refs[3:]
    if has_columns:
        (w_out, column_starts), refs = refs[:2], refs[2:]
    held, refs = (refs[:3], refs[3:]) if has_rows else (None, refs)
    sums, refs = (refs[:3], refs[3:]) if has_sums else (None, refs)
    outs, wanted, refs = refs[:3], refs[3:6], refs[6:]
    depth = xs[0].shape[1]

    def rows_to(k, targets, semaphores):
        rows = pl.ds(pl.multiple_of(starts[k], depth), depth)
        return [
            pltpu.make_async_copy(weights[i].at[rows, :], targets[i], semaphores.at[i])
            for i in range(3)
        ]

    brought = []
    if has_columns:
        target, refs = refs[0], refs[1:]
        size = target.shape[1]
        cut = pl.ds(pl.multiple_of(column_starts[next_place], size), size)
        brought.append(pltpu.make_async_copy(w_out.at[:, cut], target, refs[0].at[3]))
    brought = rows_to(next_place, wanted, refs[0]) + brought
    copies = []
    if not has_rows:
        held = refs[1:4]
        copies = rows_to(place, held, refs[4])
    for copy in (*copies, *brought):
        copy.start()
    chunk = jnp.concatenate([x[...] for x in xs], 0)
    for i in range(3):
        if copies:
            copies[i].wait()

        @pl.loop(0, outs[0].shape[1] // block)
        def _(j, i=i):
            cut = columns_of(j, block)
            part = dot(chunk, held[i][:, cut])
            outs[i][:, cut] = part if sums is None else sums[i][:, cut] + part

    for bring in brought:
        bring.wait()


def project(chunk, starts, place, weights, held, sums, block, next_place, extra=None):
    rows = sum(piece.shape[0] for piece in chunk)
    depth, width = chunk[0].shape[1], weights[0].shape[1]
    inputs = [(starts, pltpu.SMEM)] + [(array, pltpu.VMEM) for array in chunk]
    inputs += [(weight, pltpu.HBM) for weight in weights]
    outputs = [((rows, width), F32)] * 3 + [((depth, width), BF16)] * 3
    scratch = [pltpu.SemaphoreType.DMA((4,))]
    if extra is not None:
        w_out, column_starts, columns = extra
        inputs += [(w_out, pltpu.HBM), (column_starts, pltpu.SMEM)]
        outputs += [((w_out.shape[0], columns), BF16)]
    if held is None:
        scratch += [pltpu.VMEM((depth, width), BF16)] * 3 + [pltpu.SemaphoreType.DMA((3,))]
    else:
        inputs += [(weight, pltpu.VMEM) for weight in held]
    aliases = {}
    if sums is not None:
        aliases = {len(inputs) + i: i for i in range(3)}
        inputs += [(s, pltpu.VMEM) for s in sums]
    body = functools.partial(
        project_body,
        len(chunk),
        sums is not None,
        held is not None,
        block,
        place,
        next_place,
        extra is not None,
    )
    out = kernel(body, inputs, outputs, aliases, scratch, PROJECT_BYTES)
    return out[:3], out[3:]


def keys_body(pieces, size, block, *refs):
    xs = refs[:pieces]
    w_key, w_value, key_sum, value_sum, keys_out, values_out, state_out = refs[pieces:]
    heads = block // size
    chunk = jnp.concatenate([x[...] for x in xs], 0)

    @pl.loop(0, keys_out.shape[1] // block)
    def _(j):
        cut = columns_of(j, block)
        keys = (key_sum[:, cut] + dot(chunk, w_key[:, cut])).astype(BF16)
        keys_out[:, cut] = keys
        values = (value_sum[:, cut] + dot(chunk, w_value[:, cut])).astype(BF16)
        values_out[:, cut] = values
        for h in range(heads):
            own = slice(h * size, (h + 1) * size)
            state_out[j * heads + h] = dot_rows(keys[:, own], values[:, own])


def finish_keys(chunk, w_key, w_value, key_sum, value_sum, block, size):
    rows, width = key_sum.shape
    arrays = (*chunk, w_key, w_value, key_sum, value_sum)
    outputs = [((rows, width), BF16)] * 2 + [((width // size, size, size), F32)]
    body = functools.partial(keys_body, len(chunk), size, block)
    return kernel(body, [(array, pltpu.VMEM) for array in arrays], outputs)


def within_body(pieces, size, block, *refs):
    xs = refs[:pieces]
    w_query, query_sum, keys_in, values_in, query_out, within_out = refs[pieces:]
    rows, width = query_sum.shape
    chunk = jnp.concatenate([x[...] for x in xs], 0)
    tile = rows // 2
    causal = lax.broadcasted_iota(jnp.int32, (tile, tile), 0) >= lax.broadcasted_iota(
        jnp.int32, (tile, tile), 1
    )

    @pl.loop(0, width // block)
    def _(j):
        cut = columns_of(j, block)
        query = (query_sum[:, cut] + dot(chunk, w_query[:, cut])).astype(BF16)
        query_out[:, cut] = query
        keys, values = keys_in[:, cut], values_in[:, cut]
        sums = []
        for h in range(block // size):
            own = slice(h * size, (h + 1) * size)
            q, k, v = query[:, own], keys[:, own], values[:, own]
            first = jnp.where(causal, dot_columns(q[:tile], k[:tile]), 0.0).astype(BF16)
            lower = dot_columns(q[tile:], k[:tile]).astype(BF16)
            second = jnp.where(causal, dot_columns(q[tile:], k[tile:]), 0.0).astype(BF16)
            bottom = dot(lower, v[:tile]) + dot(second, v[tile:])
            sums.append(jnp.concatenate([dot(first, v[:tile]), bottom], 0))
        within_out[:, cut] = jnp.concatenate(sums, 1)


def finish_query(chunk, w_query, query_sum, keys, values, block, size):
    arrays = (*chunk, w_query, query_sum, keys, values)
    outputs = [(query_sum.shape, BF16), (query_sum.shape, F32)]
    body = functools.partial(within_body, len(chunk), size, block)
    return kernel(body, [(array, pltpu.VMEM) for array in arrays], outputs)


def attend_body(earlier, size, odd, query, within, carry, partner, *refs):
    others = refs[:earlier]
    w_first, top_out, bottom_out, top_first, bottom_first = refs[earlier:]
    heads = carry.shape[0]
    half = query.shape[0] // 2
    for h in range(heads):
        cut = slice(h * size, (h + 1) * size)
        prior = carry[h] + jnp.where(odd[0] == 1, partner[h], 0.0)
        for other in others:
            prior = prior + other[h].astype(F32)
        high = prior.astype(BF16)
        low = (prior - high.astype(F32)).astype(BF16)
        q = query[:, cut]
        o = within[:, cut] + dot(q, high) + dot(q, low)
        o = o * lax.rsqrt(jnp.mean(o * o, axis=-1, keepdims=True) + EPSILON)
        attended = o.astype(BF16)
        top_out[:, cut] = attended[:half]
        bottom_out[:, cut] = attended[half:]
    block = 256 if w_first.shape[1] % 256 == 0 else 128

    @pl.loop(0, w_first.shape[1] // block)
    def _(j):
        cut = columns_of(j, block)
        weight = w_first[:, cut]
        top_first[:, cut] = dot(top_out[...], weight).astype(BF16)
        bottom_first[:, cut] = dot(bottom_out[...], weight).astype(BF16)


def attend(odd, query, within, carry, partner, others, w_first, size):
    rows, width = query.shape
    inputs = [(odd, pltpu.SMEM)]
    inputs += [(s, pltpu.VMEM) for s in (query, within, carry, partner, *others, w_first)]
    outputs = [((rows // 2, width), BF16)] * 2 + [((rows // 2, w_first.shape[1]), BF16)] * 2
    return kernel(functools.partial(attend_body, len(others), size), inputs, outputs)


def pair_body(own, partner, out):
    out[...] = (own[...] + partner[...]).astype(BF16)


def finish_body(top_sum, bottom_sum, top, bottom, out):
    half = top.shape[0]
    out[:half] = (top_sum[...] + top[...].astype(F32)).astype(BF16)
    out[half:] = (bottom_sum[...] + bottom[...].astype(F32)).astype(BF16)


def local(tokens, w_query, w_key, w_value, w_out, carry):
    row_count = tokens.shape[0]
    head_count, size = carry.shape[:2]
    block = size * (2 if head_count % 2 == 0 else 1)
    half = row_count // 2
    count = lax.axis_size("tp")
    reach = count // 2
    order = ring_order(count)
    forward = [(order[i], order[(i + 1) % count]) for i in range(count)]
    backward = [(b, a) for a, b in forward]
    index = lax.axis_index("tp")
    depth = tokens.shape[1]
    columns = w_out.shape[1] // count

    offsets = list(range(-reach + 1, reach + 1))
    numbers = [
        lookup([order[(order.index(i) + offset) % count] for i in range(count)], index)
        for offset in offsets
    ]
    column_starts = [n * columns for n in numbers]
    row_table = jnp.stack([n * depth for n in numbers])
    column_table = jnp.stack(column_starts)
    odd = jnp.reshape(lax.rem(lax.axis_index("seq"), 2), (1,))
    tokens, odd, row_table, column_table, column_starts = lax.optimization_barrier(
        (tokens, odd, row_table, column_table, column_starts)
    )

    def add(chunk, offset, held, sums, next_offset, extra=None):
        places = offsets.index(offset), offsets.index(next_offset)
        return project(chunk, row_table, places[0], weights, held, sums, block, places[1], extra)

    weights = (w_query, w_key, w_value)
    offset_of = [0]
    for step in range(1, reach):
        offset_of += [-step, step]
    windows = 2 * reach - 1
    ahead = {(0, 0): tokens[:half], (0, 1): tokens[half:]}
    behind = dict(ahead)

    def send(slot):
        level, second = divmod(slot - 1, 2)
        up, down = (level, second), (level, 1 - second)
        ahead[level + 1, second] = lax.ppermute(ahead[up], "tp", forward)
        behind[level + 1, 1 - second] = lax.ppermute(behind[down], "tp", backward)

    def halves(offset):
        side = ahead if offset < 0 else behind
        return [side[abs(offset), 0], side[abs(offset), 1]]

    send(1)
    send(2)
    sums, held = add([tokens], 0, None, None, offset_of[1])
    for window in range(2, windows):
        level, second = divmod(window, 2)
        up, down = (level, second), (level, 1 - second)
        ahead[up], behind[down], sums, held = lax.optimization_barrier(
            (ahead[up], behind[down], sums, held)
        )
        send(window + 1)
        if window > 2:
            offset, following = offset_of[window - 2], offset_of[window - 1]
            sums, held = add(halves(offset), offset, held, sums, following)
    up, down = (reach - 1, 1), (reach - 1, 0)
    ahead[up], behind[down], sums, held = lax.optimization_barrier(
        (ahead[up], behind[down], sums, held)
    )
    offset, following = offset_of[-2:]
    sums, held = add(halves(offset), offset, held, sums, following)
    extra = (w_out, column_table, columns)
    sums, final = add(halves(following), following, held, sums, reach, extra)
    ahead, behind = ahead[reach, 0], behind[reach, 1]
    last = [ahead, behind]
    w_query_last, w_key_last, w_value_last, w_first = final
    keys, values, state = finish_keys(
        last, w_key_last, w_value_last, sums[1], sums[2], block, size
    )

    members = lax.axis_size("seq")
    partner = lax.ppermute(state, "seq", [(i, i ^ 1) for i in range(members)])
    pair = kernel(
        pair_body,
        [(state, pltpu.VMEM), (partner, pltpu.VMEM)],
        [(state.shape, BF16)],
    )[0]
    others = [
        lax.ppermute(pair, "seq", [(i, i + shift) for i in range(members - shift)])
        for shift in range(2, members, 2)
    ]
    query, within = finish_query(last, w_query_last, sums[0], keys, values, block, size)

    *parts, top, bottom = attend(odd, query, within, carry, partner, others, w_first, size)

    def partial(rows, offset):
        start = column_starts[offsets.index(offset)]
        return dot(parts[rows], cut_at(w_out, start, columns, 1))

    up = [lax.ppermute(top, "tp", forward), None]
    down = [None, lax.ppermute(bottom, "tp", backward)]
    for distance in range(reach - 1, 0, -1):
        for rows in (0, 1):
            for held, sign, hops in ((up, 1, forward), (down, -1, backward)):
                value = partial(rows, sign * distance)
                if held[rows] is not None:
                    value = value + held[rows].astype(F32)
                held[rows] = lax.ppermute(value.astype(BF16), "tp", hops)
    top_sum = partial(0, 0) + down[0].astype(F32)
    bottom_sum = partial(1, 0) + up[1].astype(F32)
    return kernel(
        finish_body,
        [(s, pltpu.VMEM) for s in (top_sum, bottom_sum, up[0], down[1])],
        [((row_count, columns), BF16)],
    )[0]


def solution(mesh):
    placed = (
        P("seq", "tp"),
        P(None, "tp"),
        P(None, "tp"),
        P(None, "tp"),
        P("tp", None),
        P("tp", None, None),
    )
    return jax.shard_map(
        local, mesh=mesh, in_specs=placed, out_specs=P("seq", "tp"), check_vma=False
    )
```

time: 497 us -> 183 us (0.37)
  waiting for transfers between devices: 413 us -> 86.5 us
  matrix products: 61.1 us -> 15.6 us
  Pallas kernels: 0 us -> 45.3 us
  starting transfers between devices: 0.26 us -> 33.7 us
  between operations: 13.2 us -> 0.27 us
  other arithmetic: 8.24 us -> 0.01 us
    reduce_scatter x1 -> x0, waiting for transfers between devices: 282 us -> none  [local(): lax.psum_scatter(lax.dot_general(w_out, attended, (((0,), (1,)), ((), ())...]
    all_gather x2 -> x0, waiting for transfers between devices: 130 us -> none  [the longest x1 130 us: local(): segment = lax.all_gather(tokens, 'tp', axis=1, tiled=True)]
    ppermute x0 -> x30, waiting for transfers between devices: none -> 86.5 us  [the longest x12 44.5 us: local(): held[rows] = lax.ppermute(value.astype(BF16), 'tp', hops)]
    dot_general x7 -> x14, matrix products: 61.1 us -> 15.6 us  [dot(): return jnp.dot(a, b, preferred_element_type=F32)]
    pallas_call x0 -> x12, Pallas kernels: none -> 45.3 us  [kernel(): pl.pallas_call(body, in_specs=[pl.BlockSpec(memory_space=space) for _, sp...]
    ppermute x0 -> x30, starting transfers between devices: none -> 33.7 us  [the longest x7 13 us: send(): ahead[level + 1, second] = lax.ppermute(ahead[up], 'tp', forward)]
  transfers between devices with their start and end apart: 3 -> 30, of which waited for: 2 -> 22; matrix products, arithmetic and copies ran while one was open for 4% -> 9% of each run, Pallas kernels for 0% -> 21%
where the time goes in v1:
time: 183 us
  waiting for transfers between devices  86.5 us (47%)
  Pallas kernels  45.3 us (25%)
  starting transfers between devices  33.7 us (18%)
  matrix products  15.6 us (9%)
    pallas_call x12, Pallas kernels, kernel(): pl.pallas_call(body, in_specs=[pl.BlockSpec(memory_space=space) for _, sp...  45.3 us
    ppermute x12, waiting for transfers between devices, local(): held[rows] = lax.ppermute(value.astype(BF16), 'tp', hops)  44.5 us
    ppermute x7, waiting for transfers between devices, send(): ahead[level + 1, second] = lax.ppermute(ahead[up], 'tp', forward)  20.7 us
    dot_general x14, matrix products, dot(): return jnp.dot(a, b, preferred_element_type=F32)  15.6 us
    ppermute x7, waiting for transfers between devices, send(): behind[level + 1, 1 - second] = lax.ppermute(behind[down], 'tp', backward)  13.3 us
    ppermute x7, starting transfers between devices, send(): ahead[level + 1, second] = lax.ppermute(ahead[up], 'tp', forward)  13 us
    ppermute x12, starting transfers between devices, local(): held[rows] = lax.ppermute(value.astype(BF16), 'tp', hops)  12.7 us
    ppermute x1, waiting for transfers between devices, local(): down = [None, lax.ppermute(bottom, 'tp', backward)]  6.22 us
  transfers between devices with their start and end apart: 30, of which 22 were waited for; matrix products, arithmetic and copies ran while one was open for 9% of the time, Pallas kernels for 21%

profile of v1, /device:TPU:0, one launch (start us, length us, event | category | flops | bytes accessed | tf_op | source)
XLA Modules:
  0.0 182.9 jit_solution(15626679849195320243)
XLA Ops:
  0.1 1.3 fusion.114
  1.4 3.1 %collective-permute-start = (bf16[256,1024]{1,0:T(8,128)(2,1)S(1)}, bf16[256,1024]{1,0:T(8,128)(2,1)S(1)}, u32[]{:S(2)}, u32[]{:S(2)}) collective-permute-start(bf16[256,1024]{1,0:T(8,128)(2,1)S(1)} %get-tuple-element.228), channel_id=1, source_target_pairs={{0,2},{2,4},{4,6},{6,7},{7,5},{5,3},{3,1},{1,0},{8,10},{10,12},{12... | collective-permute-start | bytes 1572872 | tf_op jit(solution)/shard_map/ppermute | solution.py:300
  4.5 2.0 %collective-permute-start.4 = (bf16[256,1024]{1,0:T(8,128)(2,1)S(1)}, bf16[256,1024]{1,0:T(8,128)(2,1)S(1)}, u32[]{:S(2)}, u32[]{:S(2)}) collective-permute-start(bf16[256,1024]{1,0:T(8,128)(2,1)S(1)} %get-tuple-element.227), channel_id=1, source_target_pairs={{0,2},{2,4},{4,6},{6,7},{7,5},{5,3},{3,1},{1,0},{8,10},{10,12},{12... | collective-permute-start | bytes 1572872 | tf_op jit(solution)/shard_map/ppermute | solution.py:300
  6.5 6.0 %shard_map.64 = (f32[512,768]{1,0:T(8,128)S(1)}, f32[512,768]{1,0:T(8,128)S(1)}, f32[512,768]{1,0:T(8,128)S(1)}, bf16[1024,768]{1,0:T(8,128)(2,1)S(1)}, bf16[102...) custom-call(s32[8]{0:T(128)S(1)} %stack.44.refs_0_.refs_7_, bf16[512,1024]{1,0:T(8,128)(2,1)S(1)} %copy-done, ...), custom_call_target="tpu_custom_call" | custom-call | bytes 1048576 | tf_op jit(solution)/shard_map/pallas_call | solution.py:57
  12.6 4.6 %collective-permute-done.refs_1_ = bf16[256,1024]{1,0:T(8,128)(2,1)S(1)} collective-permute-done((bf16[256,1024]{1,0:T(8,128)(2,1)S(1)}, bf16[256,1024]{1,0:T(8,128)(2,1)S(1)}, u32[]{:S(2)}, u32[]{:S(2)}) %collective-permute-start) | collective-permute-done | bytes 524320 | tf_op jit(solution)/shard_map/ppermute | solution.py:300
  17.2 2.2 %collective-permute-done.1.refs_2_ = bf16[256,1024]{1,0:T(8,128)(2,1)S(1)} collective-permute-done((bf16[256,1024]{1,0:T(8,128)(2,1)S(1)}, bf16[256,1024]{1,0:T(8,128)(2,1)S(1)}, u32[]{:S(2)}, u32[]{:S(2)}) %collective-permute-start.1) | collective-permute-done | bytes 524320 | tf_op jit(solution)/shard_map/ppermute | solution.py:301
  19.4 1.6 collective-permute-start.2
  21.4 7.0 %collective-permute-done.4.refs_2_ = bf16[256,1024]{1,0:T(8,128)(2,1)S(1)} collective-permute-done((bf16[256,1024]{1,0:T(8,128)(2,1)S(1)}, bf16[256,1024]{1,0:T(8,128)(2,1)S(1)}, u32[]{:S(2)}, u32[]{:S(2)}) %collective-permute-start.4) | collective-permute-done | bytes 524320 | tf_op jit(solution)/shard_map/ppermute | solution.py:300
  28.4 2.2 %collective-permute-done.5.refs_1_ = bf16[256,1024]{1,0:T(8,128)(2,1)S(1)} collective-permute-done((bf16[256,1024]{1,0:T(8,128)(2,1)S(1)}, bf16[256,1024]{1,0:T(8,128)(2,1)S(1)}, u32[]{:S(2)}, u32[]{:S(2)}) %collective-permute-start.5) | collective-permute-done | bytes 524320 | tf_op jit(solution)/shard_map/ppermute | solution.py:301
  30.6 1.6 collective-permute-start.8
  32.6 4.7 %shard_map.65 = (f32[512,768]{1,0:T(8,128)S(1)}, f32[512,768]{1,0:T(8,128)S(1)}, f32[512,768]{1,0:T(8,128)S(1)}, bf16[1024,768]{1,0:T(8,128)(2,1)S(1)}, bf16[102...) custom-call(s32[8]{0:T(128)S(1)} %stack.44.refs_0_.refs_7_, ...), custom_call_target="tpu_custom_call", output_to_operand_aliasing={{0}: (9, {}), {1}: (10, {}), {2}: (11, {})} | custom-call | bytes 1048576 | tf_op jit(solution)/shard_map/pallas_call | solution.py:57
  37.4 2.3 %collective-permute-done.2.refs_1_ = bf16[256,1024]{1,0:T(8,128)(2,1)S(1)} collective-permute-done((bf16[256,1024]{1,0:T(8,128)(2,1)S(1)}, bf16[256,1024]{1,0:T(8,128)(2,1)S(1)}, u32[]{:S(2)}, u32[]{:S(2)}) %collective-permute-start.2) | collective-permute-done | bytes 524320 | tf_op jit(solution)/shard_map/ppermute | solution.py:300
  39.6 2.2 %collective-permute-done.3.refs_2_ = bf16[256,1024]{1,0:T(8,128)(2,1)S(1)} collective-permute-done((bf16[256,1024]{1,0:T(8,128)(2,1)S(1)}, bf16[256,1024]{1,0:T(8,128)(2,1)S(1)}, u32[]{:S(2)}, u32[]{:S(2)}) %collective-permute-start.3) | collective-permute-done | bytes 524320 | tf_op jit(solution)/shard_map/ppermute | solution.py:301
  41.8 1.6 collective-permute-start.6
  43.9 4.8 %shard_map.66 = (f32[512,768]{1,0:T(8,128)S(1)}, f32[512,768]{1,0:T(8,128)S(1)}, f32[512,768]{1,0:T(8,128)S(1)}, bf16[1024,768]{1,0:T(8,128)(2,1)S(1)}, bf16[102...) custom-call(s32[8]{0:T(128)S(1)} %stack.44.refs_0_.refs_7_, ...), custom_call_target="tpu_custom_call", output_to_operand_aliasing={{0}: (9, {}), {1}: (10, {}), {2}: (11, {})} | custom-call | bytes 1048576 | tf_op jit(solution)/shard_map/pallas_call | solution.py:57
  48.6 2.3 %collective-permute-done.8.refs_2_ = bf16[256,1024]{1,0:T(8,128)(2,1)S(1)} collective-permute-done((bf16[256,1024]{1,0:T(8,128)(2,1)S(1)}, bf16[256,1024]{1,0:T(8,128)(2,1)S(1)}, u32[]{:S(2)}, u32[]{:S(2)}) %collective-permute-start.8) | collective-permute-done | bytes 524320 | tf_op jit(solution)/shard_map/ppermute | solution.py:300
  50.9 2.2 %collective-permute-done.9.refs_1_ = bf16[256,1024]{1,0:T(8,128)(2,1)S(1)} collective-permute-done((bf16[256,1024]{1,0:T(8,128)(2,1)S(1)}, bf16[256,1024]{1,0:T(8,128)(2,1)S(1)}, u32[]{:S(2)}, u32[]{:S(2)}) %collective-permute-start.9) | collective-permute-done | bytes 524320 | tf_op jit(solution)/shard_map/ppermute | solution.py:301
  53.1 1.6 collective-permute-start.12
  55.1 4.8 %shard_map.67 = (f32[512,768]{1,0:T(8,128)S(1)}, f32[512,768]{1,0:T(8,128)S(1)}, f32[512,768]{1,0:T(8,128)S(1)}, bf16[1024,768]{1,0:T(8,128)(2,1)S(1)}, bf16[102...) custom-call(s32[8]{0:T(128)S(1)} %stack.44.refs_0_.refs_7_, ...), custom_call_target="tpu_custom_call", output_to_operand_aliasing={{0}: (9, {}), {1}: (10, {}), {2}: (11, {})} | custom-call | bytes 1048576 | tf_op jit(solution)/shard_map/pallas_call | solution.py:57
  59.9 2.3 %collective-permute-done.6.refs_1_ = bf16[256,1024]{1,0:T(8,128)(2,1)S(1)} collective-permute-done((bf16[256,1024]{1,0:T(8,128)(2,1)S(1)}, bf16[256,1024]{1,0:T(8,128)(2,1)S(1)}, u32[]{:S(2)}, u32[]{:S(2)}) %collective-permute-start.6) | collective-permute-done | bytes 524320 | tf_op jit(solution)/shard_map/ppermute | solution.py:300
  62.1 2.2 %collective-permute-done.7.refs_2_ = bf16[256,1024]{1,0:T(8,128)(2,1)S(1)} collective-permute-done((bf16[256,1024]{1,0:T(8,128)(2,1)S(1)}, bf16[256,1024]{1,0:T(8,128)(2,1)S(1)}, u32[]{:S(2)}, u32[]{:S(2)}) %collective-permute-start.7) | collective-permute-done | bytes 524320 | tf_op jit(solution)/shard_map/ppermute | solution.py:301
  64.3 1.6 collective-permute-start.10
  66.3 4.8 %shard_map.68 = (f32[512,768]{1,0:T(8,128)S(1)}, f32[512,768]{1,0:T(8,128)S(1)}, f32[512,768]{1,0:T(8,128)S(1)}, bf16[1024,768]{1,0:T(8,128)(2,1)S(1)}, bf16[102...) custom-call(s32[8]{0:T(128)S(1)} %stack.44.refs_0_.refs_7_, ...), custom_call_target="tpu_custom_call", output_to_operand_aliasing={{0}: (9, {}), {1}: (10, {}), {2}: (11, {})} | custom-call | bytes 1048576 | tf_op jit(solution)/shard_map/pallas_call | solution.py:57
  71.1 2.3 %collective-permute-done.12.refs_2_ = bf16[256,1024]{1,0:T(8,128)(2,1)S(1)} collective-permute-done((bf16[256,1024]{1,0:T(8,128)(2,1)S(1)}, bf16[256,1024]{1,0:T(8,128)(2,1)S(1)}, u32[]{:S(2)}, u32[]{:S(2)}) %collective-permute-start.12) | collective-permute-done | bytes 524320 | tf_op jit(solution)/shard_map/ppermute | solution.py:300
  73.4 2.2 %collective-permute-done.13.refs_1_ = bf16[256,1024]{1,0:T(8,128)(2,1)S(1)} collective-permute-done((bf16[256,1024]{1,0:T(8,128)(2,1)S(1)}, bf16[256,1024]{1,0:T(8,128)(2,1)S(1)}, u32[]{:S(2)}, u32[]{:S(2)}) %collective-permute-start.13) | collective-permute-done | bytes 524320 | tf_op jit(solution)/shard_map/ppermute | solution.py:301
  75.5 4.8 %shard_map.69 = (f32[512,768]{1,0:T(8,128)S(1)}, f32[512,768]{1,0:T(8,128)S(1)}, f32[512,768]{1,0:T(8,128)S(1)}, bf16[1024,768]{1,0:T(8,128)(2,1)S(1)}, bf16[102...) custom-call(s32[8]{0:T(128)S(1)} %stack.44.refs_0_.refs_7_, ...), custom_call_target="tpu_custom_call", output_to_operand_aliasing={{0}: (9, {}), {1}: (10, {}), {2}: (11, {})} | custom-call | bytes 1048576 | tf_op jit(solution)/shard_map/pallas_call | solution.py:57
  80.3 4.8 %shard_map.70 = (f32[512,768]{1,0:T(8,128)S(1)}, f32[512,768]{1,0:T(8,128)S(1)}, f32[512,768]{1,0:T(8,128)S(1)}, bf16[1024,768]{1,0:T(8,128)(2,1)S(1)}, bf16[102...) custom-call(s32[8]{0:T(128)S(1)} %stack.44.refs_0_.refs_7_, ...), custom_call_target="tpu_custom_call", output_to_operand_aliasing={{0}: (11, {}), {1}: (12, {}), {2}: (13, {})} | custom-call | bytes 1048576 | tf_op jit(solution)/shard_map/pallas_call | solution.py:57
  85.3 3.0 %shard_map.71 = (bf16[512,768]{1,0:T(8,128)(2,1)S(1)}, bf16[512,768]{1,0:T(8,128)(2,1)S(1)}, f32[6,128,128]{2,1,0:T(8,128)S(1)}) custom-call(bf16[256,1024]{1,0:T(8,128)(2,1)S(1)} %collective-permute-done.10.refs_0_, bf16[256,1024]{1,0:T(8,128)(2,1)S(1)} %collective-permute-done.11.refs_1_, bf16[1024,768]{1,0:T(8,128)(2,1)S(1)} %get-tuple-element.206.refs_2_, ...), custom_call_target="tpu_custom_call" | custom-call | bytes 1048576 | tf_op jit(solution)/shard_map/pallas_call | solution.py:57
  88.3 1.7 collective-permute-done.14.partner
  90.1 3.4 %collective-permute-start.15 = (bf16[6,128,128]{2,1,0:T(8,128)(2,1)S(1)}, bf16[6,128,128]{2,1,0:T(8,128)(2,1)S(1)}, u32[]{:S(2)}, u32[]{:S(2)}) collective-permute-start(bf16[6,128,128]{2,1,0:T(8,128)(2,1)S(1)} %shard_map.73), channel_id=1, source_target_pairs={{0,16},{8,24},{1,17},{9,25},{2,18},{10,26},{3,19},{11,27},{4,20},{... | collective-permute-start | bytes 589832 | tf_op jit(solution)/shard_map/ppermute | solution.py:343
  93.6 4.4 %shard_map.72 = (bf16[512,768]{1,0:T(8,128)(2,1)S(1)}, f32[512,768]{1,0:T(8,128)S(1)}) custom-call(bf16[256,1024]{1,0:T(8,128)(2,1)S(1)} %collective-permute-done.10.refs_0_, bf16[256,1024]{1,0:T(8,128)(2,1)S(1)} %collective-permute-done.11.refs_1_, bf16[1024,768]{1,0:T(8,128)(2,1)S(1)} %get-tuple-element.204.refs_2_, ...), custom_call_target="tpu_custom_call" | custom-call | bytes 1048576 | tf_op jit(solution)/shard_map/pallas_call | solution.py:57
  98.0 2.2 %shard_map.74 = (bf16[256,768]{1,0:T(8,128)(2,1)S(1)}, bf16[256,768]{1,0:T(8,128)(2,1)S(1)}, bf16[256,1024]{1,0:T(8,128)(2,1)S(1)}, bf16[256,1024]{1,0:T(8,128)(2,1)S(1)}) custom-call(s32[1]{0:T(128)} %bitcast.odd, bf16[512,768]{1,0:T(8,128)(2,1)S(1)} %get-tuple-element.212.query, f32[512,768]{1,0:T(8,128)S(1)} %get-tuple-element.213.within, ...), custom_call_target="tpu_custom_call" | custom-call | bytes 1048576 | tf_op jit(solution)/shard_map/pallas_call | solution.py:57
  100.2 0.7 collective-permute-start.26
  100.9 1.6 collective-permute-start.22
  102.5 2.2 %fusion.97 = bf16[256,1024]{1,0:T(8,128)(2,1)S(1)} fusion(bf16[256,768]{1,0:T(8,128)(2,1)S(1)} %get-tuple-element.221, bf16[768,8192]{1,0:T(8,128)(2,1)} %refs_6_.1, s32[]{:T(128)} %mul.38), kind=kOutput, calls=%fused_computation.51 | convolution fusion | flops 402915328 | bytes 2490880 | tf_op jit(solution)/shard_map/dot_general | solution.py:45
  104.7 1.6 collective-permute-start.19
  106.3 2.2 %fusion.94 = bf16[256,1024]{1,0:T(8,128)(2,1)S(1)} fusion(bf16[256,768]{1,0:T(8,128)(2,1)S(1)} %get-tuple-element.216, bf16[768,8192]{1,0:T(8,128)(2,1)} %refs_6_.1, s32[]{:T(128)} %mul.32), kind=kOutput, calls=%fused_computation.50 | convolution fusion | flops 402915328 | bytes 2490880 | tf_op jit(solution)/shard_map/dot_general | solution.py:45
  108.5 0.5 collective-permute-start.16
  109.1 6.2 %collective-permute-done.26 = bf16[256,1024]{1,0:T(8,128)(2,1)S(1)} collective-permute-done((bf16[256,1024]{1,0:T(8,128)(2,1)S(1)}, bf16[256,1024]{1,0:T(8,128)(2,1)S(1)}, u32[]{:S(2)}, u32[]{:S(2)}) %collective-permute-start.26) | collective-permute-done | bytes 524320 | tf_op jit(solution)/shard_map/ppermute | solution.py:355
  115.3 2.3 %fusion.79 = bf16[256,1024]{1,0:T(8,128)(2,1)S(1)} fusion(bf16[256,768]{1,0:T(8,128)(2,1)S(1)} %get-tuple-element.221, bf16[768,8192]{1,0:T(8,128)(2,1)} %refs_6_.1, s32[]{:T(128)} %mul.32, bf16[256,1024]{1,0:T(8,128)(2,1)S(1)} %collective-permute-done.26), kind=kOutput, calls=%fused_computation.45 | convolution fusion | flops 403439616 | bytes 3015168 | tf_op jit(solution)/shard_map/dot_general | solution.py:45
  118.0 0.8 fusion.64
  118.8 1.7 collective-permute-start.23
  120.5 6.5 %collective-permute-done.19 = bf16[256,1024]{1,0:T(8,128)(2,1)S(1)} collective-permute-done((bf16[256,1024]{1,0:T(8,128)(2,1)S(1)}, bf16[256,1024]{1,0:T(8,128)(2,1)S(1)}, u32[]{:S(2)}, u32[]{:S(2)}) %collective-permute-start.19) | collective-permute-done | bytes 524320 | tf_op jit(solution)/shard_map/ppermute | solution.py:362
  127.0 0.8 fusion.70
  127.8 1.6 collective-permute-start.20
  129.4 0.8 fusion.85
  130.2 0.5 collective-permute-start.17
  130.7 7.0 %collective-permute-done.27 = bf16[256,1024]{1,0:T(8,128)(2,1)S(1)} collective-permute-done((bf16[256,1024]{1,0:T(8,128)(2,1)S(1)}, bf16[256,1024]{1,0:T(8,128)(2,1)S(1)}, u32[]{:S(2)}, u32[]{:S(2)}) %collective-permute-start.27) | collective-permute-done | bytes 524320 | tf_op jit(solution)/shard_map/ppermute | solution.py:362
  137.7 0.8 fusion.82
  139.0 0.8 fusion.67
  139.9 1.6 collective-permute-start.24
  141.5 8.0 %collective-permute-done.20 = bf16[256,1024]{1,0:T(8,128)(2,1)S(1)} collective-permute-done((bf16[256,1024]{1,0:T(8,128)(2,1)S(1)}, bf16[256,1024]{1,0:T(8,128)(2,1)S(1)}, u32[]{:S(2)}, u32[]{:S(2)}) %collective-permute-start.20) | collective-permute-done | bytes 524320 | tf_op jit(solution)/shard_map/ppermute | solution.py:362
  149.5 0.8 fusion.76
  150.3 1.6 collective-permute-start.21
  151.9 0.8 fusion.91
  153.2 7.0 %collective-permute-done.28 = bf16[256,1024]{1,0:T(8,128)(2,1)S(1)} collective-permute-done((bf16[256,1024]{1,0:T(8,128)(2,1)S(1)}, bf16[256,1024]{1,0:T(8,128)(2,1)S(1)}, u32[]{:S(2)}, u32[]{:S(2)}) %collective-permute-start.28) | collective-permute-done | bytes 524320 | tf_op jit(solution)/shard_map/ppermute | solution.py:362
  160.2 0.8 fusion.88
  161.5 0.8 fusion.73
  162.3 1.6 collective-permute-start.25
  164.0 8.0 %collective-permute-done.21 = bf16[256,1024]{1,0:T(8,128)(2,1)S(1)} collective-permute-done((bf16[256,1024]{1,0:T(8,128)(2,1)S(1)}, bf16[256,1024]{1,0:T(8,128)(2,1)S(1)}, u32[]{:S(2)}, u32[]{:S(2)}) %collective-permute-start.21) | collective-permute-done | bytes 524320 | tf_op jit(solution)/shard_map/ppermute | solution.py:362
  171.9 0.8 fusion.31.bottom_sum
  172.7 0.8 fusion.28.top_sum
  173.5 8.0 %collective-permute-done.29.bottom = bf16[256,1024]{1,0:T(8,128)(2,1)S(1)} collective-permute-done((bf16[256,1024]{1,0:T(8,128)(2,1)S(1)}, bf16[256,1024]{1,0:T(8,128)(2,1)S(1)}, u32[]{:S(2)}, u32[]{:S(2)}) %collective-permute-start.29) | collective-permute-done | bytes 524320 | tf_op jit(solution)/shard_map/ppermute | solution.py:362
  181.7 1.1 shard_map.75
  (35 shorter events, 4.8 us)
Async XLA Ops:
  0.0 6.5 %copy-start = (bf16[512,1024]{1,0:T(8,128)(2,1)S(1)}, bf16[512,1024]{1,0:T(8,128)(2,1)}, u32[]{:S(2)}) copy-start(bf16[512,1024]{1,0:T(8,128)(2,1)} %refs_1_) | copy-start | bytes 3145732
  1.4 15.7 %collective-permute-start = (bf16[256,1024]{1,0:T(8,128)(2,1)S(1)}, bf16[256,1024]{1,0:T(8,128)(2,1)S(1)}, u32[]{:S(2)}, u32[]{:S(2)}) collective-permute-start(bf16[256,1024]{1,0:T(8,128)(2,1)S(1)} %get-tuple-element.228), channel_id=1, source_target_pairs={{0,2},{2,4},{4,6},{6,7},{7,5},{5,3},{3,1},{1,0},{8,10},{10,12},{12... | collective-permute-start | bytes 1572872 | tf_op jit(solution)/shard_map/ppermute | solution.py:300
  4.5 14.8 %collective-permute-start.1 = (bf16[256,1024]{1,0:T(8,128)(2,1)S(1)}, bf16[256,1024]{1,0:T(8,128)(2,1)S(1)}, u32[]{:S(2)}, u32[]{:S(2)}) collective-permute-start(bf16[256,1024]{1,0:T(8,128)(2,1)S(1)} %get-tuple-element.227), channel_id=1, source_target_pairs={{2,0},{4,2},{6,4},{7,6},{5,7},{3,5},{1,3},{0,1},{10,8},{12,10},{14... | collective-permute-start | bytes 1572872 | tf_op jit(solution)/shard_map/ppermute | solution.py:301
  4.5 23.9 %collective-permute-start.4 = (bf16[256,1024]{1,0:T(8,128)(2,1)S(1)}, bf16[256,1024]{1,0:T(8,128)(2,1)S(1)}, u32[]{:S(2)}, u32[]{:S(2)}) collective-permute-start(bf16[256,1024]{1,0:T(8,128)(2,1)S(1)} %get-tuple-element.227), channel_id=1, source_target_pairs={{0,2},{2,4},{4,6},{6,7},{7,5},{5,3},{3,1},{1,0},{8,10},{10,12},{12... | collective-permute-start | bytes 1572872 | tf_op jit(solution)/shard_map/ppermute | solution.py:300
  6.5 24.1 %collective-permute-start.5 = (bf16[256,1024]{1,0:T(8,128)(2,1)S(1)}, bf16[256,1024]{1,0:T(8,128)(2,1)S(1)}, u32[]{:S(2)}, u32[]{:S(2)}) collective-permute-start(bf16[256,1024]{1,0:T(8,128)(2,1)S(1)} %get-tuple-element.228), channel_id=1, source_target_pairs={{2,0},{4,2},{6,4},{7,6},{5,7},{3,5},{1,3},{0,1},{10,8},{12,10},{14... | collective-permute-start | bytes 1572872 | tf_op jit(solution)/shard_map/ppermute | solution.py:301
  19.4 20.3 %collective-permute-start.2 = (bf16[256,1024]{1,0:T(8,128)(2,1)S(1)}, bf16[256,1024]{1,0:T(8,128)(2,1)S(1)}, u32[]{:S(2)}, u32[]{:S(2)}) collective-permute-start(bf16[256,1024]{1,0:T(8,128)(2,1)S(1)} %collective-permute-done.refs_1_), channel_id=1, source_target_pairs={{0,2},{2,4},{4,6},{6,7},{7,5},{5,3},{3,1},{1,0},{8,10},{10,12},{12... | collective-permute-start | bytes 1572872 | tf_op jit(solution)/shard_map/ppermute | solution.py:300
  20.9 20.9 %collective-permute-start.3 = (bf16[256,1024]{1,0:T(8,128)(2,1)S(1)}, bf16[256,1024]{1,0:T(8,128)(2,1)S(1)}, u32[]{:S(2)}, u32[]{:S(2)}) collective-permute-start(bf16[256,1024]{1,0:T(8,128)(2,1)S(1)} %collective-permute-done.1.refs_2_), channel_id=1, source_target_pairs={{2,0},{4,2},{6,4},{7,6},{5,7},{3,5},{1,3},{0,1},{10,8},{12,10},{14... | collective-permute-start | bytes 1572872 | tf_op jit(solution)/shard_map/ppermute | solution.py:301
  30.6 20.3 %collective-permute-start.8 = (bf16[256,1024]{1,0:T(8,128)(2,1)S(1)}, bf16[256,1024]{1,0:T(8,128)(2,1)S(1)}, u32[]{:S(2)}, u32[]{:S(2)}) collective-permute-start(bf16[256,1024]{1,0:T(8,128)(2,1)S(1)} %collective-permute-done.4.refs_2_), channel_id=1, source_target_pairs={{0,2},{2,4},{4,6},{6,7},{7,5},{5,3},{3,1},{1,0},{8,10},{10,12},{12... | collective-permute-start | bytes 1572872 | tf_op jit(solution)/shard_map/ppermute | solution.py:300
  32.2 20.9 %collective-permute-start.9 = (bf16[256,1024]{1,0:T(8,128)(2,1)S(1)}, bf16[256,1024]{1,0:T(8,128)(2,1)S(1)}, u32[]{:S(2)}, u32[]{:S(2)}) collective-permute-start(bf16[256,1024]{1,0:T(8,128)(2,1)S(1)} %collective-permute-done.5.refs_1_), channel_id=1, source_target_pairs={{2,0},{4,2},{6,4},{7,6},{5,7},{3,5},{1,3},{0,1},{10,8},{12,10},{14... | collective-permute-start | bytes 1572872 | tf_op jit(solution)/shard_map/ppermute | solution.py:301
  41.8 20.3 %collective-permute-start.6 = (bf16[256,1024]{1,0:T(8,128)(2,1)S(1)}, bf16[256,1024]{1,0:T(8,128)(2,1)S(1)}, u32[]{:S(2)}, u32[]{:S(2)}) collective-permute-start(bf16[256,1024]{1,0:T(8,128)(2,1)S(1)} %collective-permute-done.2.refs_1_), channel_id=1, source_target_pairs={{0,2},{2,4},{4,6},{6,7},{7,5},{5,3},{3,1},{1,0},{8,10},{10,12},{12... | collective-permute-start | bytes 1572872 | tf_op jit(solution)/shard_map/ppermute | solution.py:300
  43.4 20.9 %collective-permute-start.7 = (bf16[256,1024]{1,0:T(8,128)(2,1)S(1)}, bf16[256,1024]{1,0:T(8,128)(2,1)S(1)}, u32[]{:S(2)}, u32[]{:S(2)}) collective-permute-start(bf16[256,1024]{1,0:T(8,128)(2,1)S(1)} %collective-permute-done.3.refs_2_), channel_id=1, source_target_pairs={{2,0},{4,2},{6,4},{7,6},{5,7},{3,5},{1,3},{0,1},{10,8},{12,10},{14... | collective-permute-start | bytes 1572872 | tf_op jit(solution)/shard_map/ppermute | solution.py:301
  53.1 20.3 %collective-permute-start.12 = (bf16[256,1024]{1,0:T(8,128)(2,1)S(1)}, bf16[256,1024]{1,0:T(8,128)(2,1)S(1)}, u32[]{:S(2)}, u32[]{:S(2)}) collective-permute-start(bf16[256,1024]{1,0:T(8,128)(2,1)S(1)} %collective-permute-done.8.refs_2_), channel_id=1, source_target_pairs={{0,2},{2,4},{4,6},{6,7},{7,5},{5,3},{3,1},{1,0},{8,10},{10,12},{12... | collective-permute-start | bytes 1572872 | tf_op jit(solution)/shard_map/ppermute | solution.py:300
  54.6 20.9 %collective-permute-start.13 = (bf16[256,1024]{1,0:T(8,128)(2,1)S(1)}, bf16[256,1024]{1,0:T(8,128)(2,1)S(1)}, u32[]{:S(2)}, u32[]{:S(2)}) collective-permute-start(bf16[256,1024]{1,0:T(8,128)(2,1)S(1)} %collective-permute-done.9.refs_1_), channel_id=1, source_target_pairs={{2,0},{4,2},{6,4},{7,6},{5,7},{3,5},{1,3},{0,1},{10,8},{12,10},{14... | collective-permute-start | bytes 1572872 | tf_op jit(solution)/shard_map/ppermute | solution.py:301
  64.3 20.8 %collective-permute-start.10 = (bf16[256,1024]{1,0:T(8,128)(2,1)S(1)}, bf16[256,1024]{1,0:T(8,128)(2,1)S(1)}, u32[]{:S(2)}, u32[]{:S(2)}) collective-permute-start(bf16[256,1024]{1,0:T(8,128)(2,1)S(1)} %collective-permute-done.6.refs_1_), channel_id=1, source_target_pairs={{0,2},{2,4},{4,6},{6,7},{7,5},{5,3},{3,1},{1,0},{8,10},{10,12},{12... | collective-permute-start | bytes 1572872 | tf_op jit(solution)/shard_map/ppermute | solution.py:300
  65.9 19.4 %collective-permute-start.11 = (bf16[256,1024]{1,0:T(8,128)(2,1)S(1)}, bf16[256,1024]{1,0:T(8,128)(2,1)S(1)}, u32[]{:S(2)}, u32[]{:S(2)}) collective-permute-start(bf16[256,1024]{1,0:T(8,128)(2,1)S(1)} %collective-permute-done.7.refs_2_), channel_id=1, source_target_pairs={{2,0},{4,2},{6,4},{7,6},{5,7},{3,5},{1,3},{0,1},{10,8},{12,10},{14... | collective-permute-start | bytes 1572872 | tf_op jit(solution)/shard_map/ppermute | solution.py:301
  85.3 32.7 %slice-start = ((s8[12582912]{0:T(1024)(128)(4,1)}), s8[4194304]{0:T(1024)(128)(4,1)S(1)}, s32[]{:S(2)}) async-start(s8[12582912]{0:T(1024)(128)(4,1)} %bitcast.23), calls=%async_computation | async-start | bytes 8388608
  88.3 1.8 collective-permute-start.14
  90.1 7.9 %collective-permute-start.15 = (bf16[6,128,128]{2,1,0:T(8,128)(2,1)S(1)}, bf16[6,128,128]{2,1,0:T(8,128)(2,1)S(1)}, u32[]{:S(2)}, u32[]{:S(2)}) collective-permute-start(bf16[6,128,128]{2,1,0:T(8,128)(2,1)S(1)} %shard_map.73), channel_id=1, source_target_pairs={{0,16},{8,24},{1,17},{9,25},{2,18},{10,26},{3,19},{11,27},{4,20},{... | collective-permute-start | bytes 589832 | tf_op jit(solution)/shard_map/ppermute | solution.py:343
  93.5 4.4 %copy-start.1 = (f32[6,128,128]{2,1,0:T(8,128)S(1)}, f32[6,128,128]{2,1,0:T(8,128)}, u32[]{:S(2)}) copy-start(f32[6,128,128]{2,1,0:T(8,128)} %carry.1) | copy-start | bytes 1179652
  93.6 24.4 %slice-start.1 = ((s8[12582912]{0:T(1024)(128)(4,1)}), s8[4194304]{0:T(1024)(128)(4,1)S(1)}, s32[]{:S(2)}) async-start(s8[12582912]{0:T(1024)(128)(4,1)} %bitcast.23), calls=%async_computation.1 | async-start | bytes 8388608
  98.0 20.0 %slice-start.2 = ((s8[12582912]{0:T(1024)(128)(4,1)}), s8[4194304]{0:T(1024)(128)(4,1)S(1)}, s32[]{:S(2)}) async-start(s8[12582912]{0:T(1024)(128)(4,1)} %bitcast.23), calls=%async_computation.2 | async-start | bytes 8388608
  100.2 15.0 %collective-permute-start.26 = (bf16[256,1024]{1,0:T(8,128)(2,1)S(1)}, bf16[256,1024]{1,0:T(8,128)(2,1)S(1)}, u32[]{:S(2)}, u32[]{:S(2)}) collective-permute-start(bf16[256,1024]{1,0:T(8,128)(2,1)S(1)} %get-tuple-element.226), channel_id=1, source_target_pairs={{2,0},{4,2},{6,4},{7,6},{5,7},{3,5},{1,3},{0,1},{10,8},{12,10},{14... | collective-permute-start | bytes 1572872 | tf_op jit(solution)/shard_map/ppermute | solution.py:355
  100.9 17.1 %collective-permute-start.22 = (bf16[256,1024]{1,0:T(8,128)(2,1)S(1)}, bf16[256,1024]{1,0:T(8,128)(2,1)S(1)}, u32[]{:S(2)}, u32[]{:S(2)}) collective-permute-start(bf16[256,1024]{1,0:T(8,128)(2,1)S(1)} %get-tuple-element.225), channel_id=1, source_target_pairs={{0,2},{2,4},{4,6},{6,7},{7,5},{5,3},{3,1},{1,0},{8,10},{10,12},{12... | collective-permute-start | bytes 1572872 | tf_op jit(solution)/shard_map/ppermute | solution.py:354
  104.7 22.2 %collective-permute-start.19 = (bf16[256,1024]{1,0:T(8,128)(2,1)S(1)}, bf16[256,1024]{1,0:T(8,128)(2,1)S(1)}, u32[]{:S(2)}, u32[]{:S(2)}) collective-permute-start(bf16[256,1024]{1,0:T(8,128)(2,1)S(1)} %fusion.97), channel_id=1, source_target_pairs={{0,2},{2,4},{4,6},{6,7},{7,5},{5,3},{3,1},{1,0},{8,10},{10,12},{12... | collective-permute-start | bytes 1572872 | tf_op jit(solution)/shard_map/ppermute | solution.py:362
  108.5 20.9 %collective-permute-start.16 = (bf16[256,1024]{1,0:T(8,128)(2,1)S(1)}, bf16[256,1024]{1,0:T(8,128)(2,1)S(1)}, u32[]{:S(2)}, u32[]{:S(2)}) collective-permute-start(bf16[256,1024]{1,0:T(8,128)(2,1)S(1)} %fusion.94), channel_id=1, source_target_pairs={{2,0},{4,2},{6,4},{7,6},{5,7},{3,5},{1,3},{0,1},{10,8},{12,10},{14... | collective-permute-start | bytes 1572872 | tf_op jit(solution)/shard_map/ppermute | solution.py:362
  117.5 20.2 %collective-permute-start.27 = (bf16[256,1024]{1,0:T(8,128)(2,1)S(1)}, bf16[256,1024]{1,0:T(8,128)(2,1)S(1)}, u32[]{:S(2)}, u32[]{:S(2)}) collective-permute-start(bf16[256,1024]{1,0:T(8,128)(2,1)S(1)} %fusion.79), channel_id=1, source_target_pairs={{2,0},{4,2},{6,4},{7,6},{5,7},{3,5},{1,3},{0,1},{10,8},{12,10},{14... | collective-permute-start | bytes 1572872 | tf_op jit(solution)/shard_map/ppermute | solution.py:362
  118.8 20.2 %collective-permute-start.23 = (bf16[256,1024]{1,0:T(8,128)(2,1)S(1)}, bf16[256,1024]{1,0:T(8,128)(2,1)S(1)}, u32[]{:S(2)}, u32[]{:S(2)}) collective-permute-start(bf16[256,1024]{1,0:T(8,128)(2,1)S(1)} %fusion.64), channel_id=1, source_target_pairs={{0,2},{2,4},{4,6},{6,7},{7,5},{5,3},{3,1},{1,0},{8,10},{10,12},{12... | collective-permute-start | bytes 1572872 | tf_op jit(solution)/shard_map/ppermute | solution.py:362
  127.8 21.7 %collective-permute-start.20 = (bf16[256,1024]{1,0:T(8,128)(2,1)S(1)}, bf16[256,1024]{1,0:T(8,128)(2,1)S(1)}, u32[]{:S(2)}, u32[]{:S(2)}) collective-permute-start(bf16[256,1024]{1,0:T(8,128)(2,1)S(1)} %fusion.70), channel_id=1, source_target_pairs={{0,2},{2,4},{4,6},{6,7},{7,5},{5,3},{3,1},{1,0},{8,10},{10,12},{12... | collective-permute-start | bytes 1572872 | tf_op jit(solution)/shard_map/ppermute | solution.py:362
  130.2 21.7 %collective-permute-start.17 = (bf16[256,1024]{1,0:T(8,128)(2,1)S(1)}, bf16[256,1024]{1,0:T(8,128)(2,1)S(1)}, u32[]{:S(2)}, u32[]{:S(2)}) collective-permute-start(bf16[256,1024]{1,0:T(8,128)(2,1)S(1)} %fusion.85), channel_id=1, source_target_pairs={{2,0},{4,2},{6,4},{7,6},{5,7},{3,5},{1,3},{0,1},{10,8},{12,10},{14... | collective-permute-start | bytes 1572872 | tf_op jit(solution)/shard_map/ppermute | solution.py:362
  138.5 21.7 %collective-permute-start.28 = (bf16[256,1024]{1,0:T(8,128)(2,1)S(1)}, bf16[256,1024]{1,0:T(8,128)(2,1)S(1)}, u32[]{:S(2)}, u32[]{:S(2)}) collective-permute-start(bf16[256,1024]{1,0:T(8,128)(2,1)S(1)} %fusion.82), channel_id=1, source_target_pairs={{2,0},{4,2},{6,4},{7,6},{5,7},{3,5},{1,3},{0,1},{10,8},{12,10},{14... | collective-permute-start | bytes 1572872 | tf_op jit(solution)/shard_map/ppermute | solution.py:362
  139.9 21.7 %collective-permute-start.24 = (bf16[256,1024]{1,0:T(8,128)(2,1)S(1)}, bf16[256,1024]{1,0:T(8,128)(2,1)S(1)}, u32[]{:S(2)}, u32[]{:S(2)}) collective-permute-start(bf16[256,1024]{1,0:T(8,128)(2,1)S(1)} %fusion.67), channel_id=1, source_target_pairs={{0,2},{2,4},{4,6},{6,7},{7,5},{5,3},{3,1},{1,0},{8,10},{10,12},{12... | collective-permute-start | bytes 1572872 | tf_op jit(solution)/shard_map/ppermute | solution.py:362
  150.3 21.7 %collective-permute-start.21 = (bf16[256,1024]{1,0:T(8,128)(2,1)S(1)}, bf16[256,1024]{1,0:T(8,128)(2,1)S(1)}, u32[]{:S(2)}, u32[]{:S(2)}) collective-permute-start(bf16[256,1024]{1,0:T(8,128)(2,1)S(1)} %fusion.76), channel_id=1, source_target_pairs={{0,2},{2,4},{4,6},{6,7},{7,5},{5,3},{3,1},{1,0},{8,10},{10,12},{12... | collective-permute-start | bytes 1572872 | tf_op jit(solution)/shard_map/ppermute | solution.py:362
  152.7 20.0 %collective-permute-start.18 = (bf16[256,1024]{1,0:T(8,128)(2,1)S(1)}, bf16[256,1024]{1,0:T(8,128)(2,1)S(1)}, u32[]{:S(2)}, u32[]{:S(2)}) collective-permute-start(bf16[256,1024]{1,0:T(8,128)(2,1)S(1)} %fusion.91), channel_id=1, source_target_pairs={{2,0},{4,2},{6,4},{7,6},{5,7},{3,5},{1,3},{0,1},{10,8},{12,10},{14... | collective-permute-start | bytes 1572872 | tf_op jit(solution)/shard_map/ppermute | solution.py:362
  161.0 20.5 %collective-permute-start.29 = (bf16[256,1024]{1,0:T(8,128)(2,1)S(1)}, bf16[256,1024]{1,0:T(8,128)(2,1)S(1)}, u32[]{:S(2)}, u32[]{:S(2)}) collective-permute-start(bf16[256,1024]{1,0:T(8,128)(2,1)S(1)} %fusion.88), channel_id=1, source_target_pairs={{2,0},{4,2},{6,4},{7,6},{5,7},{3,5},{1,3},{0,1},{10,8},{12,10},{14... | collective-permute-start | bytes 1572872 | tf_op jit(solution)/shard_map/ppermute | solution.py:362
  162.3 19.4 %collective-permute-start.25 = (bf16[256,1024]{1,0:T(8,128)(2,1)S(1)}, bf16[256,1024]{1,0:T(8,128)(2,1)S(1)}, u32[]{:S(2)}, u32[]{:S(2)}) collective-permute-start(bf16[256,1024]{1,0:T(8,128)(2,1)S(1)} %fusion.73), channel_id=1, source_target_pairs={{0,2},{2,4},{4,6},{6,7},{7,5},{5,3},{3,1},{1,0},{8,10},{10,12},{12... | collective-permute-start | bytes 1572872 | tf_op jit(solution)/shard_map/ppermute | solution.py:362

commit v2 on v1

--- a/solution.py
+++ b/solution.py
@@ -150,26 +150,27 @@
 
 def keys_body(pieces, size, block, *refs):
     xs = refs[:pieces]
-    w_key, w_value, key_sum, value_sum, keys_out, values_out, state_out = refs[pieces:]
+    w_key, w_value, key_sum, value_sum, keys_out, values_out, state_out, sent_out = refs[pieces:]
     heads = block // size
     chunk = jnp.concatenate([x[...] for x in xs], 0)
-
-    @pl.loop(0, keys_out.shape[1] // block)
-    def _(j):
-        cut = columns_of(j, block)
+    for j in range(keys_out.shape[1] // block):
+        cut = slice(j * block, (j + 1) * block)
         keys = (key_sum[:, cut] + dot(chunk, w_key[:, cut])).astype(BF16)
         keys_out[:, cut] = keys
         values = (value_sum[:, cut] + dot(chunk, w_value[:, cut])).astype(BF16)
         values_out[:, cut] = values
+        states = dot_rows(keys, values)
         for h in range(heads):
             own = slice(h * size, (h + 1) * size)
-            state_out[j * heads + h] = dot_rows(keys[:, own], values[:, own])
+            state_out[j * heads + h] = states[own, own]
+            sent_out[j * heads + h] = states[own, own].astype(BF16)
 
 
 def finish_keys(chunk, w_key, w_value, key_sum, value_sum, block, size):
     rows, width = key_sum.shape
     arrays = (*chunk, w_key, w_value, key_sum, value_sum)
-    outputs = [((rows, width), BF16)] * 2 + [((width // size, size, size), F32)]
+    outputs = [((rows, width), BF16)] * 2
+    outputs += [((width // size, size, size), kind) for kind in (F32, BF16)]
     body = functools.partial(keys_body, len(chunk), size, block)
     return kernel(body, [(array, pltpu.VMEM) for array in arrays], outputs)
 
@@ -216,22 +217,21 @@
     half = query.shape[0] // 2
     for h in range(heads):
         cut = slice(h * size, (h + 1) * size)
-        prior = carry[h] + jnp.where(odd[0] == 1, partner[h], 0.0)
+        prior = carry[h] + jnp.where(odd[0] == 1, partner[h].astype(F32), 0.0)
         for other in others:
             prior = prior + other[h].astype(F32)
         high = prior.astype(BF16)
         low = (prior - high.astype(F32)).astype(BF16)
         q = query[:, cut]
-        o = within[:, cut] + dot(q, high) + dot(q, low)
+        o = within[:, cut] + dot(jnp.concatenate([q, q], 1), jnp.concatenate([high, low], 0))
         o = o * lax.rsqrt(jnp.mean(o * o, axis=-1, keepdims=True) + EPSILON)
         attended = o.astype(BF16)
         top_out[:, cut] = attended[:half]
         bottom_out[:, cut] = attended[half:]
     block = 256 if w_first.shape[1] % 256 == 0 else 128
 
-    @pl.loop(0, w_first.shape[1] // block)
-    def _(j):
-        cut = columns_of(j, block)
+    for j in range(w_first.shape[1] // block):
+        cut = slice(j * block, (j + 1) * block)
         weight = w_first[:, cut]
         top_first[:, cut] = dot(top_out[...], weight).astype(BF16)
         bottom_first[:, cut] = dot(bottom_out[...], weight).astype(BF16)
@@ -246,13 +246,32 @@
 
 
 def pair_body(own, partner, out):
-    out[...] = (own[...] + partner[...]).astype(BF16)
-
-
-def finish_body(top_sum, bottom_sum, top, bottom, out):
+    out[...] = (own[...] + partner[...].astype(F32)).astype(BF16)
+
+
+def finish_body(top_sum, bottom_sum, top, bottom, out, staged, moved):
     half = top.shape[0]
-    out[:half] = (top_sum[...] + top[...].astype(F32)).astype(BF16)
-    out[half:] = (bottom_sum[...] + bottom[...].astype(F32)).astype(BF16)
+    copies = []
+    for i, (total, last) in enumerate(((top_sum, top), (bottom_sum, bottom))):
+        cut = slice(i * half, (i + 1) * half)
+        staged[cut] = (total[...] + last[...].astype(F32)).astype(BF16)
+        copies.append(pltpu.make_async_copy(staged.at[cut, :], out.at[cut, :], moved.at[i]))
+        copies[-1].start()
+    for copy in copies:
+        copy.wait()
+
+
+def finish(arrays):
+    shape = (2 * arrays[0].shape[0], arrays[0].shape[1])
+    return pl.pallas_call(
+        finish_body,
+        in_specs=[pl.BlockSpec(memory_space=pltpu.VMEM)] * 4,
+        out_specs=pl.BlockSpec(memory_space=pltpu.HBM),
+        out_shape=jax.ShapeDtypeStruct(shape, BF16),
+        scratch_shapes=[pltpu.VMEM(shape, BF16), pltpu.SemaphoreType.DMA((2,))],
+        compiler_params=pltpu.CompilerParams(vmem_limit_bytes=16 << 20),
+        cost_estimate=pl.CostEstimate(flops=0, bytes_accessed=1 << 20, transcendentals=0),
+    )(*arrays)
 
 
 def local(tokens, w_query, w_key, w_value, w_out, carry):
@@ -328,12 +347,12 @@
     ahead, behind = ahead[reach, 0], behind[reach, 1]
     last = [ahead, behind]
     w_query_last, w_key_last, w_value_last, w_first = final
-    keys, values, state = finish_keys(
+    keys, values, state, sent = finish_keys(
         last, w_key_last, w_value_last, sums[1], sums[2], block, size
     )
 
     members = lax.axis_size("seq")
-    partner = lax.ppermute(state, "seq", [(i, i ^ 1) for i in range(members)])
+    partner = lax.ppermute(sent, "seq", [(i, i ^ 1) for i in range(members)])
     pair = kernel(
         pair_body,
         [(state, pltpu.VMEM), (partner, pltpu.VMEM)],
@@ -362,11 +381,7 @@
                 held[rows] = lax.ppermute(value.astype(BF16), "tp", hops)
     top_sum = partial(0, 0) + down[0].astype(F32)
     bottom_sum = partial(1, 0) + up[1].astype(F32)
-    return kernel(
-        finish_body,
-        [(s, pltpu.VMEM) for s in (top_sum, bottom_sum, up[0], down[1])],
-        [((row_count, columns), BF16)],
-    )[0]
+    return finish((top_sum, bottom_sum, up[0], down[1]))
 
 
 def solution(mesh):

time: 183 us -> 182 us (level)
    pallas_call x12 -> x11, Pallas kernels: 45.3 us -> 42.8 us  [kernel(): pl.pallas_call(body, in_specs=[pl.BlockSpec(memory_space=space) for _, sp...]
where the time goes in v2:
time: 182 us; the launch traced here: 181 us
  waiting for transfers between devices  86 us (47%)
  Pallas kernels  43.9 us (24%)
  starting transfers between devices  33.9 us (19%)
  matrix products  15.6 us (9%)
    ppermute x12, waiting for transfers between devices, local(): held[rows] = lax.ppermute(value.astype(BF16), 'tp', hops)  44.3 us
    pallas_call x11, Pallas kernels, kernel(): pl.pallas_call(body, in_specs=[pl.BlockSpec(memory_space=space) for _, sp...  42.8 us
    ppermute x7, waiting for transfers between devices, send(): ahead[level + 1, second] = lax.ppermute(ahead[up], 'tp', forward)  20.7 us
    dot_general x14, matrix products, dot(): return jnp.dot(a, b, preferred_element_type=F32)  15.6 us
    ppermute x7, waiting for transfers between devices, send(): behind[level + 1, 1 - second] = lax.ppermute(behind[down], 'tp', backward)  13.3 us
    ppermute x7, starting transfers between devices, send(): ahead[level + 1, second] = lax.ppermute(ahead[up], 'tp', forward)  13 us
    ppermute x12, starting transfers between devices, local(): held[rows] = lax.ppermute(value.astype(BF16), 'tp', hops)  12.9 us
    ppermute x1, waiting for transfers between devices, local(): down = [None, lax.ppermute(bottom, 'tp', backward)]  6.21 us
  transfers between devices with their start and end apart: 30, of which 22 were waited for; matrix products, arithmetic and copies ran while one was open for 9% of the time, Pallas kernels for 21%

profile of v2, /device:TPU:0, one launch (start us, length us, event | category | flops | bytes accessed | tf_op | source)
XLA Modules:
  0.0 181.4 jit_solution(10970460587539234611)
XLA Ops:
  0.1 1.3 fusion.114
  1.4 3.1 %collective-permute-start = (bf16[256,1024]{1,0:T(8,128)(2,1)S(1)}, bf16[256,1024]{1,0:T(8,128)(2,1)S(1)}, u32[]{:S(2)}, u32[]{:S(2)}) collective-permute-start(bf16[256,1024]{1,0:T(8,128)(2,1)S(1)} %get-tuple-element.230), channel_id=1, source_target_pairs={{0,2},{2,4},{4,6},{6,7},{7,5},{5,3},{3,1},{1,0},{8,10},{10,12},{12... | collective-permute-start | bytes 1572872 | tf_op jit(solution)/shard_map/ppermute | solution.py:319
  4.5 2.0 %collective-permute-start.4 = (bf16[256,1024]{1,0:T(8,128)(2,1)S(1)}, bf16[256,1024]{1,0:T(8,128)(2,1)S(1)}, u32[]{:S(2)}, u32[]{:S(2)}) collective-permute-start(bf16[256,1024]{1,0:T(8,128)(2,1)S(1)} %get-tuple-element.229), channel_id=1, source_target_pairs={{0,2},{2,4},{4,6},{6,7},{7,5},{5,3},{3,1},{1,0},{8,10},{10,12},{12... | collective-permute-start | bytes 1572872 | tf_op jit(solution)/shard_map/ppermute | solution.py:319
  6.5 6.0 %shard_map.64 = (f32[512,768]{1,0:T(8,128)S(1)}, f32[512,768]{1,0:T(8,128)S(1)}, f32[512,768]{1,0:T(8,128)S(1)}, bf16[1024,768]{1,0:T(8,128)(2,1)S(1)}, bf16[102...) custom-call(s32[8]{0:T(128)S(1)} %stack.44.refs_0_.refs_7_, bf16[512,1024]{1,0:T(8,128)(2,1)S(1)} %copy-done, ...), custom_call_target="tpu_custom_call" | custom-call | bytes 1048576 | tf_op jit(solution)/shard_map/pallas_call | solution.py:57
  12.6 4.6 %collective-permute-done.refs_1_ = bf16[256,1024]{1,0:T(8,128)(2,1)S(1)} collective-permute-done((bf16[256,1024]{1,0:T(8,128)(2,1)S(1)}, bf16[256,1024]{1,0:T(8,128)(2,1)S(1)}, u32[]{:S(2)}, u32[]{:S(2)}) %collective-permute-start) | collective-permute-done | bytes 524320 | tf_op jit(solution)/shard_map/ppermute | solution.py:319
  17.2 2.2 %collective-permute-done.1.refs_2_ = bf16[256,1024]{1,0:T(8,128)(2,1)S(1)} collective-permute-done((bf16[256,1024]{1,0:T(8,128)(2,1)S(1)}, bf16[256,1024]{1,0:T(8,128)(2,1)S(1)}, u32[]{:S(2)}, u32[]{:S(2)}) %collective-permute-start.1) | collective-permute-done | bytes 524320 | tf_op jit(solution)/shard_map/ppermute | solution.py:320
  19.4 1.6 collective-permute-start.2
  21.4 7.0 %collective-permute-done.4.refs_2_ = bf16[256,1024]{1,0:T(8,128)(2,1)S(1)} collective-permute-done((bf16[256,1024]{1,0:T(8,128)(2,1)S(1)}, bf16[256,1024]{1,0:T(8,128)(2,1)S(1)}, u32[]{:S(2)}, u32[]{:S(2)}) %collective-permute-start.4) | collective-permute-done | bytes 524320 | tf_op jit(solution)/shard_map/ppermute | solution.py:319
  28.4 2.2 %collective-permute-done.5.refs_1_ = bf16[256,1024]{1,0:T(8,128)(2,1)S(1)} collective-permute-done((bf16[256,1024]{1,0:T(8,128)(2,1)S(1)}, bf16[256,1024]{1,0:T(8,128)(2,1)S(1)}, u32[]{:S(2)}, u32[]{:S(2)}) %collective-permute-start.5) | collective-permute-done | bytes 524320 | tf_op jit(solution)/shard_map/ppermute | solution.py:320
  30.6 1.6 collective-permute-start.8
  32.6 4.7 %shard_map.65 = (f32[512,768]{1,0:T(8,128)S(1)}, f32[512,768]{1,0:T(8,128)S(1)}, f32[512,768]{1,0:T(8,128)S(1)}, bf16[1024,768]{1,0:T(8,128)(2,1)S(1)}, bf16[102...) custom-call(s32[8]{0:T(128)S(1)} %stack.44.refs_0_.refs_7_, ...), custom_call_target="tpu_custom_call", output_to_operand_aliasing={{0}: (9, {}), {1}: (10, {}), {2}: (11, {})} | custom-call | bytes 1048576 | tf_op jit(solution)/shard_map/pallas_call | solution.py:57
  37.4 2.3 %collective-permute-done.2.refs_1_ = bf16[256,1024]{1,0:T(8,128)(2,1)S(1)} collective-permute-done((bf16[256,1024]{1,0:T(8,128)(2,1)S(1)}, bf16[256,1024]{1,0:T(8,128)(2,1)S(1)}, u32[]{:S(2)}, u32[]{:S(2)}) %collective-permute-start.2) | collective-permute-done | bytes 524320 | tf_op jit(solution)/shard_map/ppermute | solution.py:319
  39.6 2.2 %collective-permute-done.3.refs_2_ = bf16[256,1024]{1,0:T(8,128)(2,1)S(1)} collective-permute-done((bf16[256,1024]{1,0:T(8,128)(2,1)S(1)}, bf16[256,1024]{1,0:T(8,128)(2,1)S(1)}, u32[]{:S(2)}, u32[]{:S(2)}) %collective-permute-start.3) | collective-permute-done | bytes 524320 | tf_op jit(solution)/shard_map/ppermute | solution.py:320
  41.8 1.6 collective-permute-start.6
  43.9 4.8 %shard_map.66 = (f32[512,768]{1,0:T(8,128)S(1)}, f32[512,768]{1,0:T(8,128)S(1)}, f32[512,768]{1,0:T(8,128)S(1)}, bf16[1024,768]{1,0:T(8,128)(2,1)S(1)}, bf16[102...) custom-call(s32[8]{0:T(128)S(1)} %stack.44.refs_0_.refs_7_, ...), custom_call_target="tpu_custom_call", output_to_operand_aliasing={{0}: (9, {}), {1}: (10, {}), {2}: (11, {})} | custom-call | bytes 1048576 | tf_op jit(solution)/shard_map/pallas_call | solution.py:57
  48.6 2.3 %collective-permute-done.8.refs_2_ = bf16[256,1024]{1,0:T(8,128)(2,1)S(1)} collective-permute-done((bf16[256,1024]{1,0:T(8,128)(2,1)S(1)}, bf16[256,1024]{1,0:T(8,128)(2,1)S(1)}, u32[]{:S(2)}, u32[]{:S(2)}) %collective-permute-start.8) | collective-permute-done | bytes 524320 | tf_op jit(solution)/shard_map/ppermute | solution.py:319
  50.9 2.2 %collective-permute-done.9.refs_1_ = bf16[256,1024]{1,0:T(8,128)(2,1)S(1)} collective-permute-done((bf16[256,1024]{1,0:T(8,128)(2,1)S(1)}, bf16[256,1024]{1,0:T(8,128)(2,1)S(1)}, u32[]{:S(2)}, u32[]{:S(2)}) %collective-permute-start.9) | collective-permute-done | bytes 524320 | tf_op jit(solution)/shard_map/ppermute | solution.py:320
  53.1 1.6 collective-permute-start.12
  55.1 4.8 %shard_map.67 = (f32[512,768]{1,0:T(8,128)S(1)}, f32[512,768]{1,0:T(8,128)S(1)}, f32[512,768]{1,0:T(8,128)S(1)}, bf16[1024,768]{1,0:T(8,128)(2,1)S(1)}, bf16[102...) custom-call(s32[8]{0:T(128)S(1)} %stack.44.refs_0_.refs_7_, ...), custom_call_target="tpu_custom_call", output_to_operand_aliasing={{0}: (9, {}), {1}: (10, {}), {2}: (11, {})} | custom-call | bytes 1048576 | tf_op jit(solution)/shard_map/pallas_call | solution.py:57
  59.9 2.3 %collective-permute-done.6.refs_1_ = bf16[256,1024]{1,0:T(8,128)(2,1)S(1)} collective-permute-done((bf16[256,1024]{1,0:T(8,128)(2,1)S(1)}, bf16[256,1024]{1,0:T(8,128)(2,1)S(1)}, u32[]{:S(2)}, u32[]{:S(2)}) %collective-permute-start.6) | collective-permute-done | bytes 524320 | tf_op jit(solution)/shard_map/ppermute | solution.py:319
  62.1 2.2 %collective-permute-done.7.refs_2_ = bf16[256,1024]{1,0:T(8,128)(2,1)S(1)} collective-permute-done((bf16[256,1024]{1,0:T(8,128)(2,1)S(1)}, bf16[256,1024]{1,0:T(8,128)(2,1)S(1)}, u32[]{:S(2)}, u32[]{:S(2)}) %collective-permute-start.7) | collective-permute-done | bytes 524320 | tf_op jit(solution)/shard_map/ppermute | solution.py:320
  64.3 1.6 collective-permute-start.10
  66.3 4.8 %shard_map.68 = (f32[512,768]{1,0:T(8,128)S(1)}, f32[512,768]{1,0:T(8,128)S(1)}, f32[512,768]{1,0:T(8,128)S(1)}, bf16[1024,768]{1,0:T(8,128)(2,1)S(1)}, bf16[102...) custom-call(s32[8]{0:T(128)S(1)} %stack.44.refs_0_.refs_7_, ...), custom_call_target="tpu_custom_call", output_to_operand_aliasing={{0}: (9, {}), {1}: (10, {}), {2}: (11, {})} | custom-call | bytes 1048576 | tf_op jit(solution)/shard_map/pallas_call | solution.py:57
  71.1 2.3 %collective-permute-done.12.refs_2_ = bf16[256,1024]{1,0:T(8,128)(2,1)S(1)} collective-permute-done((bf16[256,1024]{1,0:T(8,128)(2,1)S(1)}, bf16[256,1024]{1,0:T(8,128)(2,1)S(1)}, u32[]{:S(2)}, u32[]{:S(2)}) %collective-permute-start.12) | collective-permute-done | bytes 524320 | tf_op jit(solution)/shard_map/ppermute | solution.py:319
  73.4 2.2 %collective-permute-done.13.refs_1_ = bf16[256,1024]{1,0:T(8,128)(2,1)S(1)} collective-permute-done((bf16[256,1024]{1,0:T(8,128)(2,1)S(1)}, bf16[256,1024]{1,0:T(8,128)(2,1)S(1)}, u32[]{:S(2)}, u32[]{:S(2)}) %collective-permute-start.13) | collective-permute-done | bytes 524320 | tf_op jit(solution)/shard_map/ppermute | solution.py:320
  75.5 4.8 %shard_map.69 = (f32[512,768]{1,0:T(8,128)S(1)}, f32[512,768]{1,0:T(8,128)S(1)}, f32[512,768]{1,0:T(8,128)S(1)}, bf16[1024,768]{1,0:T(8,128)(2,1)S(1)}, bf16[102...) custom-call(s32[8]{0:T(128)S(1)} %stack.44.refs_0_.refs_7_, ...), custom_call_target="tpu_custom_call", output_to_operand_aliasing={{0}: (9, {}), {1}: (10, {}), {2}: (11, {})} | custom-call | bytes 1048576 | tf_op jit(solution)/shard_map/pallas_call | solution.py:57
  80.3 4.8 %shard_map.70 = (f32[512,768]{1,0:T(8,128)S(1)}, f32[512,768]{1,0:T(8,128)S(1)}, f32[512,768]{1,0:T(8,128)S(1)}, bf16[1024,768]{1,0:T(8,128)(2,1)S(1)}, bf16[102...) custom-call(s32[8]{0:T(128)S(1)} %stack.44.refs_0_.refs_7_, ...), custom_call_target="tpu_custom_call", output_to_operand_aliasing={{0}: (11, {}), {1}: (12, {}), {2}: (13, {})} | custom-call | bytes 1048576 | tf_op jit(solution)/shard_map/pallas_call | solution.py:57
  85.3 2.4 %shard_map.71 = (bf16[512,768]{1,0:T(8,128)(2,1)S(1)}, bf16[512,768]{1,0:T(8,128)(2,1)S(1)}, f32[6,128,128]{2,1,0:T(8,128)S(1)}, bf16[6,128,128]{2,1,0:T(8,128)(2,1)S(1)}) custom-call(bf16[256,1024]{1,0:T(8,128)(2,1)S(1)} %collective-permute-done.10.refs_0_, bf16[256,1024]{1,0:T(8,128)(2,1)S(1)} %collective-permute-done.11.refs_1_, ...), custom_call_target="tpu_custom_call" | custom-call | bytes 1048576 | tf_op jit(solution)/shard_map/pallas_call | solution.py:57
  87.8 1.4 collective-permute-done.14.partner
  89.3 3.6 %collective-permute-start.15 = (bf16[6,128,128]{2,1,0:T(8,128)(2,1)S(1)}, bf16[6,128,128]{2,1,0:T(8,128)(2,1)S(1)}, u32[]{:S(2)}, u32[]{:S(2)}) collective-permute-start(bf16[6,128,128]{2,1,0:T(8,128)(2,1)S(1)} %shard_map.73), channel_id=1, source_target_pairs={{0,16},{8,24},{1,17},{9,25},{2,18},{10,26},{3,19},{11,27},{4,20},{... | collective-permute-start | bytes 589832 | tf_op jit(solution)/shard_map/ppermute | solution.py:362
  92.9 4.4 %shard_map.72 = (bf16[512,768]{1,0:T(8,128)(2,1)S(1)}, f32[512,768]{1,0:T(8,128)S(1)}) custom-call(bf16[256,1024]{1,0:T(8,128)(2,1)S(1)} %collective-permute-done.10.refs_0_, bf16[256,1024]{1,0:T(8,128)(2,1)S(1)} %collective-permute-done.11.refs_1_, bf16[1024,768]{1,0:T(8,128)(2,1)S(1)} %get-tuple-element.205.refs_2_, ...), custom_call_target="tpu_custom_call" | custom-call | bytes 1048576 | tf_op jit(solution)/shard_map/pallas_call | solution.py:57
  97.3 1.4 shard_map.74
  98.8 0.5 collective-permute-start.26
  99.3 1.6 collective-permute-start.22
  100.9 2.2 %fusion.97 = bf16[256,1024]{1,0:T(8,128)(2,1)S(1)} fusion(bf16[256,768]{1,0:T(8,128)(2,1)S(1)} %get-tuple-element.223, bf16[768,8192]{1,0:T(8,128)(2,1)} %refs_6_.1, s32[]{:T(128)} %mul.38), kind=kOutput, calls=%fused_computation.51 | convolution fusion | flops 402915328 | bytes 2490880 | tf_op jit(solution)/shard_map/dot_general | solution.py:45
  103.1 1.6 collective-permute-start.19
  104.7 2.2 %fusion.94 = bf16[256,1024]{1,0:T(8,128)(2,1)S(1)} fusion(bf16[256,768]{1,0:T(8,128)(2,1)S(1)} %get-tuple-element.218, bf16[768,8192]{1,0:T(8,128)(2,1)} %refs_6_.1, s32[]{:T(128)} %mul.32), kind=kOutput, calls=%fused_computation.50 | convolution fusion | flops 402915328 | bytes 2490880 | tf_op jit(solution)/shard_map/dot_general | solution.py:45
  107.4 6.2 %collective-permute-done.26 = bf16[256,1024]{1,0:T(8,128)(2,1)S(1)} collective-permute-done((bf16[256,1024]{1,0:T(8,128)(2,1)S(1)}, bf16[256,1024]{1,0:T(8,128)(2,1)S(1)}, u32[]{:S(2)}, u32[]{:S(2)}) %collective-permute-start.26) | collective-permute-done | bytes 524320 | tf_op jit(solution)/shard_map/ppermute | solution.py:374
  113.6 2.3 %fusion.79 = bf16[256,1024]{1,0:T(8,128)(2,1)S(1)} fusion(bf16[256,768]{1,0:T(8,128)(2,1)S(1)} %get-tuple-element.223, bf16[768,8192]{1,0:T(8,128)(2,1)} %refs_6_.1, s32[]{:T(128)} %mul.32, bf16[256,1024]{1,0:T(8,128)(2,1)S(1)} %collective-permute-done.26), kind=kOutput, calls=%fused_computation.45 | convolution fusion | flops 403439616 | bytes 3015168 | tf_op jit(solution)/shard_map/dot_general | solution.py:45
  116.4 0.8 fusion.64
  117.2 1.7 collective-permute-start.23
  118.9 6.5 %collective-permute-done.19 = bf16[256,1024]{1,0:T(8,128)(2,1)S(1)} collective-permute-done((bf16[256,1024]{1,0:T(8,128)(2,1)S(1)}, bf16[256,1024]{1,0:T(8,128)(2,1)S(1)}, u32[]{:S(2)}, u32[]{:S(2)}) %collective-permute-start.19) | collective-permute-done | bytes 524320 | tf_op jit(solution)/shard_map/ppermute | solution.py:381
  125.4 0.8 fusion.70
  126.2 1.6 collective-permute-start.20
  127.8 0.8 fusion.85
  128.6 0.5 collective-permute-start.17
  129.1 7.0 %collective-permute-done.27 = bf16[256,1024]{1,0:T(8,128)(2,1)S(1)} collective-permute-done((bf16[256,1024]{1,0:T(8,128)(2,1)S(1)}, bf16[256,1024]{1,0:T(8,128)(2,1)S(1)}, u32[]{:S(2)}, u32[]{:S(2)}) %collective-permute-start.27) | collective-permute-done | bytes 524320 | tf_op jit(solution)/shard_map/ppermute | solution.py:381
  136.1 0.8 fusion.82
  137.4 0.8 fusion.67
  138.2 1.6 collective-permute-start.24
  139.9 8.0 %collective-permute-done.20 = bf16[256,1024]{1,0:T(8,128)(2,1)S(1)} collective-permute-done((bf16[256,1024]{1,0:T(8,128)(2,1)S(1)}, bf16[256,1024]{1,0:T(8,128)(2,1)S(1)}, u32[]{:S(2)}, u32[]{:S(2)}) %collective-permute-start.20) | collective-permute-done | bytes 524320 | tf_op jit(solution)/shard_map/ppermute | solution.py:381
  147.8 0.8 fusion.76
  148.6 1.6 collective-permute-start.21
  150.3 0.8 fusion.91
  151.6 7.0 %collective-permute-done.28 = bf16[256,1024]{1,0:T(8,128)(2,1)S(1)} collective-permute-done((bf16[256,1024]{1,0:T(8,128)(2,1)S(1)}, bf16[256,1024]{1,0:T(8,128)(2,1)S(1)}, u32[]{:S(2)}, u32[]{:S(2)}) %collective-permute-start.28) | collective-permute-done | bytes 524320 | tf_op jit(solution)/shard_map/ppermute | solution.py:381
  158.6 0.8 fusion.88
  159.4 0.7 collective-permute-start.29
  160.1 0.8 fusion.73
  160.9 1.6 collective-permute-start.25
  162.6 7.8 %collective-permute-done.21 = bf16[256,1024]{1,0:T(8,128)(2,1)S(1)} collective-permute-done((bf16[256,1024]{1,0:T(8,128)(2,1)S(1)}, bf16[256,1024]{1,0:T(8,128)(2,1)S(1)}, u32[]{:S(2)}, u32[]{:S(2)}) %collective-permute-start.21) | collective-permute-done | bytes 524320 | tf_op jit(solution)/shard_map/ppermute | solution.py:381
  170.3 0.8 fusion.31.bottom_sum
  171.1 0.8 fusion.28.top_sum
  171.9 8.0 %collective-permute-done.29.bottom = bf16[256,1024]{1,0:T(8,128)(2,1)S(1)} collective-permute-done((bf16[256,1024]{1,0:T(8,128)(2,1)S(1)}, bf16[256,1024]{1,0:T(8,128)(2,1)S(1)}, u32[]{:S(2)}, u32[]{:S(2)}) %collective-permute-start.29) | collective-permute-done | bytes 524320 | tf_op jit(solution)/shard_map/ppermute | solution.py:381
  180.1 1.1 shard_map.75
  (35 shorter events, 4.8 us)
Async XLA Ops:
  0.0 6.5 %copy-start = (bf16[512,1024]{1,0:T(8,128)(2,1)S(1)}, bf16[512,1024]{1,0:T(8,128)(2,1)}, u32[]{:S(2)}) copy-start(bf16[512,1024]{1,0:T(8,128)(2,1)} %refs_1_) | copy-start | bytes 3145732
  1.4 15.7 %collective-permute-start = (bf16[256,1024]{1,0:T(8,128)(2,1)S(1)}, bf16[256,1024]{1,0:T(8,128)(2,1)S(1)}, u32[]{:S(2)}, u32[]{:S(2)}) collective-permute-start(bf16[256,1024]{1,0:T(8,128)(2,1)S(1)} %get-tuple-element.230), channel_id=1, source_target_pairs={{0,2},{2,4},{4,6},{6,7},{7,5},{5,3},{3,1},{1,0},{8,10},{10,12},{12... | collective-permute-start | bytes 1572872 | tf_op jit(solution)/shard_map/ppermute | solution.py:319
  4.5 14.8 %collective-permute-start.1 = (bf16[256,1024]{1,0:T(8,128)(2,1)S(1)}, bf16[256,1024]{1,0:T(8,128)(2,1)S(1)}, u32[]{:S(2)}, u32[]{:S(2)}) collective-permute-start(bf16[256,1024]{1,0:T(8,128)(2,1)S(1)} %get-tuple-element.229), channel_id=1, source_target_pairs={{2,0},{4,2},{6,4},{7,6},{5,7},{3,5},{1,3},{0,1},{10,8},{12,10},{14... | collective-permute-start | bytes 1572872 | tf_op jit(solution)/shard_map/ppermute | solution.py:320
  4.5 23.9 %collective-permute-start.4 = (bf16[256,1024]{1,0:T(8,128)(2,1)S(1)}, bf16[256,1024]{1,0:T(8,128)(2,1)S(1)}, u32[]{:S(2)}, u32[]{:S(2)}) collective-permute-start(bf16[256,1024]{1,0:T(8,128)(2,1)S(1)} %get-tuple-element.229), channel_id=1, source_target_pairs={{0,2},{2,4},{4,6},{6,7},{7,5},{5,3},{3,1},{1,0},{8,10},{10,12},{12... | collective-permute-start | bytes 1572872 | tf_op jit(solution)/shard_map/ppermute | solution.py:319
  6.5 24.1 %collective-permute-start.5 = (bf16[256,1024]{1,0:T(8,128)(2,1)S(1)}, bf16[256,1024]{1,0:T(8,128)(2,1)S(1)}, u32[]{:S(2)}, u32[]{:S(2)}) collective-permute-start(bf16[256,1024]{1,0:T(8,128)(2,1)S(1)} %get-tuple-element.230), channel_id=1, source_target_pairs={{2,0},{4,2},{6,4},{7,6},{5,7},{3,5},{1,3},{0,1},{10,8},{12,10},{14... | collective-permute-start | bytes 1572872 | tf_op jit(solution)/shard_map/ppermute | solution.py:320
  19.4 20.3 %collective-permute-start.2 = (bf16[256,1024]{1,0:T(8,128)(2,1)S(1)}, bf16[256,1024]{1,0:T(8,128)(2,1)S(1)}, u32[]{:S(2)}, u32[]{:S(2)}) collective-permute-start(bf16[256,1024]{1,0:T(8,128)(2,1)S(1)} %collective-permute-done.refs_1_), channel_id=1, source_target_pairs={{0,2},{2,4},{4,6},{6,7},{7,5},{5,3},{3,1},{1,0},{8,10},{10,12},{12... | collective-permute-start | bytes 1572872 | tf_op jit(solution)/shard_map/ppermute | solution.py:319
  20.9 20.9 %collective-permute-start.3 = (bf16[256,1024]{1,0:T(8,128)(2,1)S(1)}, bf16[256,1024]{1,0:T(8,128)(2,1)S(1)}, u32[]{:S(2)}, u32[]{:S(2)}) collective-permute-start(bf16[256,1024]{1,0:T(8,128)(2,1)S(1)} %collective-permute-done.1.refs_2_), channel_id=1, source_target_pairs={{2,0},{4,2},{6,4},{7,6},{5,7},{3,5},{1,3},{0,1},{10,8},{12,10},{14... | collective-permute-start | bytes 1572872 | tf_op jit(solution)/shard_map/ppermute | solution.py:320
  30.6 20.3 %collective-permute-start.8 = (bf16[256,1024]{1,0:T(8,128)(2,1)S(1)}, bf16[256,1024]{1,0:T(8,128)(2,1)S(1)}, u32[]{:S(2)}, u32[]{:S(2)}) collective-permute-start(bf16[256,1024]{1,0:T(8,128)(2,1)S(1)} %collective-permute-done.4.refs_2_), channel_id=1, source_target_pairs={{0,2},{2,4},{4,6},{6,7},{7,5},{5,3},{3,1},{1,0},{8,10},{10,12},{12... | collective-permute-start | bytes 1572872 | tf_op jit(solution)/shard_map/ppermute | solution.py:319
  32.2 20.9 %collective-permute-start.9 = (bf16[256,1024]{1,0:T(8,128)(2,1)S(1)}, bf16[256,1024]{1,0:T(8,128)(2,1)S(1)}, u32[]{:S(2)}, u32[]{:S(2)}) collective-permute-start(bf16[256,1024]{1,0:T(8,128)(2,1)S(1)} %collective-permute-done.5.refs_1_), channel_id=1, source_target_pairs={{2,0},{4,2},{6,4},{7,6},{5,7},{3,5},{1,3},{0,1},{10,8},{12,10},{14... | collective-permute-start | bytes 1572872 | tf_op jit(solution)/shard_map/ppermute | solution.py:320
  41.8 20.3 %collective-permute-start.6 = (bf16[256,1024]{1,0:T(8,128)(2,1)S(1)}, bf16[256,1024]{1,0:T(8,128)(2,1)S(1)}, u32[]{:S(2)}, u32[]{:S(2)}) collective-permute-start(bf16[256,1024]{1,0:T(8,128)(2,1)S(1)} %collective-permute-done.2.refs_1_), channel_id=1, source_target_pairs={{0,2},{2,4},{4,6},{6,7},{7,5},{5,3},{3,1},{1,0},{8,10},{10,12},{12... | collective-permute-start | bytes 1572872 | tf_op jit(solution)/shard_map/ppermute | solution.py:319
  43.4 20.9 %collective-permute-start.7 = (bf16[256,1024]{1,0:T(8,128)(2,1)S(1)}, bf16[256,1024]{1,0:T(8,128)(2,1)S(1)}, u32[]{:S(2)}, u32[]{:S(2)}) collective-permute-start(bf16[256,1024]{1,0:T(8,128)(2,1)S(1)} %collective-permute-done.3.refs_2_), channel_id=1, source_target_pairs={{2,0},{4,2},{6,4},{7,6},{5,7},{3,5},{1,3},{0,1},{10,8},{12,10},{14... | collective-permute-start | bytes 1572872 | tf_op jit(solution)/shard_map/ppermute | solution.py:320
  53.1 20.3 %collective-permute-start.12 = (bf16[256,1024]{1,0:T(8,128)(2,1)S(1)}, bf16[256,1024]{1,0:T(8,128)(2,1)S(1)}, u32[]{:S(2)}, u32[]{:S(2)}) collective-permute-start(bf16[256,1024]{1,0:T(8,128)(2,1)S(1)} %collective-permute-done.8.refs_2_), channel_id=1, source_target_pairs={{0,2},{2,4},{4,6},{6,7},{7,5},{5,3},{3,1},{1,0},{8,10},{10,12},{12... | collective-permute-start | bytes 1572872 | tf_op jit(solution)/shard_map/ppermute | solution.py:319
  54.6 20.9 %collective-permute-start.13 = (bf16[256,1024]{1,0:T(8,128)(2,1)S(1)}, bf16[256,1024]{1,0:T(8,128)(2,1)S(1)}, u32[]{:S(2)}, u32[]{:S(2)}) collective-permute-start(bf16[256,1024]{1,0:T(8,128)(2,1)S(1)} %collective-permute-done.9.refs_1_), channel_id=1, source_target_pairs={{2,0},{4,2},{6,4},{7,6},{5,7},{3,5},{1,3},{0,1},{10,8},{12,10},{14... | collective-permute-start | bytes 1572872 | tf_op jit(solution)/shard_map/ppermute | solution.py:320
  64.3 20.8 %collective-permute-start.10 = (bf16[256,1024]{1,0:T(8,128)(2,1)S(1)}, bf16[256,1024]{1,0:T(8,128)(2,1)S(1)}, u32[]{:S(2)}, u32[]{:S(2)}) collective-permute-start(bf16[256,1024]{1,0:T(8,128)(2,1)S(1)} %collective-permute-done.6.refs_1_), channel_id=1, source_target_pairs={{0,2},{2,4},{4,6},{6,7},{7,5},{5,3},{3,1},{1,0},{8,10},{10,12},{12... | collective-permute-start | bytes 1572872 | tf_op jit(solution)/shard_map/ppermute | solution.py:319
  65.9 19.4 %collective-permute-start.11 = (bf16[256,1024]{1,0:T(8,128)(2,1)S(1)}, bf16[256,1024]{1,0:T(8,128)(2,1)S(1)}, u32[]{:S(2)}, u32[]{:S(2)}) collective-permute-start(bf16[256,1024]{1,0:T(8,128)(2,1)S(1)} %collective-permute-done.7.refs_2_), channel_id=1, source_target_pairs={{2,0},{4,2},{6,4},{7,6},{5,7},{3,5},{1,3},{0,1},{10,8},{12,10},{14... | collective-permute-start | bytes 1572872 | tf_op jit(solution)/shard_map/ppermute | solution.py:320
  85.3 31.1 %slice-start = ((s8[12582912]{0:T(1024)(128)(4,1)}), s8[4194304]{0:T(1024)(128)(4,1)S(1)}, s32[]{:S(2)}) async-start(s8[12582912]{0:T(1024)(128)(4,1)} %bitcast.23), calls=%async_computation | async-start | bytes 8388608
  87.7 1.5 collective-permute-start.14
  89.3 8.0 %collective-permute-start.15 = (bf16[6,128,128]{2,1,0:T(8,128)(2,1)S(1)}, bf16[6,128,128]{2,1,0:T(8,128)(2,1)S(1)}, u32[]{:S(2)}, u32[]{:S(2)}) collective-permute-start(bf16[6,128,128]{2,1,0:T(8,128)(2,1)S(1)} %shard_map.73), channel_id=1, source_target_pairs={{0,16},{8,24},{1,17},{9,25},{2,18},{10,26},{3,19},{11,27},{4,20},{... | collective-permute-start | bytes 589832 | tf_op jit(solution)/shard_map/ppermute | solution.py:362
  92.9 4.4 %copy-start.1 = (f32[6,128,128]{2,1,0:T(8,128)S(1)}, f32[6,128,128]{2,1,0:T(8,128)}, u32[]{:S(2)}) copy-start(f32[6,128,128]{2,1,0:T(8,128)} %carry.1) | copy-start | bytes 1179652
  92.9 23.4 %slice-start.1 = ((s8[12582912]{0:T(1024)(128)(4,1)}), s8[4194304]{0:T(1024)(128)(4,1)S(1)}, s32[]{:S(2)}) async-start(s8[12582912]{0:T(1024)(128)(4,1)} %bitcast.23), calls=%async_computation.1 | async-start | bytes 8388608
  97.3 19.1 %slice-start.2 = ((s8[12582912]{0:T(1024)(128)(4,1)}), s8[4194304]{0:T(1024)(128)(4,1)S(1)}, s32[]{:S(2)}) async-start(s8[12582912]{0:T(1024)(128)(4,1)} %bitcast.23), calls=%async_computation.2 | async-start | bytes 8388608
  98.8 14.9 %collective-permute-start.26 = (bf16[256,1024]{1,0:T(8,128)(2,1)S(1)}, bf16[256,1024]{1,0:T(8,128)(2,1)S(1)}, u32[]{:S(2)}, u32[]{:S(2)}) collective-permute-start(bf16[256,1024]{1,0:T(8,128)(2,1)S(1)} %get-tuple-element.228), channel_id=1, source_target_pairs={{2,0},{4,2},{6,4},{7,6},{5,7},{3,5},{1,3},{0,1},{10,8},{12,10},{14... | collective-permute-start | bytes 1572872 | tf_op jit(solution)/shard_map/ppermute | solution.py:374
  99.3 17.1 %collective-permute-start.22 = (bf16[256,1024]{1,0:T(8,128)(2,1)S(1)}, bf16[256,1024]{1,0:T(8,128)(2,1)S(1)}, u32[]{:S(2)}, u32[]{:S(2)}) collective-permute-start(bf16[256,1024]{1,0:T(8,128)(2,1)S(1)} %get-tuple-element.227), channel_id=1, source_target_pairs={{0,2},{2,4},{4,6},{6,7},{7,5},{5,3},{3,1},{1,0},{8,10},{10,12},{12... | collective-permute-start | bytes 1572872 | tf_op jit(solution)/shard_map/ppermute | solution.py:373
  103.1 22.3 %collective-permute-start.19 = (bf16[256,1024]{1,0:T(8,128)(2,1)S(1)}, bf16[256,1024]{1,0:T(8,128)(2,1)S(1)}, u32[]{:S(2)}, u32[]{:S(2)}) collective-permute-start(bf16[256,1024]{1,0:T(8,128)(2,1)S(1)} %fusion.97), channel_id=1, source_target_pairs={{0,2},{2,4},{4,6},{6,7},{7,5},{5,3},{3,1},{1,0},{8,10},{10,12},{12... | collective-permute-start | bytes 1572872 | tf_op jit(solution)/shard_map/ppermute | solution.py:381
  106.9 20.9 %collective-permute-start.16 = (bf16[256,1024]{1,0:T(8,128)(2,1)S(1)}, bf16[256,1024]{1,0:T(8,128)(2,1)S(1)}, u32[]{:S(2)}, u32[]{:S(2)}) collective-permute-start(bf16[256,1024]{1,0:T(8,128)(2,1)S(1)} %fusion.94), channel_id=1, source_target_pairs={{2,0},{4,2},{6,4},{7,6},{5,7},{3,5},{1,3},{0,1},{10,8},{12,10},{14... | collective-permute-start | bytes 1572872 | tf_op jit(solution)/shard_map/ppermute | solution.py:381
  115.9 20.2 %collective-permute-start.27 = (bf16[256,1024]{1,0:T(8,128)(2,1)S(1)}, bf16[256,1024]{1,0:T(8,128)(2,1)S(1)}, u32[]{:S(2)}, u32[]{:S(2)}) collective-permute-start(bf16[256,1024]{1,0:T(8,128)(2,1)S(1)} %fusion.79), channel_id=1, source_target_pairs={{2,0},{4,2},{6,4},{7,6},{5,7},{3,5},{1,3},{0,1},{10,8},{12,10},{14... | collective-permute-start | bytes 1572872 | tf_op jit(solution)/shard_map/ppermute | solution.py:381
  117.2 20.2 %collective-permute-start.23 = (bf16[256,1024]{1,0:T(8,128)(2,1)S(1)}, bf16[256,1024]{1,0:T(8,128)(2,1)S(1)}, u32[]{:S(2)}, u32[]{:S(2)}) collective-permute-start(bf16[256,1024]{1,0:T(8,128)(2,1)S(1)} %fusion.64), channel_id=1, source_target_pairs={{0,2},{2,4},{4,6},{6,7},{7,5},{5,3},{3,1},{1,0},{8,10},{10,12},{12... | collective-permute-start | bytes 1572872 | tf_op jit(solution)/shard_map/ppermute | solution.py:381
  126.2 21.7 %collective-permute-start.20 = (bf16[256,1024]{1,0:T(8,128)(2,1)S(1)}, bf16[256,1024]{1,0:T(8,128)(2,1)S(1)}, u32[]{:S(2)}, u32[]{:S(2)}) collective-permute-start(bf16[256,1024]{1,0:T(8,128)(2,1)S(1)} %fusion.70), channel_id=1, source_target_pairs={{0,2},{2,4},{4,6},{6,7},{7,5},{5,3},{3,1},{1,0},{8,10},{10,12},{12... | collective-permute-start | bytes 1572872 | tf_op jit(solution)/shard_map/ppermute | solution.py:381
  128.6 21.7 %collective-permute-start.17 = (bf16[256,1024]{1,0:T(8,128)(2,1)S(1)}, bf16[256,1024]{1,0:T(8,128)(2,1)S(1)}, u32[]{:S(2)}, u32[]{:S(2)}) collective-permute-start(bf16[256,1024]{1,0:T(8,128)(2,1)S(1)} %fusion.85), channel_id=1, source_target_pairs={{2,0},{4,2},{6,4},{7,6},{5,7},{3,5},{1,3},{0,1},{10,8},{12,10},{14... | collective-permute-start | bytes 1572872 | tf_op jit(solution)/shard_map/ppermute | solution.py:381
  136.9 21.7 %collective-permute-start.28 = (bf16[256,1024]{1,0:T(8,128)(2,1)S(1)}, bf16[256,1024]{1,0:T(8,128)(2,1)S(1)}, u32[]{:S(2)}, u32[]{:S(2)}) collective-permute-start(bf16[256,1024]{1,0:T(8,128)(2,1)S(1)} %fusion.82), channel_id=1, source_target_pairs={{2,0},{4,2},{6,4},{7,6},{5,7},{3,5},{1,3},{0,1},{10,8},{12,10},{14... | collective-permute-start | bytes 1572872 | tf_op jit(solution)/shard_map/ppermute | solution.py:381
  138.2 21.9 %collective-permute-start.24 = (bf16[256,1024]{1,0:T(8,128)(2,1)S(1)}, bf16[256,1024]{1,0:T(8,128)(2,1)S(1)}, u32[]{:S(2)}, u32[]{:S(2)}) collective-permute-start(bf16[256,1024]{1,0:T(8,128)(2,1)S(1)} %fusion.67), channel_id=1, source_target_pairs={{0,2},{2,4},{4,6},{6,7},{7,5},{5,3},{3,1},{1,0},{8,10},{10,12},{12... | collective-permute-start | bytes 1572872 | tf_op jit(solution)/shard_map/ppermute | solution.py:381
  148.6 21.7 %collective-permute-start.21 = (bf16[256,1024]{1,0:T(8,128)(2,1)S(1)}, bf16[256,1024]{1,0:T(8,128)(2,1)S(1)}, u32[]{:S(2)}, u32[]{:S(2)}) collective-permute-start(bf16[256,1024]{1,0:T(8,128)(2,1)S(1)} %fusion.76), channel_id=1, source_target_pairs={{0,2},{2,4},{4,6},{6,7},{7,5},{5,3},{3,1},{1,0},{8,10},{10,12},{12... | collective-permute-start | bytes 1572872 | tf_op jit(solution)/shard_map/ppermute | solution.py:381
  151.1 20.0 %collective-permute-start.18 = (bf16[256,1024]{1,0:T(8,128)(2,1)S(1)}, bf16[256,1024]{1,0:T(8,128)(2,1)S(1)}, u32[]{:S(2)}, u32[]{:S(2)}) collective-permute-start(bf16[256,1024]{1,0:T(8,128)(2,1)S(1)} %fusion.91), channel_id=1, source_target_pairs={{2,0},{4,2},{6,4},{7,6},{5,7},{3,5},{1,3},{0,1},{10,8},{12,10},{14... | collective-permute-start | bytes 1572872 | tf_op jit(solution)/shard_map/ppermute | solution.py:381
  159.4 20.5 %collective-permute-start.29 = (bf16[256,1024]{1,0:T(8,128)(2,1)S(1)}, bf16[256,1024]{1,0:T(8,128)(2,1)S(1)}, u32[]{:S(2)}, u32[]{:S(2)}) collective-permute-start(bf16[256,1024]{1,0:T(8,128)(2,1)S(1)} %fusion.88), channel_id=1, source_target_pairs={{2,0},{4,2},{6,4},{7,6},{5,7},{3,5},{1,3},{0,1},{10,8},{12,10},{14... | collective-permute-start | bytes 1572872 | tf_op jit(solution)/shard_map/ppermute | solution.py:381
  160.9 19.2 %collective-permute-start.25 = (bf16[256,1024]{1,0:T(8,128)(2,1)S(1)}, bf16[256,1024]{1,0:T(8,128)(2,1)S(1)}, u32[]{:S(2)}, u32[]{:S(2)}) collective-permute-start(bf16[256,1024]{1,0:T(8,128)(2,1)S(1)} %fusion.73), channel_id=1, source_target_pairs={{0,2},{2,4},{4,6},{6,7},{7,5},{5,3},{3,1},{1,0},{8,10},{10,12},{12... | collective-permute-start | bytes 1572872 | tf_op jit(solution)/shard_map/ppermute | solution.py:381

commit v3 on v2

--- a/solution.py
+++ b/solution.py
@@ -10,7 +10,7 @@
 EPSILON = 1e-05
 BF16 = jnp.bfloat16
 F32 = jnp.float32
-PROJECT_BYTES = 34 << 20
+PROJECT_BYTES = 32 << 20
 
 
 def ring_order(count):
@@ -70,30 +70,33 @@
     return pl.ds(pl.multiple_of(j * block, block), block)
 
 
-def project_body(pieces, has_sums, has_rows, block, place, next_place, has_columns, *refs):
+def project_body(pieces, has_sums, has_rows, block, place, bring, has_columns, *refs):
     starts, xs, refs = refs[0], refs[1 : 1 + pieces], refs[1 + pieces :]
     weights, refs = refs[:3], refs[3:]
     if has_columns:
         (w_out, column_starts), refs = refs[:2], refs[2:]
     held, refs = (refs[:3], refs[3:]) if has_rows else (None, refs)
     sums, refs = (refs[:3], refs[3:]) if has_sums else (None, refs)
-    outs, wanted, refs = refs[:3], refs[3:6], refs[6:]
+    outs, refs = refs[:3], refs[3:]
+    wanted, refs = refs[: 3 * len(bring)], refs[3 * len(bring) :]
     depth = xs[0].shape[1]
 
-    def rows_to(k, targets, semaphores):
+    def rows_to(k, targets, semaphores, first=0):
         rows = pl.ds(pl.multiple_of(starts[k], depth), depth)
         return [
-            pltpu.make_async_copy(weights[i].at[rows, :], targets[i], semaphores.at[i])
+            pltpu.make_async_copy(weights[i].at[rows, :], targets[i], semaphores.at[first + i])
             for i in range(3)
         ]
 
-    brought = []
     if has_columns:
         target, refs = refs[0], refs[1:]
+    brought = []
+    for n, k in enumerate(bring):
+        brought += rows_to(k, wanted[3 * n : 3 * n + 3], refs[0], 3 * n)
+    if has_columns:
         size = target.shape[1]
-        cut = pl.ds(pl.multiple_of(column_starts[next_place], size), size)
-        brought.append(pltpu.make_async_copy(w_out.at[:, cut], target, refs[0].at[3]))
-    brought = rows_to(next_place, wanted, refs[0]) + brought
+        cut = pl.ds(pl.multiple_of(column_starts[bring[0]], size), size)
+        brought.append(pltpu.make_async_copy(w_out.at[:, cut], target, refs[0].at[3 * len(bring)]))
     copies = []
     if not has_rows:
         held = refs[1:4]
@@ -101,27 +104,27 @@
     for copy in (*copies, *brought):
         copy.start()
     chunk = jnp.concatenate([x[...] for x in xs], 0)
-    for i in range(3):
-        if copies:
-            copies[i].wait()
-
-        @pl.loop(0, outs[0].shape[1] // block)
-        def _(j, i=i):
-            cut = columns_of(j, block)
+    for copy in copies:
+        copy.wait()
+
+    @pl.loop(0, outs[0].shape[1] // block)
+    def _(j):
+        cut = columns_of(j, block)
+        for i in range(3):
             part = dot(chunk, held[i][:, cut])
             outs[i][:, cut] = part if sums is None else sums[i][:, cut] + part
 
-    for bring in brought:
-        bring.wait()
-
-
-def project(chunk, starts, place, weights, held, sums, block, next_place, extra=None):
+    for copy in brought:
+        copy.wait()
+
+
+def project(chunk, starts, place, weights, held, sums, block, bring, extra=None):
     rows = sum(piece.shape[0] for piece in chunk)
     depth, width = chunk[0].shape[1], weights[0].shape[1]
     inputs = [(starts, pltpu.SMEM)] + [(array, pltpu.VMEM) for array in chunk]
     inputs += [(weight, pltpu.HBM) for weight in weights]
-    outputs = [((rows, width), F32)] * 3 + [((depth, width), BF16)] * 3
-    scratch = [pltpu.SemaphoreType.DMA((4,))]
+    outputs = [((rows, width), F32)] * 3 + [((depth, width), BF16)] * (3 * len(bring))
+    scratch = [pltpu.SemaphoreType.DMA((3 * len(bring) + 1,))]
     if extra is not None:
         w_out, column_starts, columns = extra
         inputs += [(w_out, pltpu.HBM), (column_starts, pltpu.SMEM)]
@@ -141,11 +144,12 @@
         held is not None,
         block,
         place,
-        next_place,
+        bring,
         extra is not None,
     )
     out = kernel(body, inputs, outputs, aliases, scratch, PROJECT_BYTES)
-    return out[:3], out[3:]
+    sets = [out[3 + 3 * n : 6 + 3 * n] for n in range(len(bring))]
+    return out[:3], sets, out[3 + 3 * len(bring) :]
 
 
 def keys_body(pieces, size, block, *refs):
@@ -185,9 +189,8 @@
         jnp.int32, (tile, tile), 1
     )
 
-    @pl.loop(0, width // block)
-    def _(j):
-        cut = columns_of(j, block)
+    for j in range(width // block):
+        cut = slice(j * block, (j + 1) * block)
         query = (query_sum[:, cut] + dot(chunk, w_query[:, cut])).astype(BF16)
         query_out[:, cut] = query
         keys, values = keys_in[:, cut], values_in[:, cut]
@@ -210,14 +213,14 @@
     return kernel(body, [(array, pltpu.VMEM) for array in arrays], outputs)
 
 
-def attend_body(earlier, size, odd, query, within, carry, partner, *refs):
+def attend_body(earlier, size, query, within, carry, *refs):
     others = refs[:earlier]
     w_first, top_out, bottom_out, top_first, bottom_first = refs[earlier:]
     heads = carry.shape[0]
     half = query.shape[0] // 2
     for h in range(heads):
         cut = slice(h * size, (h + 1) * size)
-        prior = carry[h] + jnp.where(odd[0] == 1, partner[h].astype(F32), 0.0)
+        prior = carry[h]
         for other in others:
             prior = prior + other[h].astype(F32)
         high = prior.astype(BF16)
@@ -237,16 +240,19 @@
         bottom_first[:, cut] = dot(bottom_out[...], weight).astype(BF16)
 
 
-def attend(odd, query, within, carry, partner, others, w_first, size):
+def attend(query, within, carry, others, w_first, size):
     rows, width = query.shape
-    inputs = [(odd, pltpu.SMEM)]
-    inputs += [(s, pltpu.VMEM) for s in (query, within, carry, partner, *others, w_first)]
+    inputs = [(s, pltpu.VMEM) for s in (query, within, carry, *others, w_first)]
     outputs = [((rows // 2, width), BF16)] * 2 + [((rows // 2, w_first.shape[1]), BF16)] * 2
     return kernel(functools.partial(attend_body, len(others), size), inputs, outputs)
 
 
-def pair_body(own, partner, out):
-    out[...] = (own[...] + partner[...].astype(F32)).astype(BF16)
+def share_body(odd, own, *refs):
+    *others, out = refs
+    total = jnp.where(odd[0] == 1, 0.0, own[...])
+    for other in others:
+        total = total + other[...].astype(F32)
+    out[...] = total.astype(BF16)
 
 
 def finish_body(top_sum, bottom_sum, top, bottom, out, staged, moved):
@@ -301,9 +307,19 @@
         (tokens, odd, row_table, column_table, column_starts)
     )
 
-    def add(chunk, offset, held, sums, next_offset, extra=None):
-        places = offsets.index(offset), offsets.index(next_offset)
-        return project(chunk, row_table, places[0], weights, held, sums, block, places[1], extra)
+    def add(item, chunk, held, sums):
+        bring = [i for i in ((1, 2) if item == 0 else (item + 2,)) if i < len(offset_of)]
+        bring = [offsets.index(offset_of[i]) for i in bring]
+        extra = None
+        if item == len(offset_of) - 2:
+            bring, extra = [offsets.index(reach)], (w_out, column_table, columns)
+        now, held = (held[0], held[1:]) if held else (None, [])
+        place = offsets.index(offset_of[item])
+        sums, sets, rest = project(
+            chunk, row_table, place, weights, now, sums, block, bring, extra
+        )
+        held = [*held, *sets, *rest]
+        return sums, held
 
     weights = (w_query, w_key, w_value)
     offset_of = [0]
@@ -325,7 +341,7 @@
 
     send(1)
     send(2)
-    sums, held = add([tokens], 0, None, None, offset_of[1])
+    sums, held = add(0, [tokens], [], None)
     for window in range(2, windows):
         level, second = divmod(window, 2)
         up, down = (level, second), (level, 1 - second)
@@ -334,16 +350,14 @@
         )
         send(window + 1)
         if window > 2:
-            offset, following = offset_of[window - 2], offset_of[window - 1]
-            sums, held = add(halves(offset), offset, held, sums, following)
+            sums, held = add(window - 2, halves(offset_of[window - 2]), held, sums)
     up, down = (reach - 1, 1), (reach - 1, 0)
     ahead[up], behind[down], sums, held = lax.optimization_barrier(
         (ahead[up], behind[down], sums, held)
     )
-    offset, following = offset_of[-2:]
-    sums, held = add(halves(offset), offset, held, sums, following)
-    extra = (w_out, column_table, columns)
-    sums, final = add(halves(following), following, held, sums, reach, extra)
+    for item in (windows - 2, windows - 1):
+        sums, held = add(item, halves(offset_of[item]), held, sums)
+    final = [*held[0], held[1]]
     ahead, behind = ahead[reach, 0], behind[reach, 1]
     last = [ahead, behind]
     w_query_last, w_key_last, w_value_last, w_first = final
@@ -352,19 +366,20 @@
     )
 
     members = lax.axis_size("seq")
-    partner = lax.ppermute(sent, "seq", [(i, i ^ 1) for i in range(members)])
-    pair = kernel(
-        pair_body,
-        [(state, pltpu.VMEM), (partner, pltpu.VMEM)],
-        [(state.shape, BF16)],
-    )[0]
     others = [
-        lax.ppermute(pair, "seq", [(i, i + shift) for i in range(members - shift)])
+        lax.ppermute(sent, "seq", [(i, i + shift) for i in range(members - shift)])
         for shift in range(2, members, 2)
     ]
     query, within = finish_query(last, w_query_last, sums[0], keys, values, block, size)
-
-    *parts, top, bottom = attend(odd, query, within, carry, partner, others, w_first, size)
+    others, query, within = lax.optimization_barrier((others, query, within))
+    share = kernel(
+        share_body,
+        [(odd, pltpu.SMEM), (state, pltpu.VMEM), *[(other, pltpu.VMEM) for other in others]],
+        [(state.shape, BF16)],
+    )[0]
+    others.append(lax.ppermute(share, "seq", [(i, i ^ 1) for i in range(members)]))
+
+    *parts, top, bottom = attend(query, within, carry, others, w_first, size)
 
     def partial(rows, offset):
         start = column_starts[offsets.index(offset)]

time: 182 us -> 181 us (level)
  waiting for transfers between devices: 86 us -> 91.8 us
  Pallas kernels: 43.9 us -> 39.4 us
    pallas_call x11, Pallas kernels: 42.8 us -> 38.3 us  [kernel(): pl.pallas_call(body, in_specs=[pl.BlockSpec(memory_space=space) for _, sp...]
    ppermute x7, waiting for transfers between devices: 20.7 us -> 23.4 us  [send(): ahead[level + 1, second] = lax.ppermute(ahead[up], 'tp', forward)]
  transfers between devices with their start and end apart: 30 -> 30, of which waited for: 22 -> 23; matrix products, arithmetic and copies ran while one was open for 9% -> 8% of each run, Pallas kernels for 21% -> 19%
where the time goes in v3:
time: 181 us
  waiting for transfers between devices  91.8 us (51%)
  Pallas kernels  39.4 us (22%)
  starting transfers between devices  33.9 us (19%)
  matrix products  14.2 us (8%)
    ppermute x12, waiting for transfers between devices, local(): held[rows] = lax.ppermute(value.astype(BF16), 'tp', hops)  46.1 us
    pallas_call x11, Pallas kernels, kernel(): pl.pallas_call(body, in_specs=[pl.BlockSpec(memory_space=space) for _, sp...  38.3 us
    ppermute x7, waiting for transfers between devices, send(): ahead[level + 1, second] = lax.ppermute(ahead[up], 'tp', forward)  23.4 us
    ppermute x7, waiting for transfers between devices, send(): behind[level + 1, 1 - second] = lax.ppermute(behind[down], 'tp', backward)  14.6 us
    dot_general x14, matrix products, dot(): return jnp.dot(a, b, preferred_element_type=F32)  14.2 us
    ppermute x7, starting transfers between devices, send(): ahead[level + 1, second] = lax.ppermute(ahead[up], 'tp', forward)  13 us
    ppermute x12, starting transfers between devices, local(): held[rows] = lax.ppermute(value.astype(BF16), 'tp', hops)  12.9 us
    ppermute x1, waiting for transfers between devices, local(): down = [None, lax.ppermute(bottom, 'tp', backward)]  6.17 us
  transfers between devices with their start and end apart: 30, of which 23 were waited for; matrix products, arithmetic and copies ran while one was open for 8% of the time, Pallas kernels for 19%

profile of v3, /device:TPU:0, one launch (start us, length us, event | category | flops | bytes accessed | tf_op | source)
XLA Modules:
  0.0 181.2 jit_solution(15939149933534514335)
XLA Ops:
  0.1 1.3 fusion.114
  1.4 3.1 %collective-permute-start = (bf16[256,1024]{1,0:T(8,128)(2,1)S(1)}, bf16[256,1024]{1,0:T(8,128)(2,1)S(1)}, u32[]{:S(2)}, u32[]{:S(2)}) collective-permute-start(bf16[256,1024]{1,0:T(8,128)(2,1)S(1)} %get-tuple-element.272), channel_id=1, source_target_pairs={{0,2},{2,4},{4,6},{6,7},{7,5},{5,3},{3,1},{1,0},{8,10},{10,12},{12... | collective-permute-start | bytes 1572872 | tf_op jit(solution)/shard_map/ppermute | solution.py:335
  4.5 2.0 %collective-permute-start.4 = (bf16[256,1024]{1,0:T(8,128)(2,1)S(1)}, bf16[256,1024]{1,0:T(8,128)(2,1)S(1)}, u32[]{:S(2)}, u32[]{:S(2)}) collective-permute-start(bf16[256,1024]{1,0:T(8,128)(2,1)S(1)} %get-tuple-element.271), channel_id=1, source_target_pairs={{0,2},{2,4},{4,6},{6,7},{7,5},{5,3},{3,1},{1,0},{8,10},{10,12},{12... | collective-permute-start | bytes 1572872 | tf_op jit(solution)/shard_map/ppermute | solution.py:335
  6.5 8.3 %shard_map.64 = (f32[512,768]{1,0:T(8,128)S(1)}, f32[512,768]{1,0:T(8,128)S(1)}, f32[512,768]{1,0:T(8,128)S(1)}, bf16[1024,768]{1,0:T(8,128)(2,1)S(1)}, bf16[102...) custom-call(s32[8]{0:T(128)S(1)} %stack.44.refs_0_.refs_7_, ...), custom_call_target="tpu_custom_call" | custom-call | bytes 1048576 | tf_op jit(solution)/shard_map/pallas_call | solution.py:57
  14.8 2.4 %collective-permute-done.refs_1_ = bf16[256,1024]{1,0:T(8,128)(2,1)S(1)} collective-permute-done((bf16[256,1024]{1,0:T(8,128)(2,1)S(1)}, bf16[256,1024]{1,0:T(8,128)(2,1)S(1)}, u32[]{:S(2)}, u32[]{:S(2)}) %collective-permute-start) | collective-permute-done | bytes 524320 | tf_op jit(solution)/shard_map/ppermute | solution.py:335
  17.2 2.2 %collective-permute-done.1.refs_2_ = bf16[256,1024]{1,0:T(8,128)(2,1)S(1)} collective-permute-done((bf16[256,1024]{1,0:T(8,128)(2,1)S(1)}, bf16[256,1024]{1,0:T(8,128)(2,1)S(1)}, u32[]{:S(2)}, u32[]{:S(2)}) %collective-permute-start.1) | collective-permute-done | bytes 524320 | tf_op jit(solution)/shard_map/ppermute | solution.py:336
  19.4 1.6 collective-permute-start.2
  21.4 7.0 %collective-permute-done.4.refs_2_ = bf16[256,1024]{1,0:T(8,128)(2,1)S(1)} collective-permute-done((bf16[256,1024]{1,0:T(8,128)(2,1)S(1)}, bf16[256,1024]{1,0:T(8,128)(2,1)S(1)}, u32[]{:S(2)}, u32[]{:S(2)}) %collective-permute-start.4) | collective-permute-done | bytes 524320 | tf_op jit(solution)/shard_map/ppermute | solution.py:335
  28.4 2.2 %collective-permute-done.5.refs_1_ = bf16[256,1024]{1,0:T(8,128)(2,1)S(1)} collective-permute-done((bf16[256,1024]{1,0:T(8,128)(2,1)S(1)}, bf16[256,1024]{1,0:T(8,128)(2,1)S(1)}, u32[]{:S(2)}, u32[]{:S(2)}) %collective-permute-start.5) | collective-permute-done | bytes 524320 | tf_op jit(solution)/shard_map/ppermute | solution.py:336
  30.6 1.6 collective-permute-start.8
  32.6 3.7 %shard_map.65 = (f32[512,768]{1,0:T(8,128)S(1)}, f32[512,768]{1,0:T(8,128)S(1)}, f32[512,768]{1,0:T(8,128)S(1)}, bf16[1024,768]{1,0:T(8,128)(2,1)S(1)}, bf16[102...) custom-call(s32[8]{0:T(128)S(1)} %stack.44.refs_0_.refs_7_, ...), custom_call_target="tpu_custom_call", output_to_operand_aliasing={{0}: (9, {}), {1}: (10, {}), {2}: (11, {})} | custom-call | bytes 1048576 | tf_op jit(solution)/shard_map/pallas_call | solution.py:57
  36.3 3.3 %collective-permute-done.2.refs_1_ = bf16[256,1024]{1,0:T(8,128)(2,1)S(1)} collective-permute-done((bf16[256,1024]{1,0:T(8,128)(2,1)S(1)}, bf16[256,1024]{1,0:T(8,128)(2,1)S(1)}, u32[]{:S(2)}, u32[]{:S(2)}) %collective-permute-start.2) | collective-permute-done | bytes 524320 | tf_op jit(solution)/shard_map/ppermute | solution.py:335
  39.6 2.2 %collective-permute-done.3.refs_2_ = bf16[256,1024]{1,0:T(8,128)(2,1)S(1)} collective-permute-done((bf16[256,1024]{1,0:T(8,128)(2,1)S(1)}, bf16[256,1024]{1,0:T(8,128)(2,1)S(1)}, u32[]{:S(2)}, u32[]{:S(2)}) %collective-permute-start.3) | collective-permute-done | bytes 524320 | tf_op jit(solution)/shard_map/ppermute | solution.py:336
  41.8 1.6 collective-permute-start.6
  43.9 3.7 %shard_map.66 = (f32[512,768]{1,0:T(8,128)S(1)}, f32[512,768]{1,0:T(8,128)S(1)}, f32[512,768]{1,0:T(8,128)S(1)}, bf16[1024,768]{1,0:T(8,128)(2,1)S(1)}, bf16[102...) custom-call(s32[8]{0:T(128)S(1)} %stack.44.refs_0_.refs_7_, ...), custom_call_target="tpu_custom_call", output_to_operand_aliasing={{0}: (9, {}), {1}: (10, {}), {2}: (11, {})} | custom-call | bytes 1048576 | tf_op jit(solution)/shard_map/pallas_call | solution.py:57
  47.6 3.3 %collective-permute-done.8.refs_2_ = bf16[256,1024]{1,0:T(8,128)(2,1)S(1)} collective-permute-done((bf16[256,1024]{1,0:T(8,128)(2,1)S(1)}, bf16[256,1024]{1,0:T(8,128)(2,1)S(1)}, u32[]{:S(2)}, u32[]{:S(2)}) %collective-permute-start.8) | collective-permute-done | bytes 524320 | tf_op jit(solution)/shard_map/ppermute | solution.py:335
  50.9 2.2 %collective-permute-done.9.refs_1_ = bf16[256,1024]{1,0:T(8,128)(2,1)S(1)} collective-permute-done((bf16[256,1024]{1,0:T(8,128)(2,1)S(1)}, bf16[256,1024]{1,0:T(8,128)(2,1)S(1)}, u32[]{:S(2)}, u32[]{:S(2)}) %collective-permute-start.9) | collective-permute-done | bytes 524320 | tf_op jit(solution)/shard_map/ppermute | solution.py:336
  53.1 1.6 collective-permute-start.12
  55.1 3.7 %shard_map.67 = (f32[512,768]{1,0:T(8,128)S(1)}, f32[512,768]{1,0:T(8,128)S(1)}, f32[512,768]{1,0:T(8,128)S(1)}, bf16[1024,768]{1,0:T(8,128)(2,1)S(1)}, bf16[102...) custom-call(s32[8]{0:T(128)S(1)} %stack.44.refs_0_.refs_7_, ...), custom_call_target="tpu_custom_call", output_to_operand_aliasing={{0}: (9, {}), {1}: (10, {}), {2}: (11, {})} | custom-call | bytes 1048576 | tf_op jit(solution)/shard_map/pallas_call | solution.py:57
  58.8 3.3 %collective-permute-done.6.refs_1_ = bf16[256,1024]{1,0:T(8,128)(2,1)S(1)} collective-permute-done((bf16[256,1024]{1,0:T(8,128)(2,1)S(1)}, bf16[256,1024]{1,0:T(8,128)(2,1)S(1)}, u32[]{:S(2)}, u32[]{:S(2)}) %collective-permute-start.6) | collective-permute-done | bytes 524320 | tf_op jit(solution)/shard_map/ppermute | solution.py:335
  62.1 2.2 %collective-permute-done.7.refs_2_ = bf16[256,1024]{1,0:T(8,128)(2,1)S(1)} collective-permute-done((bf16[256,1024]{1,0:T(8,128)(2,1)S(1)}, bf16[256,1024]{1,0:T(8,128)(2,1)S(1)}, u32[]{:S(2)}, u32[]{:S(2)}) %collective-permute-start.7) | collective-permute-done | bytes 524320 | tf_op jit(solution)/shard_map/ppermute | solution.py:336
  64.3 1.6 collective-permute-start.10
  66.3 3.7 %shard_map.68 = (f32[512,768]{1,0:T(8,128)S(1)}, f32[512,768]{1,0:T(8,128)S(1)}, f32[512,768]{1,0:T(8,128)S(1)}, bf16[1024,768]{1,0:T(8,128)(2,1)S(1)}, bf16[102...) custom-call(s32[8]{0:T(128)S(1)} %stack.44.refs_0_.refs_7_, ...), custom_call_target="tpu_custom_call", output_to_operand_aliasing={{0}: (9, {}), {1}: (10, {}), {2}: (11, {})} | custom-call | bytes 1048576 | tf_op jit(solution)/shard_map/pallas_call | solution.py:57
  70.0 3.3 %collective-permute-done.12.refs_2_ = bf16[256,1024]{1,0:T(8,128)(2,1)S(1)} collective-permute-done((bf16[256,1024]{1,0:T(8,128)(2,1)S(1)}, bf16[256,1024]{1,0:T(8,128)(2,1)S(1)}, u32[]{:S(2)}, u32[]{:S(2)}) %collective-permute-start.12) | collective-permute-done | bytes 524320 | tf_op jit(solution)/shard_map/ppermute | solution.py:335
  73.4 2.2 %collective-permute-done.13.refs_1_ = bf16[256,1024]{1,0:T(8,128)(2,1)S(1)} collective-permute-done((bf16[256,1024]{1,0:T(8,128)(2,1)S(1)}, bf16[256,1024]{1,0:T(8,128)(2,1)S(1)}, u32[]{:S(2)}, u32[]{:S(2)}) %collective-permute-start.13) | collective-permute-done | bytes 524320 | tf_op jit(solution)/shard_map/ppermute | solution.py:336
  75.5 3.7 %shard_map.69 = (f32[512,768]{1,0:T(8,128)S(1)}, f32[512,768]{1,0:T(8,128)S(1)}, f32[512,768]{1,0:T(8,128)S(1)}, bf16[1024,768]{1,0:T(8,128)(2,1)S(1)}, bf16[102...) custom-call(s32[8]{0:T(128)S(1)} %stack.44.refs_0_.refs_7_, ...), custom_call_target="tpu_custom_call", output_to_operand_aliasing={{0}: (11, {}), {1}: (12, {}), {2}: (13, {})} | custom-call | bytes 1048576 | tf_op jit(solution)/shard_map/pallas_call | solution.py:57
  79.3 3.7 %shard_map.70 = (f32[512,768]{1,0:T(8,128)S(1)}, f32[512,768]{1,0:T(8,128)S(1)}, f32[512,768]{1,0:T(8,128)S(1)}) custom-call(s32[8]{0:T(128)S(1)} %stack.44.refs_0_.refs_7_, bf16[256,1024]{1,0:T(8,128)(2,1)S(1)} %collective-permute-done.13.refs_1_, ...), custom_call_target="tpu_custom_call", output_to_operand_aliasing={{0}: (9, {}), {1}: (10, {}), {2}: (11, {})} | custom-call | bytes 1048576 | tf_op jit(solution)/shard_map/pallas_call | solution.py:57
  82.9 0.8 collective-permute-done.10.refs_0_
  83.8 1.5 collective-permute-done.11.refs_1_
  85.3 2.4 %shard_map.71 = (bf16[512,768]{1,0:T(8,128)(2,1)S(1)}, bf16[512,768]{1,0:T(8,128)(2,1)S(1)}, f32[6,128,128]{2,1,0:T(8,128)S(1)}, bf16[6,128,128]{2,1,0:T(8,128)(2,1)S(1)}) custom-call(bf16[256,1024]{1,0:T(8,128)(2,1)S(1)} %collective-permute-done.10.refs_0_, bf16[256,1024]{1,0:T(8,128)(2,1)S(1)} %collective-permute-done.11.refs_1_, ...), custom_call_target="tpu_custom_call" | custom-call | bytes 1048576 | tf_op jit(solution)/shard_map/pallas_call | solution.py:57
  87.7 3.6 %collective-permute-start.14 = (bf16[6,128,128]{2,1,0:T(8,128)(2,1)S(1)}, bf16[6,128,128]{2,1,0:T(8,128)(2,1)S(1)}, u32[]{:S(2)}, u32[]{:S(2)}) collective-permute-start(bf16[6,128,128]{2,1,0:T(8,128)(2,1)S(1)} %get-tuple-element.247), channel_id=1, source_target_pairs={{0,16},{8,24},{1,17},{9,25},{2,18},{10,26},{3,19},{11,27},{4,20},{... | collective-permute-start | bytes 589832 | tf_op jit(solution)/shard_map/ppermute | solution.py:370
  91.4 3.9 %shard_map.72 = (bf16[512,768]{1,0:T(8,128)(2,1)S(1)}, f32[512,768]{1,0:T(8,128)S(1)}) custom-call(bf16[256,1024]{1,0:T(8,128)(2,1)S(1)} %collective-permute-done.10.refs_0_, bf16[256,1024]{1,0:T(8,128)(2,1)S(1)} %collective-permute-done.11.refs_1_, bf16[1024,768]{1,0:T(8,128)(2,1)S(1)} %get-tuple-element.248.refs_2_, ...), custom_call_target="tpu_custom_call" | custom-call | bytes 1048576 | tf_op jit(solution)/shard_map/pallas_call | solution.py:57
  95.4 1.4 collective-permute-done.15.refs_1_
  96.9 1.4 shard_map.74
  98.8 1.6 collective-permute-start.22
  100.4 2.2 %fusion.97 = bf16[256,1024]{1,0:T(8,128)(2,1)S(1)} fusion(bf16[256,768]{1,0:T(8,128)(2,1)S(1)} %get-tuple-element.265, bf16[768,8192]{1,0:T(8,128)(2,1)} %refs_6_.1, s32[]{:T(128)} %mul.38), kind=kOutput, calls=%fused_computation.51 | convolution fusion | flops 402915328 | bytes 2490880 | tf_op jit(solution)/shard_map/dot_general | solution.py:45
  102.7 1.6 collective-permute-start.19
  104.2 2.2 %fusion.94 = bf16[256,1024]{1,0:T(8,128)(2,1)S(1)} fusion(bf16[256,768]{1,0:T(8,128)(2,1)S(1)} %get-tuple-element.260, bf16[768,8192]{1,0:T(8,128)(2,1)} %refs_6_.1, s32[]{:T(128)} %mul.32), kind=kOutput, calls=%fused_computation.50 | convolution fusion | flops 402915328 | bytes 2490880 | tf_op jit(solution)/shard_map/dot_general | solution.py:45
  107.0 6.2 %collective-permute-done.26 = bf16[256,1024]{1,0:T(8,128)(2,1)S(1)} collective-permute-done((bf16[256,1024]{1,0:T(8,128)(2,1)S(1)}, bf16[256,1024]{1,0:T(8,128)(2,1)S(1)}, u32[]{:S(2)}, u32[]{:S(2)}) %collective-permute-start.26) | collective-permute-done | bytes 524320 | tf_op jit(solution)/shard_map/ppermute | solution.py:389
  113.2 0.8 fusion.79
  114.5 0.8 fusion.64
  115.3 1.6 collective-permute-start.23
  116.9 7.9 %collective-permute-done.19 = bf16[256,1024]{1,0:T(8,128)(2,1)S(1)} collective-permute-done((bf16[256,1024]{1,0:T(8,128)(2,1)S(1)}, bf16[256,1024]{1,0:T(8,128)(2,1)S(1)}, u32[]{:S(2)}, u32[]{:S(2)}) %collective-permute-start.19) | collective-permute-done | bytes 524320 | tf_op jit(solution)/shard_map/ppermute | solution.py:396
  124.9 0.8 fusion.70
  125.7 1.6 collective-permute-start.20
  127.3 0.8 fusion.85
  128.6 7.0 %collective-permute-done.27 = bf16[256,1024]{1,0:T(8,128)(2,1)S(1)} collective-permute-done((bf16[256,1024]{1,0:T(8,128)(2,1)S(1)}, bf16[256,1024]{1,0:T(8,128)(2,1)S(1)}, u32[]{:S(2)}, u32[]{:S(2)}) %collective-permute-start.27) | collective-permute-done | bytes 524320 | tf_op jit(solution)/shard_map/ppermute | solution.py:396
  135.6 0.8 fusion.82
  136.9 0.8 fusion.67
  137.7 1.8 %collective-permute-start.24 = (bf16[256,1024]{1,0:T(8,128)(2,1)S(1)}, bf16[256,1024]{1,0:T(8,128)(2,1)S(1)}, u32[]{:S(2)}, u32[]{:S(2)}) collective-permute-start(bf16[256,1024]{1,0:T(8,128)(2,1)S(1)} %fusion.67), channel_id=1, source_target_pairs={{0,2},{2,4},{4,6},{6,7},{7,5},{5,3},{3,1},{1,0},{8,10},{10,12},{12... | collective-permute-start | bytes 1572872 | tf_op jit(solution)/shard_map/ppermute | solution.py:396
  139.6 7.8 %collective-permute-done.20 = bf16[256,1024]{1,0:T(8,128)(2,1)S(1)} collective-permute-done((bf16[256,1024]{1,0:T(8,128)(2,1)S(1)}, bf16[256,1024]{1,0:T(8,128)(2,1)S(1)}, u32[]{:S(2)}, u32[]{:S(2)}) %collective-permute-start.20) | collective-permute-done | bytes 524320 | tf_op jit(solution)/shard_map/ppermute | solution.py:396
  147.3 0.8 fusion.76
  148.2 1.6 collective-permute-start.21
  149.8 0.8 fusion.91
  150.6 0.5 collective-permute-start.18
  151.1 7.0 %collective-permute-done.28 = bf16[256,1024]{1,0:T(8,128)(2,1)S(1)} collective-permute-done((bf16[256,1024]{1,0:T(8,128)(2,1)S(1)}, bf16[256,1024]{1,0:T(8,128)(2,1)S(1)}, u32[]{:S(2)}, u32[]{:S(2)}) %collective-permute-start.28) | collective-permute-done | bytes 524320 | tf_op jit(solution)/shard_map/ppermute | solution.py:396
  158.1 0.8 fusion.88
  159.4 0.8 fusion.73
  160.2 1.6 collective-permute-start.25
  161.8 8.0 %collective-permute-done.21 = bf16[256,1024]{1,0:T(8,128)(2,1)S(1)} collective-permute-done((bf16[256,1024]{1,0:T(8,128)(2,1)S(1)}, bf16[256,1024]{1,0:T(8,128)(2,1)S(1)}, u32[]{:S(2)}, u32[]{:S(2)}) %collective-permute-start.21) | collective-permute-done | bytes 524320 | tf_op jit(solution)/shard_map/ppermute | solution.py:396
  169.8 0.8 fusion.31.bottom_sum
  170.6 0.8 fusion.28.top_sum
  171.4 8.3 %collective-permute-done.29.bottom = bf16[256,1024]{1,0:T(8,128)(2,1)S(1)} collective-permute-done((bf16[256,1024]{1,0:T(8,128)(2,1)S(1)}, bf16[256,1024]{1,0:T(8,128)(2,1)S(1)}, u32[]{:S(2)}, u32[]{:S(2)}) %collective-permute-start.29) | collective-permute-done | bytes 524320 | tf_op jit(solution)/shard_map/ppermute | solution.py:396
  179.9 1.1 shard_map.75
  (35 shorter events, 5.7 us)
Async XLA Ops:
  0.0 6.5 %copy-start = (bf16[512,1024]{1,0:T(8,128)(2,1)S(1)}, bf16[512,1024]{1,0:T(8,128)(2,1)}, u32[]{:S(2)}) copy-start(bf16[512,1024]{1,0:T(8,128)(2,1)} %refs_1_) | copy-start | bytes 3145732
  1.4 15.7 %collective-permute-start = (bf16[256,1024]{1,0:T(8,128)(2,1)S(1)}, bf16[256,1024]{1,0:T(8,128)(2,1)S(1)}, u32[]{:S(2)}, u32[]{:S(2)}) collective-permute-start(bf16[256,1024]{1,0:T(8,128)(2,1)S(1)} %get-tuple-element.272), channel_id=1, source_target_pairs={{0,2},{2,4},{4,6},{6,7},{7,5},{5,3},{3,1},{1,0},{8,10},{10,12},{12... | collective-permute-start | bytes 1572872 | tf_op jit(solution)/shard_map/ppermute | solution.py:335
  4.5 14.8 %collective-permute-start.1 = (bf16[256,1024]{1,0:T(8,128)(2,1)S(1)}, bf16[256,1024]{1,0:T(8,128)(2,1)S(1)}, u32[]{:S(2)}, u32[]{:S(2)}) collective-permute-start(bf16[256,1024]{1,0:T(8,128)(2,1)S(1)} %get-tuple-element.271), channel_id=1, source_target_pairs={{2,0},{4,2},{6,4},{7,6},{5,7},{3,5},{1,3},{0,1},{10,8},{12,10},{14... | collective-permute-start | bytes 1572872 | tf_op jit(solution)/shard_map/ppermute | solution.py:336
  4.5 23.9 %collective-permute-start.4 = (bf16[256,1024]{1,0:T(8,128)(2,1)S(1)}, bf16[256,1024]{1,0:T(8,128)(2,1)S(1)}, u32[]{:S(2)}, u32[]{:S(2)}) collective-permute-start(bf16[256,1024]{1,0:T(8,128)(2,1)S(1)} %get-tuple-element.271), channel_id=1, source_target_pairs={{0,2},{2,4},{4,6},{6,7},{7,5},{5,3},{3,1},{1,0},{8,10},{10,12},{12... | collective-permute-start | bytes 1572872 | tf_op jit(solution)/shard_map/ppermute | solution.py:335
  6.5 24.1 %collective-permute-start.5 = (bf16[256,1024]{1,0:T(8,128)(2,1)S(1)}, bf16[256,1024]{1,0:T(8,128)(2,1)S(1)}, u32[]{:S(2)}, u32[]{:S(2)}) collective-permute-start(bf16[256,1024]{1,0:T(8,128)(2,1)S(1)} %get-tuple-element.272), channel_id=1, source_target_pairs={{2,0},{4,2},{6,4},{7,6},{5,7},{3,5},{1,3},{0,1},{10,8},{12,10},{14... | collective-permute-start | bytes 1572872 | tf_op jit(solution)/shard_map/ppermute | solution.py:336
  19.4 20.3 %collective-permute-start.2 = (bf16[256,1024]{1,0:T(8,128)(2,1)S(1)}, bf16[256,1024]{1,0:T(8,128)(2,1)S(1)}, u32[]{:S(2)}, u32[]{:S(2)}) collective-permute-start(bf16[256,1024]{1,0:T(8,128)(2,1)S(1)} %collective-permute-done.refs_1_), channel_id=1, source_target_pairs={{0,2},{2,4},{4,6},{6,7},{7,5},{5,3},{3,1},{1,0},{8,10},{10,12},{12... | collective-permute-start | bytes 1572872 | tf_op jit(solution)/shard_map/ppermute | solution.py:335
  20.9 20.9 %collective-permute-start.3 = (bf16[256,1024]{1,0:T(8,128)(2,1)S(1)}, bf16[256,1024]{1,0:T(8,128)(2,1)S(1)}, u32[]{:S(2)}, u32[]{:S(2)}) collective-permute-start(bf16[256,1024]{1,0:T(8,128)(2,1)S(1)} %collective-permute-done.1.refs_2_), channel_id=1, source_target_pairs={{2,0},{4,2},{6,4},{7,6},{5,7},{3,5},{1,3},{0,1},{10,8},{12,10},{14... | collective-permute-start | bytes 1572872 | tf_op jit(solution)/shard_map/ppermute | solution.py:336
  30.6 20.3 %collective-permute-start.8 = (bf16[256,1024]{1,0:T(8,128)(2,1)S(1)}, bf16[256,1024]{1,0:T(8,128)(2,1)S(1)}, u32[]{:S(2)}, u32[]{:S(2)}) collective-permute-start(bf16[256,1024]{1,0:T(8,128)(2,1)S(1)} %collective-permute-done.4.refs_2_), channel_id=1, source_target_pairs={{0,2},{2,4},{4,6},{6,7},{7,5},{5,3},{3,1},{1,0},{8,10},{10,12},{12... | collective-permute-start | bytes 1572872 | tf_op jit(solution)/shard_map/ppermute | solution.py:335
  32.2 20.9 %collective-permute-start.9 = (bf16[256,1024]{1,0:T(8,128)(2,1)S(1)}, bf16[256,1024]{1,0:T(8,128)(2,1)S(1)}, u32[]{:S(2)}, u32[]{:S(2)}) collective-permute-start(bf16[256,1024]{1,0:T(8,128)(2,1)S(1)} %collective-permute-done.5.refs_1_), channel_id=1, source_target_pairs={{2,0},{4,2},{6,4},{7,6},{5,7},{3,5},{1,3},{0,1},{10,8},{12,10},{14... | collective-permute-start | bytes 1572872 | tf_op jit(solution)/shard_map/ppermute | solution.py:336
  41.8 20.3 %collective-permute-start.6 = (bf16[256,1024]{1,0:T(8,128)(2,1)S(1)}, bf16[256,1024]{1,0:T(8,128)(2,1)S(1)}, u32[]{:S(2)}, u32[]{:S(2)}) collective-permute-start(bf16[256,1024]{1,0:T(8,128)(2,1)S(1)} %collective-permute-done.2.refs_1_), channel_id=1, source_target_pairs={{0,2},{2,4},{4,6},{6,7},{7,5},{5,3},{3,1},{1,0},{8,10},{10,12},{12... | collective-permute-start | bytes 1572872 | tf_op jit(solution)/shard_map/ppermute | solution.py:335
  43.4 20.9 %collective-permute-start.7 = (bf16[256,1024]{1,0:T(8,128)(2,1)S(1)}, bf16[256,1024]{1,0:T(8,128)(2,1)S(1)}, u32[]{:S(2)}, u32[]{:S(2)}) collective-permute-start(bf16[256,1024]{1,0:T(8,128)(2,1)S(1)} %collective-permute-done.3.refs_2_), channel_id=1, source_target_pairs={{2,0},{4,2},{6,4},{7,6},{5,7},{3,5},{1,3},{0,1},{10,8},{12,10},{14... | collective-permute-start | bytes 1572872 | tf_op jit(solution)/shard_map/ppermute | solution.py:336
  53.1 20.3 %collective-permute-start.12 = (bf16[256,1024]{1,0:T(8,128)(2,1)S(1)}, bf16[256,1024]{1,0:T(8,128)(2,1)S(1)}, u32[]{:S(2)}, u32[]{:S(2)}) collective-permute-start(bf16[256,1024]{1,0:T(8,128)(2,1)S(1)} %collective-permute-done.8.refs_2_), channel_id=1, source_target_pairs={{0,2},{2,4},{4,6},{6,7},{7,5},{5,3},{3,1},{1,0},{8,10},{10,12},{12... | collective-permute-start | bytes 1572872 | tf_op jit(solution)/shard_map/ppermute | solution.py:335
  54.6 20.9 %collective-permute-start.13 = (bf16[256,1024]{1,0:T(8,128)(2,1)S(1)}, bf16[256,1024]{1,0:T(8,128)(2,1)S(1)}, u32[]{:S(2)}, u32[]{:S(2)}) collective-permute-start(bf16[256,1024]{1,0:T(8,128)(2,1)S(1)} %collective-permute-done.9.refs_1_), channel_id=1, source_target_pairs={{2,0},{4,2},{6,4},{7,6},{5,7},{3,5},{1,3},{0,1},{10,8},{12,10},{14... | collective-permute-start | bytes 1572872 | tf_op jit(solution)/shard_map/ppermute | solution.py:336
  64.3 19.5 %collective-permute-start.10 = (bf16[256,1024]{1,0:T(8,128)(2,1)S(1)}, bf16[256,1024]{1,0:T(8,128)(2,1)S(1)}, u32[]{:S(2)}, u32[]{:S(2)}) collective-permute-start(bf16[256,1024]{1,0:T(8,128)(2,1)S(1)} %collective-permute-done.6.refs_1_), channel_id=1, source_target_pairs={{0,2},{2,4},{4,6},{6,7},{7,5},{5,3},{3,1},{1,0},{8,10},{10,12},{12... | collective-permute-start | bytes 1572872 | tf_op jit(solution)/shard_map/ppermute | solution.py:335
  65.9 19.4 %collective-permute-start.11 = (bf16[256,1024]{1,0:T(8,128)(2,1)S(1)}, bf16[256,1024]{1,0:T(8,128)(2,1)S(1)}, u32[]{:S(2)}, u32[]{:S(2)}) collective-permute-start(bf16[256,1024]{1,0:T(8,128)(2,1)S(1)} %collective-permute-done.7.refs_2_), channel_id=1, source_target_pairs={{2,0},{4,2},{6,4},{7,6},{5,7},{3,5},{1,3},{0,1},{10,8},{12,10},{14... | collective-permute-start | bytes 1572872 | tf_op jit(solution)/shard_map/ppermute | solution.py:336
  85.3 27.8 %slice-start = ((s8[12582912]{0:T(1024)(128)(4,1)}), s8[4194304]{0:T(1024)(128)(4,1)S(1)}, s32[]{:S(2)}) async-start(s8[12582912]{0:T(1024)(128)(4,1)} %bitcast.23), calls=%async_computation | async-start | bytes 8388608
  87.7 7.6 %collective-permute-start.14 = (bf16[6,128,128]{2,1,0:T(8,128)(2,1)S(1)}, bf16[6,128,128]{2,1,0:T(8,128)(2,1)S(1)}, u32[]{:S(2)}, u32[]{:S(2)}) collective-permute-start(bf16[6,128,128]{2,1,0:T(8,128)(2,1)S(1)} %get-tuple-element.247), channel_id=1, source_target_pairs={{0,16},{8,24},{1,17},{9,25},{2,18},{10,26},{3,19},{11,27},{4,20},{... | collective-permute-start | bytes 589832 | tf_op jit(solution)/shard_map/ppermute | solution.py:370
  91.4 5.5 %copy-start.1 = (f32[6,128,128]{2,1,0:T(8,128)S(1)}, f32[6,128,128]{2,1,0:T(8,128)}, u32[]{:S(2)}) copy-start(f32[6,128,128]{2,1,0:T(8,128)} %carry.1) | copy-start | bytes 1179652
  91.4 21.8 %slice-start.1 = ((s8[12582912]{0:T(1024)(128)(4,1)}), s8[4194304]{0:T(1024)(128)(4,1)S(1)}, s32[]{:S(2)}) async-start(s8[12582912]{0:T(1024)(128)(4,1)} %bitcast.23), calls=%async_computation.1 | async-start | bytes 8388608
  95.4 1.5 collective-permute-start.15
  96.9 16.3 %slice-start.2 = ((s8[12582912]{0:T(1024)(128)(4,1)}), s8[4194304]{0:T(1024)(128)(4,1)S(1)}, s32[]{:S(2)}) async-start(s8[12582912]{0:T(1024)(128)(4,1)} %bitcast.23), calls=%async_computation.2 | async-start | bytes 8388608
  98.3 14.8 %collective-permute-start.26 = (bf16[256,1024]{1,0:T(8,128)(2,1)S(1)}, bf16[256,1024]{1,0:T(8,128)(2,1)S(1)}, u32[]{:S(2)}, u32[]{:S(2)}) collective-permute-start(bf16[256,1024]{1,0:T(8,128)(2,1)S(1)} %get-tuple-element.270), channel_id=1, source_target_pairs={{2,0},{4,2},{6,4},{7,6},{5,7},{3,5},{1,3},{0,1},{10,8},{12,10},{14... | collective-permute-start | bytes 1572872 | tf_op jit(solution)/shard_map/ppermute | solution.py:389
  98.8 15.7 %collective-permute-start.22 = (bf16[256,1024]{1,0:T(8,128)(2,1)S(1)}, bf16[256,1024]{1,0:T(8,128)(2,1)S(1)}, u32[]{:S(2)}, u32[]{:S(2)}) collective-permute-start(bf16[256,1024]{1,0:T(8,128)(2,1)S(1)} %get-tuple-element.269), channel_id=1, source_target_pairs={{0,2},{2,4},{4,6},{6,7},{7,5},{5,3},{3,1},{1,0},{8,10},{10,12},{12... | collective-permute-start | bytes 1572872 | tf_op jit(solution)/shard_map/ppermute | solution.py:388
  102.7 22.2 %collective-permute-start.19 = (bf16[256,1024]{1,0:T(8,128)(2,1)S(1)}, bf16[256,1024]{1,0:T(8,128)(2,1)S(1)}, u32[]{:S(2)}, u32[]{:S(2)}) collective-permute-start(bf16[256,1024]{1,0:T(8,128)(2,1)S(1)} %fusion.97), channel_id=1, source_target_pairs={{0,2},{2,4},{4,6},{6,7},{7,5},{5,3},{3,1},{1,0},{8,10},{10,12},{12... | collective-permute-start | bytes 1572872 | tf_op jit(solution)/shard_map/ppermute | solution.py:396
  106.5 20.8 %collective-permute-start.16 = (bf16[256,1024]{1,0:T(8,128)(2,1)S(1)}, bf16[256,1024]{1,0:T(8,128)(2,1)S(1)}, u32[]{:S(2)}, u32[]{:S(2)}) collective-permute-start(bf16[256,1024]{1,0:T(8,128)(2,1)S(1)} %fusion.94), channel_id=1, source_target_pairs={{2,0},{4,2},{6,4},{7,6},{5,7},{3,5},{1,3},{0,1},{10,8},{12,10},{14... | collective-permute-start | bytes 1572872 | tf_op jit(solution)/shard_map/ppermute | solution.py:396
  114.0 21.6 %collective-permute-start.27 = (bf16[256,1024]{1,0:T(8,128)(2,1)S(1)}, bf16[256,1024]{1,0:T(8,128)(2,1)S(1)}, u32[]{:S(2)}, u32[]{:S(2)}) collective-permute-start(bf16[256,1024]{1,0:T(8,128)(2,1)S(1)} %fusion.79), channel_id=1, source_target_pairs={{2,0},{4,2},{6,4},{7,6},{5,7},{3,5},{1,3},{0,1},{10,8},{12,10},{14... | collective-permute-start | bytes 1572872 | tf_op jit(solution)/shard_map/ppermute | solution.py:396
  115.3 21.6 %collective-permute-start.23 = (bf16[256,1024]{1,0:T(8,128)(2,1)S(1)}, bf16[256,1024]{1,0:T(8,128)(2,1)S(1)}, u32[]{:S(2)}, u32[]{:S(2)}) collective-permute-start(bf16[256,1024]{1,0:T(8,128)(2,1)S(1)} %fusion.64), channel_id=1, source_target_pairs={{0,2},{2,4},{4,6},{6,7},{7,5},{5,3},{3,1},{1,0},{8,10},{10,12},{12... | collective-permute-start | bytes 1572872 | tf_op jit(solution)/shard_map/ppermute | solution.py:396
  125.7 21.7 %collective-permute-start.20 = (bf16[256,1024]{1,0:T(8,128)(2,1)S(1)}, bf16[256,1024]{1,0:T(8,128)(2,1)S(1)}, u32[]{:S(2)}, u32[]{:S(2)}) collective-permute-start(bf16[256,1024]{1,0:T(8,128)(2,1)S(1)} %fusion.70), channel_id=1, source_target_pairs={{0,2},{2,4},{4,6},{6,7},{7,5},{5,3},{3,1},{1,0},{8,10},{10,12},{12... | collective-permute-start | bytes 1572872 | tf_op jit(solution)/shard_map/ppermute | solution.py:396
  128.1 21.7 %collective-permute-start.17 = (bf16[256,1024]{1,0:T(8,128)(2,1)S(1)}, bf16[256,1024]{1,0:T(8,128)(2,1)S(1)}, u32[]{:S(2)}, u32[]{:S(2)}) collective-permute-start(bf16[256,1024]{1,0:T(8,128)(2,1)S(1)} %fusion.85), channel_id=1, source_target_pairs={{2,0},{4,2},{6,4},{7,6},{5,7},{3,5},{1,3},{0,1},{10,8},{12,10},{14... | collective-permute-start | bytes 1572872 | tf_op jit(solution)/shard_map/ppermute | solution.py:396
  136.4 21.7 %collective-permute-start.28 = (bf16[256,1024]{1,0:T(8,128)(2,1)S(1)}, bf16[256,1024]{1,0:T(8,128)(2,1)S(1)}, u32[]{:S(2)}, u32[]{:S(2)}) collective-permute-start(bf16[256,1024]{1,0:T(8,128)(2,1)S(1)} %fusion.82), channel_id=1, source_target_pairs={{2,0},{4,2},{6,4},{7,6},{5,7},{3,5},{1,3},{0,1},{10,8},{12,10},{14... | collective-permute-start | bytes 1572872 | tf_op jit(solution)/shard_map/ppermute | solution.py:396
  137.7 21.7 %collective-permute-start.24 = (bf16[256,1024]{1,0:T(8,128)(2,1)S(1)}, bf16[256,1024]{1,0:T(8,128)(2,1)S(1)}, u32[]{:S(2)}, u32[]{:S(2)}) collective-permute-start(bf16[256,1024]{1,0:T(8,128)(2,1)S(1)} %fusion.67), channel_id=1, source_target_pairs={{0,2},{2,4},{4,6},{6,7},{7,5},{5,3},{3,1},{1,0},{8,10},{10,12},{12... | collective-permute-start | bytes 1572872 | tf_op jit(solution)/shard_map/ppermute | solution.py:396
  148.2 21.7 %collective-permute-start.21 = (bf16[256,1024]{1,0:T(8,128)(2,1)S(1)}, bf16[256,1024]{1,0:T(8,128)(2,1)S(1)}, u32[]{:S(2)}, u32[]{:S(2)}) collective-permute-start(bf16[256,1024]{1,0:T(8,128)(2,1)S(1)} %fusion.76), channel_id=1, source_target_pairs={{0,2},{2,4},{4,6},{6,7},{7,5},{5,3},{3,1},{1,0},{8,10},{10,12},{12... | collective-permute-start | bytes 1572872 | tf_op jit(solution)/shard_map/ppermute | solution.py:396
  150.6 20.0 %collective-permute-start.18 = (bf16[256,1024]{1,0:T(8,128)(2,1)S(1)}, bf16[256,1024]{1,0:T(8,128)(2,1)S(1)}, u32[]{:S(2)}, u32[]{:S(2)}) collective-permute-start(bf16[256,1024]{1,0:T(8,128)(2,1)S(1)} %fusion.91), channel_id=1, source_target_pairs={{2,0},{4,2},{6,4},{7,6},{5,7},{3,5},{1,3},{0,1},{10,8},{12,10},{14... | collective-permute-start | bytes 1572872 | tf_op jit(solution)/shard_map/ppermute | solution.py:396
  158.9 20.9 %collective-permute-start.29 = (bf16[256,1024]{1,0:T(8,128)(2,1)S(1)}, bf16[256,1024]{1,0:T(8,128)(2,1)S(1)}, u32[]{:S(2)}, u32[]{:S(2)}) collective-permute-start(bf16[256,1024]{1,0:T(8,128)(2,1)S(1)} %fusion.88), channel_id=1, source_target_pairs={{2,0},{4,2},{6,4},{7,6},{5,7},{3,5},{1,3},{0,1},{10,8},{12,10},{14... | collective-permute-start | bytes 1572872 | tf_op jit(solution)/shard_map/ppermute | solution.py:396
  160.2 19.7 %collective-permute-start.25 = (bf16[256,1024]{1,0:T(8,128)(2,1)S(1)}, bf16[256,1024]{1,0:T(8,128)(2,1)S(1)}, u32[]{:S(2)}, u32[]{:S(2)}) collective-permute-start(bf16[256,1024]{1,0:T(8,128)(2,1)S(1)} %fusion.73), channel_id=1, source_target_pairs={{0,2},{2,4},{4,6},{6,7},{7,5},{5,3},{3,1},{1,0},{8,10},{10,12},{12... | collective-permute-start | bytes 1572872 | tf_op jit(solution)/shard_map/ppermute | solution.py:396

commit v4 on v3

--- a/solution.py
+++ b/solution.py
@@ -256,13 +256,16 @@
 
 
 def finish_body(top_sum, bottom_sum, top, bottom, out, staged, moved):
-    half = top.shape[0]
+    half, parts = top.shape[0], moved.shape[1]
+    rows = half // parts
     copies = []
     for i, (total, last) in enumerate(((top_sum, top), (bottom_sum, bottom))):
-        cut = slice(i * half, (i + 1) * half)
-        staged[cut] = (total[...] + last[...].astype(F32)).astype(BF16)
-        copies.append(pltpu.make_async_copy(staged.at[cut, :], out.at[cut, :], moved.at[i]))
-        copies[-1].start()
+        for p in range(parts):
+            mine = slice(p * rows, (p + 1) * rows)
+            cut = slice(i * half + p * rows, i * half + (p + 1) * rows)
+            staged[cut] = (total[mine] + last[mine].astype(F32)).astype(BF16)
+            copies.append(pltpu.make_async_copy(staged.at[cut, :], out.at[cut, :], moved.at[i, p]))
+            copies[-1].start()
     for copy in copies:
         copy.wait()
 
@@ -274,7 +277,7 @@
         in_specs=[pl.BlockSpec(memory_space=pltpu.VMEM)] * 4,
         out_specs=pl.BlockSpec(memory_space=pltpu.HBM),
         out_shape=jax.ShapeDtypeStruct(shape, BF16),
-        scratch_shapes=[pltpu.VMEM(shape, BF16), pltpu.SemaphoreType.DMA((2,))],
+        scratch_shapes=[pltpu.VMEM(shape, BF16), pltpu.SemaphoreType.DMA((2, 4))],
         compiler_params=pltpu.CompilerParams(vmem_limit_bytes=16 << 20),
         cost_estimate=pl.CostEstimate(flops=0, bytes_accessed=1 << 20, transcendentals=0),
     )(*arrays)
@@ -341,7 +344,7 @@
 
     send(1)
     send(2)
-    sums, held = add(0, [tokens], [], None)
+    sums, held = add(0, halves(0), [], None)
     for window in range(2, windows):
         level, second = divmod(window, 2)
         up, down = (level, second), (level, 1 - second)

time: 181 us -> 181 us (level)
  no operation moved by 1% of the time
where the time goes in v4:
time: 181 us
  waiting for transfers between devices  91.9 us (51%)
  Pallas kernels  39.3 us (22%)
  starting transfers between devices  33.9 us (19%)
  matrix products  14.1 us (8%)
    ppermute x12, waiting for transfers between devices, local(): held[rows] = lax.ppermute(value.astype(BF16), 'tp', hops)  46.1 us
    pallas_call x11, Pallas kernels, kernel(): pl.pallas_call(body, in_specs=[pl.BlockSpec(memory_space=space) for _, sp...  38.2 us
    ppermute x7, waiting for transfers between devices, send(): ahead[level + 1, second] = lax.ppermute(ahead[up], 'tp', forward)  23.5 us
    ppermute x7, waiting for transfers between devices, send(): behind[level + 1, 1 - second] = lax.ppermute(behind[down], 'tp', backward)  14.6 us
    dot_general x14, matrix products, dot(): return jnp.dot(a, b, preferred_element_type=F32)  14.1 us
    ppermute x7, starting transfers between devices, send(): ahead[level + 1, second] = lax.ppermute(ahead[up], 'tp', forward)  13 us
    ppermute x12, starting transfers between devices, local(): held[rows] = lax.ppermute(value.astype(BF16), 'tp', hops)  12.9 us
    ppermute x1, waiting for transfers between devices, local(): down = [None, lax.ppermute(bottom, 'tp', backward)]  6.17 us
  transfers between devices with their start and end apart: 30, of which 23 were waited for; matrix products, arithmetic and copies ran while one was open for 8% of the time, Pallas kernels for 19%

profile of v4, /device:TPU:0, one launch (start us, length us, event | category | flops | bytes accessed | tf_op | source)
XLA Modules:
  0.0 181.1 jit_solution(9313918890954855458)
XLA Ops:
  0.1 1.3 fusion.114
  1.4 3.1 %collective-permute-start = (bf16[256,1024]{1,0:T(8,128)(2,1)S(1)}, bf16[256,1024]{1,0:T(8,128)(2,1)S(1)}, u32[]{:S(2)}, u32[]{:S(2)}) collective-permute-start(bf16[256,1024]{1,0:T(8,128)(2,1)S(1)} %get-tuple-element.272.refs_1_), channel_id=1, source_target_pairs={{0,2},{2,4},{4,6},{6,7},{7,5},{5,3},{3,1},{1,0},{8,10},{10,12},{12... | collective-permute-start | bytes 1572872 | tf_op jit(solution)/shard_map/ppermute | solution.py:338
  4.4 2.0 %collective-permute-start.4 = (bf16[256,1024]{1,0:T(8,128)(2,1)S(1)}, bf16[256,1024]{1,0:T(8,128)(2,1)S(1)}, u32[]{:S(2)}, u32[]{:S(2)}) collective-permute-start(bf16[256,1024]{1,0:T(8,128)(2,1)S(1)} %get-tuple-element.271.refs_2_), channel_id=1, source_target_pairs={{0,2},{2,4},{4,6},{6,7},{7,5},{5,3},{3,1},{1,0},{8,10},{10,12},{12... | collective-permute-start | bytes 1572872 | tf_op jit(solution)/shard_map/ppermute | solution.py:338
  6.5 8.2 %shard_map.64 = (f32[512,768]{1,0:T(8,128)S(1)}, f32[512,768]{1,0:T(8,128)S(1)}, f32[512,768]{1,0:T(8,128)S(1)}, bf16[1024,768]{1,0:T(8,128)(2,1)S(1)}, bf16[102...) custom-call(s32[8]{0:T(128)S(1)} %stack.44.refs_0_.refs_7_, ...), custom_call_target="tpu_custom_call" | custom-call | bytes 1048576 | tf_op jit(solution)/shard_map/pallas_call | solution.py:57
  14.7 2.4 %collective-permute-done.refs_1_ = bf16[256,1024]{1,0:T(8,128)(2,1)S(1)} collective-permute-done((bf16[256,1024]{1,0:T(8,128)(2,1)S(1)}, bf16[256,1024]{1,0:T(8,128)(2,1)S(1)}, u32[]{:S(2)}, u32[]{:S(2)}) %collective-permute-start) | collective-permute-done | bytes 524320 | tf_op jit(solution)/shard_map/ppermute | solution.py:338
  17.1 2.2 %collective-permute-done.1.refs_2_ = bf16[256,1024]{1,0:T(8,128)(2,1)S(1)} collective-permute-done((bf16[256,1024]{1,0:T(8,128)(2,1)S(1)}, bf16[256,1024]{1,0:T(8,128)(2,1)S(1)}, u32[]{:S(2)}, u32[]{:S(2)}) %collective-permute-start.1) | collective-permute-done | bytes 524320 | tf_op jit(solution)/shard_map/ppermute | solution.py:339
  19.3 1.6 collective-permute-start.2
  21.3 7.0 %collective-permute-done.4.refs_2_ = bf16[256,1024]{1,0:T(8,128)(2,1)S(1)} collective-permute-done((bf16[256,1024]{1,0:T(8,128)(2,1)S(1)}, bf16[256,1024]{1,0:T(8,128)(2,1)S(1)}, u32[]{:S(2)}, u32[]{:S(2)}) %collective-permute-start.4) | collective-permute-done | bytes 524320 | tf_op jit(solution)/shard_map/ppermute | solution.py:338
  28.3 2.2 %collective-permute-done.5.refs_1_ = bf16[256,1024]{1,0:T(8,128)(2,1)S(1)} collective-permute-done((bf16[256,1024]{1,0:T(8,128)(2,1)S(1)}, bf16[256,1024]{1,0:T(8,128)(2,1)S(1)}, u32[]{:S(2)}, u32[]{:S(2)}) %collective-permute-start.5) | collective-permute-done | bytes 524320 | tf_op jit(solution)/shard_map/ppermute | solution.py:339
  30.5 1.6 collective-permute-start.8
  32.5 3.7 %shard_map.65 = (f32[512,768]{1,0:T(8,128)S(1)}, f32[512,768]{1,0:T(8,128)S(1)}, f32[512,768]{1,0:T(8,128)S(1)}, bf16[1024,768]{1,0:T(8,128)(2,1)S(1)}, bf16[102...) custom-call(s32[8]{0:T(128)S(1)} %stack.44.refs_0_.refs_7_, ...), custom_call_target="tpu_custom_call", output_to_operand_aliasing={{0}: (9, {}), {1}: (10, {}), {2}: (11, {})} | custom-call | bytes 1048576 | tf_op jit(solution)/shard_map/pallas_call | solution.py:57
  36.3 3.3 %collective-permute-done.2.refs_1_ = bf16[256,1024]{1,0:T(8,128)(2,1)S(1)} collective-permute-done((bf16[256,1024]{1,0:T(8,128)(2,1)S(1)}, bf16[256,1024]{1,0:T(8,128)(2,1)S(1)}, u32[]{:S(2)}, u32[]{:S(2)}) %collective-permute-start.2) | collective-permute-done | bytes 524320 | tf_op jit(solution)/shard_map/ppermute | solution.py:338
  39.6 2.2 %collective-permute-done.3.refs_2_ = bf16[256,1024]{1,0:T(8,128)(2,1)S(1)} collective-permute-done((bf16[256,1024]{1,0:T(8,128)(2,1)S(1)}, bf16[256,1024]{1,0:T(8,128)(2,1)S(1)}, u32[]{:S(2)}, u32[]{:S(2)}) %collective-permute-start.3) | collective-permute-done | bytes 524320 | tf_op jit(solution)/shard_map/ppermute | solution.py:339
  41.8 1.6 collective-permute-start.6
  43.8 3.7 %shard_map.66 = (f32[512,768]{1,0:T(8,128)S(1)}, f32[512,768]{1,0:T(8,128)S(1)}, f32[512,768]{1,0:T(8,128)S(1)}, bf16[1024,768]{1,0:T(8,128)(2,1)S(1)}, bf16[102...) custom-call(s32[8]{0:T(128)S(1)} %stack.44.refs_0_.refs_7_, ...), custom_call_target="tpu_custom_call", output_to_operand_aliasing={{0}: (9, {}), {1}: (10, {}), {2}: (11, {})} | custom-call | bytes 1048576 | tf_op jit(solution)/shard_map/pallas_call | solution.py:57
  47.5 3.3 %collective-permute-done.8.refs_2_ = bf16[256,1024]{1,0:T(8,128)(2,1)S(1)} collective-permute-done((bf16[256,1024]{1,0:T(8,128)(2,1)S(1)}, bf16[256,1024]{1,0:T(8,128)(2,1)S(1)}, u32[]{:S(2)}, u32[]{:S(2)}) %collective-permute-start.8) | collective-permute-done | bytes 524320 | tf_op jit(solution)/shard_map/ppermute | solution.py:338
  50.8 2.2 %collective-permute-done.9.refs_1_ = bf16[256,1024]{1,0:T(8,128)(2,1)S(1)} collective-permute-done((bf16[256,1024]{1,0:T(8,128)(2,1)S(1)}, bf16[256,1024]{1,0:T(8,128)(2,1)S(1)}, u32[]{:S(2)}, u32[]{:S(2)}) %collective-permute-start.9) | collective-permute-done | bytes 524320 | tf_op jit(solution)/shard_map/ppermute | solution.py:339
  53.0 1.6 collective-permute-start.12
  55.0 3.7 %shard_map.67 = (f32[512,768]{1,0:T(8,128)S(1)}, f32[512,768]{1,0:T(8,128)S(1)}, f32[512,768]{1,0:T(8,128)S(1)}, bf16[1024,768]{1,0:T(8,128)(2,1)S(1)}, bf16[102...) custom-call(s32[8]{0:T(128)S(1)} %stack.44.refs_0_.refs_7_, ...), custom_call_target="tpu_custom_call", output_to_operand_aliasing={{0}: (9, {}), {1}: (10, {}), {2}: (11, {})} | custom-call | bytes 1048576 | tf_op jit(solution)/shard_map/pallas_call | solution.py:57
  58.7 3.3 %collective-permute-done.6.refs_1_ = bf16[256,1024]{1,0:T(8,128)(2,1)S(1)} collective-permute-done((bf16[256,1024]{1,0:T(8,128)(2,1)S(1)}, bf16[256,1024]{1,0:T(8,128)(2,1)S(1)}, u32[]{:S(2)}, u32[]{:S(2)}) %collective-permute-start.6) | collective-permute-done | bytes 524320 | tf_op jit(solution)/shard_map/ppermute | solution.py:338
  62.0 2.2 %collective-permute-done.7.refs_2_ = bf16[256,1024]{1,0:T(8,128)(2,1)S(1)} collective-permute-done((bf16[256,1024]{1,0:T(8,128)(2,1)S(1)}, bf16[256,1024]{1,0:T(8,128)(2,1)S(1)}, u32[]{:S(2)}, u32[]{:S(2)}) %collective-permute-start.7) | collective-permute-done | bytes 524320 | tf_op jit(solution)/shard_map/ppermute | solution.py:339
  64.2 1.6 collective-permute-start.10
  66.3 3.7 %shard_map.68 = (f32[512,768]{1,0:T(8,128)S(1)}, f32[512,768]{1,0:T(8,128)S(1)}, f32[512,768]{1,0:T(8,128)S(1)}, bf16[1024,768]{1,0:T(8,128)(2,1)S(1)}, bf16[102...) custom-call(s32[8]{0:T(128)S(1)} %stack.44.refs_0_.refs_7_, ...), custom_call_target="tpu_custom_call", output_to_operand_aliasing={{0}: (9, {}), {1}: (10, {}), {2}: (11, {})} | custom-call | bytes 1048576 | tf_op jit(solution)/shard_map/pallas_call | solution.py:57
  70.0 3.3 %collective-permute-done.12.refs_2_ = bf16[256,1024]{1,0:T(8,128)(2,1)S(1)} collective-permute-done((bf16[256,1024]{1,0:T(8,128)(2,1)S(1)}, bf16[256,1024]{1,0:T(8,128)(2,1)S(1)}, u32[]{:S(2)}, u32[]{:S(2)}) %collective-permute-start.12) | collective-permute-done | bytes 524320 | tf_op jit(solution)/shard_map/ppermute | solution.py:338
  73.3 2.2 %collective-permute-done.13.refs_1_ = bf16[256,1024]{1,0:T(8,128)(2,1)S(1)} collective-permute-done((bf16[256,1024]{1,0:T(8,128)(2,1)S(1)}, bf16[256,1024]{1,0:T(8,128)(2,1)S(1)}, u32[]{:S(2)}, u32[]{:S(2)}) %collective-permute-start.13) | collective-permute-done | bytes 524320 | tf_op jit(solution)/shard_map/ppermute | solution.py:339
  75.5 3.7 %shard_map.69 = (f32[512,768]{1,0:T(8,128)S(1)}, f32[512,768]{1,0:T(8,128)S(1)}, f32[512,768]{1,0:T(8,128)S(1)}, bf16[1024,768]{1,0:T(8,128)(2,1)S(1)}, bf16[102...) custom-call(s32[8]{0:T(128)S(1)} %stack.44.refs_0_.refs_7_, ...), custom_call_target="tpu_custom_call", output_to_operand_aliasing={{0}: (11, {}), {1}: (12, {}), {2}: (13, {})} | custom-call | bytes 1048576 | tf_op jit(solution)/shard_map/pallas_call | solution.py:57
  79.2 3.7 %shard_map.70 = (f32[512,768]{1,0:T(8,128)S(1)}, f32[512,768]{1,0:T(8,128)S(1)}, f32[512,768]{1,0:T(8,128)S(1)}) custom-call(s32[8]{0:T(128)S(1)} %stack.44.refs_0_.refs_7_, bf16[256,1024]{1,0:T(8,128)(2,1)S(1)} %collective-permute-done.13.refs_1_, ...), custom_call_target="tpu_custom_call", output_to_operand_aliasing={{0}: (9, {}), {1}: (10, {}), {2}: (11, {})} | custom-call | bytes 1048576 | tf_op jit(solution)/shard_map/pallas_call | solution.py:57
  82.9 0.8 collective-permute-done.10.refs_0_
  83.7 1.5 collective-permute-done.11.refs_1_
  85.2 2.4 %shard_map.71 = (bf16[512,768]{1,0:T(8,128)(2,1)S(1)}, bf16[512,768]{1,0:T(8,128)(2,1)S(1)}, f32[6,128,128]{2,1,0:T(8,128)S(1)}, bf16[6,128,128]{2,1,0:T(8,128)(2,1)S(1)}) custom-call(bf16[256,1024]{1,0:T(8,128)(2,1)S(1)} %collective-permute-done.10.refs_0_, bf16[256,1024]{1,0:T(8,128)(2,1)S(1)} %collective-permute-done.11.refs_1_, ...), custom_call_target="tpu_custom_call" | custom-call | bytes 1048576 | tf_op jit(solution)/shard_map/pallas_call | solution.py:57
  87.7 3.6 %collective-permute-start.14 = (bf16[6,128,128]{2,1,0:T(8,128)(2,1)S(1)}, bf16[6,128,128]{2,1,0:T(8,128)(2,1)S(1)}, u32[]{:S(2)}, u32[]{:S(2)}) collective-permute-start(bf16[6,128,128]{2,1,0:T(8,128)(2,1)S(1)} %get-tuple-element.247), channel_id=1, source_target_pairs={{0,16},{8,24},{1,17},{9,25},{2,18},{10,26},{3,19},{11,27},{4,20},{... | collective-permute-start | bytes 589832 | tf_op jit(solution)/shard_map/ppermute | solution.py:373
  91.3 3.9 %shard_map.72 = (bf16[512,768]{1,0:T(8,128)(2,1)S(1)}, f32[512,768]{1,0:T(8,128)S(1)}) custom-call(bf16[256,1024]{1,0:T(8,128)(2,1)S(1)} %collective-permute-done.10.refs_0_, bf16[256,1024]{1,0:T(8,128)(2,1)S(1)} %collective-permute-done.11.refs_1_, bf16[1024,768]{1,0:T(8,128)(2,1)S(1)} %get-tuple-element.248.refs_2_, ...), custom_call_target="tpu_custom_call" | custom-call | bytes 1048576 | tf_op jit(solution)/shard_map/pallas_call | solution.py:57
  95.4 1.4 collective-permute-done.15.refs_1_
  96.8 1.4 shard_map.74
  98.8 1.6 collective-permute-start.22
  100.3 2.2 %fusion.97 = bf16[256,1024]{1,0:T(8,128)(2,1)S(1)} fusion(bf16[256,768]{1,0:T(8,128)(2,1)S(1)} %get-tuple-element.265, bf16[768,8192]{1,0:T(8,128)(2,1)} %refs_6_.1, s32[]{:T(128)} %mul.38), kind=kOutput, calls=%fused_computation.51 | convolution fusion | flops 402915328 | bytes 2490880 | tf_op jit(solution)/shard_map/dot_general | solution.py:45
  102.6 1.6 collective-permute-start.19
  104.1 2.2 %fusion.94 = bf16[256,1024]{1,0:T(8,128)(2,1)S(1)} fusion(bf16[256,768]{1,0:T(8,128)(2,1)S(1)} %get-tuple-element.260, bf16[768,8192]{1,0:T(8,128)(2,1)} %refs_6_.1, s32[]{:T(128)} %mul.32), kind=kOutput, calls=%fused_computation.50 | convolution fusion | flops 402915328 | bytes 2490880 | tf_op jit(solution)/shard_map/dot_general | solution.py:45
  106.9 6.2 %collective-permute-done.26 = bf16[256,1024]{1,0:T(8,128)(2,1)S(1)} collective-permute-done((bf16[256,1024]{1,0:T(8,128)(2,1)S(1)}, bf16[256,1024]{1,0:T(8,128)(2,1)S(1)}, u32[]{:S(2)}, u32[]{:S(2)}) %collective-permute-start.26) | collective-permute-done | bytes 524320 | tf_op jit(solution)/shard_map/ppermute | solution.py:392
  113.1 0.8 fusion.79
  114.4 0.8 fusion.64
  115.2 1.6 collective-permute-start.23
  116.9 7.9 %collective-permute-done.19 = bf16[256,1024]{1,0:T(8,128)(2,1)S(1)} collective-permute-done((bf16[256,1024]{1,0:T(8,128)(2,1)S(1)}, bf16[256,1024]{1,0:T(8,128)(2,1)S(1)}, u32[]{:S(2)}, u32[]{:S(2)}) %collective-permute-start.19) | collective-permute-done | bytes 524320 | tf_op jit(solution)/shard_map/ppermute | solution.py:399
  124.8 0.8 fusion.70
  125.6 1.6 collective-permute-start.20
  127.2 0.8 fusion.85
  128.5 7.0 %collective-permute-done.27 = bf16[256,1024]{1,0:T(8,128)(2,1)S(1)} collective-permute-done((bf16[256,1024]{1,0:T(8,128)(2,1)S(1)}, bf16[256,1024]{1,0:T(8,128)(2,1)S(1)}, u32[]{:S(2)}, u32[]{:S(2)}) %collective-permute-start.27) | collective-permute-done | bytes 524320 | tf_op jit(solution)/shard_map/ppermute | solution.py:399
  135.5 0.8 fusion.82
  136.9 0.8 fusion.67
  137.7 1.8 %collective-permute-start.24 = (bf16[256,1024]{1,0:T(8,128)(2,1)S(1)}, bf16[256,1024]{1,0:T(8,128)(2,1)S(1)}, u32[]{:S(2)}, u32[]{:S(2)}) collective-permute-start(bf16[256,1024]{1,0:T(8,128)(2,1)S(1)} %fusion.67), channel_id=1, source_target_pairs={{0,2},{2,4},{4,6},{6,7},{7,5},{5,3},{3,1},{1,0},{8,10},{10,12},{12... | collective-permute-start | bytes 1572872 | tf_op jit(solution)/shard_map/ppermute | solution.py:399
  139.5 7.8 %collective-permute-done.20 = bf16[256,1024]{1,0:T(8,128)(2,1)S(1)} collective-permute-done((bf16[256,1024]{1,0:T(8,128)(2,1)S(1)}, bf16[256,1024]{1,0:T(8,128)(2,1)S(1)}, u32[]{:S(2)}, u32[]{:S(2)}) %collective-permute-start.20) | collective-permute-done | bytes 524320 | tf_op jit(solution)/shard_map/ppermute | solution.py:399
  147.3 0.8 fusion.76
  148.1 1.6 collective-permute-start.21
  149.7 0.8 fusion.91
  150.5 0.5 collective-permute-start.18
  151.0 7.0 %collective-permute-done.28 = bf16[256,1024]{1,0:T(8,128)(2,1)S(1)} collective-permute-done((bf16[256,1024]{1,0:T(8,128)(2,1)S(1)}, bf16[256,1024]{1,0:T(8,128)(2,1)S(1)}, u32[]{:S(2)}, u32[]{:S(2)}) %collective-permute-start.28) | collective-permute-done | bytes 524320 | tf_op jit(solution)/shard_map/ppermute | solution.py:399
  158.0 0.8 fusion.88
  159.3 0.8 fusion.73
  160.1 1.6 collective-permute-start.25
  161.8 8.0 %collective-permute-done.21 = bf16[256,1024]{1,0:T(8,128)(2,1)S(1)} collective-permute-done((bf16[256,1024]{1,0:T(8,128)(2,1)S(1)}, bf16[256,1024]{1,0:T(8,128)(2,1)S(1)}, u32[]{:S(2)}, u32[]{:S(2)}) %collective-permute-start.21) | collective-permute-done | bytes 524320 | tf_op jit(solution)/shard_map/ppermute | solution.py:399
  169.7 0.8 fusion.31.bottom_sum
  170.5 0.8 fusion.28.top_sum
  171.3 8.3 %collective-permute-done.29.bottom = bf16[256,1024]{1,0:T(8,128)(2,1)S(1)} collective-permute-done((bf16[256,1024]{1,0:T(8,128)(2,1)S(1)}, bf16[256,1024]{1,0:T(8,128)(2,1)S(1)}, u32[]{:S(2)}, u32[]{:S(2)}) %collective-permute-start.29) | collective-permute-done | bytes 524320 | tf_op jit(solution)/shard_map/ppermute | solution.py:399
  179.9 1.0 shard_map.75
  (33 shorter events, 5.7 us)
Async XLA Ops:
  1.4 15.7 %collective-permute-start = (bf16[256,1024]{1,0:T(8,128)(2,1)S(1)}, bf16[256,1024]{1,0:T(8,128)(2,1)S(1)}, u32[]{:S(2)}, u32[]{:S(2)}) collective-permute-start(bf16[256,1024]{1,0:T(8,128)(2,1)S(1)} %get-tuple-element.272.refs_1_), channel_id=1, source_target_pairs={{0,2},{2,4},{4,6},{6,7},{7,5},{5,3},{3,1},{1,0},{8,10},{10,12},{12... | collective-permute-start | bytes 1572872 | tf_op jit(solution)/shard_map/ppermute | solution.py:338
  4.4 14.8 %collective-permute-start.1 = (bf16[256,1024]{1,0:T(8,128)(2,1)S(1)}, bf16[256,1024]{1,0:T(8,128)(2,1)S(1)}, u32[]{:S(2)}, u32[]{:S(2)}) collective-permute-start(bf16[256,1024]{1,0:T(8,128)(2,1)S(1)} %get-tuple-element.271.refs_2_), channel_id=1, source_target_pairs={{2,0},{4,2},{6,4},{7,6},{5,7},{3,5},{1,3},{0,1},{10,8},{12,10},{14... | collective-permute-start | bytes 1572872 | tf_op jit(solution)/shard_map/ppermute | solution.py:339
  4.4 23.9 %collective-permute-start.4 = (bf16[256,1024]{1,0:T(8,128)(2,1)S(1)}, bf16[256,1024]{1,0:T(8,128)(2,1)S(1)}, u32[]{:S(2)}, u32[]{:S(2)}) collective-permute-start(bf16[256,1024]{1,0:T(8,128)(2,1)S(1)} %get-tuple-element.271.refs_2_), channel_id=1, source_target_pairs={{0,2},{2,4},{4,6},{6,7},{7,5},{5,3},{3,1},{1,0},{8,10},{10,12},{12... | collective-permute-start | bytes 1572872 | tf_op jit(solution)/shard_map/ppermute | solution.py:338
  6.5 24.1 %collective-permute-start.5 = (bf16[256,1024]{1,0:T(8,128)(2,1)S(1)}, bf16[256,1024]{1,0:T(8,128)(2,1)S(1)}, u32[]{:S(2)}, u32[]{:S(2)}) collective-permute-start(bf16[256,1024]{1,0:T(8,128)(2,1)S(1)} %get-tuple-element.272.refs_1_), channel_id=1, source_target_pairs={{2,0},{4,2},{6,4},{7,6},{5,7},{3,5},{1,3},{0,1},{10,8},{12,10},{14... | collective-permute-start | bytes 1572872 | tf_op jit(solution)/shard_map/ppermute | solution.py:339
  19.3 20.3 %collective-permute-start.2 = (bf16[256,1024]{1,0:T(8,128)(2,1)S(1)}, bf16[256,1024]{1,0:T(8,128)(2,1)S(1)}, u32[]{:S(2)}, u32[]{:S(2)}) collective-permute-start(bf16[256,1024]{1,0:T(8,128)(2,1)S(1)} %collective-permute-done.refs_1_), channel_id=1, source_target_pairs={{0,2},{2,4},{4,6},{6,7},{7,5},{5,3},{3,1},{1,0},{8,10},{10,12},{12... | collective-permute-start | bytes 1572872 | tf_op jit(solution)/shard_map/ppermute | solution.py:338
  20.9 20.9 %collective-permute-start.3 = (bf16[256,1024]{1,0:T(8,128)(2,1)S(1)}, bf16[256,1024]{1,0:T(8,128)(2,1)S(1)}, u32[]{:S(2)}, u32[]{:S(2)}) collective-permute-start(bf16[256,1024]{1,0:T(8,128)(2,1)S(1)} %collective-permute-done.1.refs_2_), channel_id=1, source_target_pairs={{2,0},{4,2},{6,4},{7,6},{5,7},{3,5},{1,3},{0,1},{10,8},{12,10},{14... | collective-permute-start | bytes 1572872 | tf_op jit(solution)/shard_map/ppermute | solution.py:339
  30.5 20.3 %collective-permute-start.8 = (bf16[256,1024]{1,0:T(8,128)(2,1)S(1)}, bf16[256,1024]{1,0:T(8,128)(2,1)S(1)}, u32[]{:S(2)}, u32[]{:S(2)}) collective-permute-start(bf16[256,1024]{1,0:T(8,128)(2,1)S(1)} %collective-permute-done.4.refs_2_), channel_id=1, source_target_pairs={{0,2},{2,4},{4,6},{6,7},{7,5},{5,3},{3,1},{1,0},{8,10},{10,12},{12... | collective-permute-start | bytes 1572872 | tf_op jit(solution)/shard_map/ppermute | solution.py:338
  32.1 20.9 %collective-permute-start.9 = (bf16[256,1024]{1,0:T(8,128)(2,1)S(1)}, bf16[256,1024]{1,0:T(8,128)(2,1)S(1)}, u32[]{:S(2)}, u32[]{:S(2)}) collective-permute-start(bf16[256,1024]{1,0:T(8,128)(2,1)S(1)} %collective-permute-done.5.refs_1_), channel_id=1, source_target_pairs={{2,0},{4,2},{6,4},{7,6},{5,7},{3,5},{1,3},{0,1},{10,8},{12,10},{14... | collective-permute-start | bytes 1572872 | tf_op jit(solution)/shard_map/ppermute | solution.py:339
  41.8 20.3 %collective-permute-start.6 = (bf16[256,1024]{1,0:T(8,128)(2,1)S(1)}, bf16[256,1024]{1,0:T(8,128)(2,1)S(1)}, u32[]{:S(2)}, u32[]{:S(2)}) collective-permute-start(bf16[256,1024]{1,0:T(8,128)(2,1)S(1)} %collective-permute-done.2.refs_1_), channel_id=1, source_target_pairs={{0,2},{2,4},{4,6},{6,7},{7,5},{5,3},{3,1},{1,0},{8,10},{10,12},{12... | collective-permute-start | bytes 1572872 | tf_op jit(solution)/shard_map/ppermute | solution.py:338
  43.3 20.9 %collective-permute-start.7 = (bf16[256,1024]{1,0:T(8,128)(2,1)S(1)}, bf16[256,1024]{1,0:T(8,128)(2,1)S(1)}, u32[]{:S(2)}, u32[]{:S(2)}) collective-permute-start(bf16[256,1024]{1,0:T(8,128)(2,1)S(1)} %collective-permute-done.3.refs_2_), channel_id=1, source_target_pairs={{2,0},{4,2},{6,4},{7,6},{5,7},{3,5},{1,3},{0,1},{10,8},{12,10},{14... | collective-permute-start | bytes 1572872 | tf_op jit(solution)/shard_map/ppermute | solution.py:339
  53.0 20.3 %collective-permute-start.12 = (bf16[256,1024]{1,0:T(8,128)(2,1)S(1)}, bf16[256,1024]{1,0:T(8,128)(2,1)S(1)}, u32[]{:S(2)}, u32[]{:S(2)}) collective-permute-start(bf16[256,1024]{1,0:T(8,128)(2,1)S(1)} %collective-permute-done.8.refs_2_), channel_id=1, source_target_pairs={{0,2},{2,4},{4,6},{6,7},{7,5},{5,3},{3,1},{1,0},{8,10},{10,12},{12... | collective-permute-start | bytes 1572872 | tf_op jit(solution)/shard_map/ppermute | solution.py:338
  54.6 20.9 %collective-permute-start.13 = (bf16[256,1024]{1,0:T(8,128)(2,1)S(1)}, bf16[256,1024]{1,0:T(8,128)(2,1)S(1)}, u32[]{:S(2)}, u32[]{:S(2)}) collective-permute-start(bf16[256,1024]{1,0:T(8,128)(2,1)S(1)} %collective-permute-done.9.refs_1_), channel_id=1, source_target_pairs={{2,0},{4,2},{6,4},{7,6},{5,7},{3,5},{1,3},{0,1},{10,8},{12,10},{14... | collective-permute-start | bytes 1572872 | tf_op jit(solution)/shard_map/ppermute | solution.py:339
  64.2 19.5 %collective-permute-start.10 = (bf16[256,1024]{1,0:T(8,128)(2,1)S(1)}, bf16[256,1024]{1,0:T(8,128)(2,1)S(1)}, u32[]{:S(2)}, u32[]{:S(2)}) collective-permute-start(bf16[256,1024]{1,0:T(8,128)(2,1)S(1)} %collective-permute-done.6.refs_1_), channel_id=1, source_target_pairs={{0,2},{2,4},{4,6},{6,7},{7,5},{5,3},{3,1},{1,0},{8,10},{10,12},{12... | collective-permute-start | bytes 1572872 | tf_op jit(solution)/shard_map/ppermute | solution.py:338
  65.8 19.4 %collective-permute-start.11 = (bf16[256,1024]{1,0:T(8,128)(2,1)S(1)}, bf16[256,1024]{1,0:T(8,128)(2,1)S(1)}, u32[]{:S(2)}, u32[]{:S(2)}) collective-permute-start(bf16[256,1024]{1,0:T(8,128)(2,1)S(1)} %collective-permute-done.7.refs_2_), channel_id=1, source_target_pairs={{2,0},{4,2},{6,4},{7,6},{5,7},{3,5},{1,3},{0,1},{10,8},{12,10},{14... | collective-permute-start | bytes 1572872 | tf_op jit(solution)/shard_map/ppermute | solution.py:339
  85.2 27.8 %slice-start = ((s8[12582912]{0:T(1024)(128)(4,1)}), s8[4194304]{0:T(1024)(128)(4,1)S(1)}, s32[]{:S(2)}) async-start(s8[12582912]{0:T(1024)(128)(4,1)} %bitcast.23), calls=%async_computation | async-start | bytes 8388608
  87.7 7.6 %collective-permute-start.14 = (bf16[6,128,128]{2,1,0:T(8,128)(2,1)S(1)}, bf16[6,128,128]{2,1,0:T(8,128)(2,1)S(1)}, u32[]{:S(2)}, u32[]{:S(2)}) collective-permute-start(bf16[6,128,128]{2,1,0:T(8,128)(2,1)S(1)} %get-tuple-element.247), channel_id=1, source_target_pairs={{0,16},{8,24},{1,17},{9,25},{2,18},{10,26},{3,19},{11,27},{4,20},{... | collective-permute-start | bytes 589832 | tf_op jit(solution)/shard_map/ppermute | solution.py:373
  91.3 5.5 %copy-start = (f32[6,128,128]{2,1,0:T(8,128)S(1)}, f32[6,128,128]{2,1,0:T(8,128)}, u32[]{:S(2)}) copy-start(f32[6,128,128]{2,1,0:T(8,128)} %carry.1) | copy-start | bytes 1179652
  91.3 21.8 %slice-start.1 = ((s8[12582912]{0:T(1024)(128)(4,1)}), s8[4194304]{0:T(1024)(128)(4,1)S(1)}, s32[]{:S(2)}) async-start(s8[12582912]{0:T(1024)(128)(4,1)} %bitcast.23), calls=%async_computation.1 | async-start | bytes 8388608
  95.3 1.5 collective-permute-start.15
  96.8 16.3 %slice-start.2 = ((s8[12582912]{0:T(1024)(128)(4,1)}), s8[4194304]{0:T(1024)(128)(4,1)S(1)}, s32[]{:S(2)}) async-start(s8[12582912]{0:T(1024)(128)(4,1)} %bitcast.23), calls=%async_computation.2 | async-start | bytes 8388608
  98.2 14.8 %collective-permute-start.26 = (bf16[256,1024]{1,0:T(8,128)(2,1)S(1)}, bf16[256,1024]{1,0:T(8,128)(2,1)S(1)}, u32[]{:S(2)}, u32[]{:S(2)}) collective-permute-start(bf16[256,1024]{1,0:T(8,128)(2,1)S(1)} %get-tuple-element.270), channel_id=1, source_target_pairs={{2,0},{4,2},{6,4},{7,6},{5,7},{3,5},{1,3},{0,1},{10,8},{12,10},{14... | collective-permute-start | bytes 1572872 | tf_op jit(solution)/shard_map/ppermute | solution.py:392
  98.8 15.7 %collective-permute-start.22 = (bf16[256,1024]{1,0:T(8,128)(2,1)S(1)}, bf16[256,1024]{1,0:T(8,128)(2,1)S(1)}, u32[]{:S(2)}, u32[]{:S(2)}) collective-permute-start(bf16[256,1024]{1,0:T(8,128)(2,1)S(1)} %get-tuple-element.269), channel_id=1, source_target_pairs={{0,2},{2,4},{4,6},{6,7},{7,5},{5,3},{3,1},{1,0},{8,10},{10,12},{12... | collective-permute-start | bytes 1572872 | tf_op jit(solution)/shard_map/ppermute | solution.py:391
  102.6 22.2 %collective-permute-start.19 = (bf16[256,1024]{1,0:T(8,128)(2,1)S(1)}, bf16[256,1024]{1,0:T(8,128)(2,1)S(1)}, u32[]{:S(2)}, u32[]{:S(2)}) collective-permute-start(bf16[256,1024]{1,0:T(8,128)(2,1)S(1)} %fusion.97), channel_id=1, source_target_pairs={{0,2},{2,4},{4,6},{6,7},{7,5},{5,3},{3,1},{1,0},{8,10},{10,12},{12... | collective-permute-start | bytes 1572872 | tf_op jit(solution)/shard_map/ppermute | solution.py:399
  106.4 20.8 %collective-permute-start.16 = (bf16[256,1024]{1,0:T(8,128)(2,1)S(1)}, bf16[256,1024]{1,0:T(8,128)(2,1)S(1)}, u32[]{:S(2)}, u32[]{:S(2)}) collective-permute-start(bf16[256,1024]{1,0:T(8,128)(2,1)S(1)} %fusion.94), channel_id=1, source_target_pairs={{2,0},{4,2},{6,4},{7,6},{5,7},{3,5},{1,3},{0,1},{10,8},{12,10},{14... | collective-permute-start | bytes 1572872 | tf_op jit(solution)/shard_map/ppermute | solution.py:399
  113.9 21.6 %collective-permute-start.27 = (bf16[256,1024]{1,0:T(8,128)(2,1)S(1)}, bf16[256,1024]{1,0:T(8,128)(2,1)S(1)}, u32[]{:S(2)}, u32[]{:S(2)}) collective-permute-start(bf16[256,1024]{1,0:T(8,128)(2,1)S(1)} %fusion.79), channel_id=1, source_target_pairs={{2,0},{4,2},{6,4},{7,6},{5,7},{3,5},{1,3},{0,1},{10,8},{12,10},{14... | collective-permute-start | bytes 1572872 | tf_op jit(solution)/shard_map/ppermute | solution.py:399
  115.2 21.6 %collective-permute-start.23 = (bf16[256,1024]{1,0:T(8,128)(2,1)S(1)}, bf16[256,1024]{1,0:T(8,128)(2,1)S(1)}, u32[]{:S(2)}, u32[]{:S(2)}) collective-permute-start(bf16[256,1024]{1,0:T(8,128)(2,1)S(1)} %fusion.64), channel_id=1, source_target_pairs={{0,2},{2,4},{4,6},{6,7},{7,5},{5,3},{3,1},{1,0},{8,10},{10,12},{12... | collective-permute-start | bytes 1572872 | tf_op jit(solution)/shard_map/ppermute | solution.py:399
  125.6 21.7 %collective-permute-start.20 = (bf16[256,1024]{1,0:T(8,128)(2,1)S(1)}, bf16[256,1024]{1,0:T(8,128)(2,1)S(1)}, u32[]{:S(2)}, u32[]{:S(2)}) collective-permute-start(bf16[256,1024]{1,0:T(8,128)(2,1)S(1)} %fusion.70), channel_id=1, source_target_pairs={{0,2},{2,4},{4,6},{6,7},{7,5},{5,3},{3,1},{1,0},{8,10},{10,12},{12... | collective-permute-start | bytes 1572872 | tf_op jit(solution)/shard_map/ppermute | solution.py:399
  128.0 21.7 %collective-permute-start.17 = (bf16[256,1024]{1,0:T(8,128)(2,1)S(1)}, bf16[256,1024]{1,0:T(8,128)(2,1)S(1)}, u32[]{:S(2)}, u32[]{:S(2)}) collective-permute-start(bf16[256,1024]{1,0:T(8,128)(2,1)S(1)} %fusion.85), channel_id=1, source_target_pairs={{2,0},{4,2},{6,4},{7,6},{5,7},{3,5},{1,3},{0,1},{10,8},{12,10},{14... | collective-permute-start | bytes 1572872 | tf_op jit(solution)/shard_map/ppermute | solution.py:399
  136.3 21.7 %collective-permute-start.28 = (bf16[256,1024]{1,0:T(8,128)(2,1)S(1)}, bf16[256,1024]{1,0:T(8,128)(2,1)S(1)}, u32[]{:S(2)}, u32[]{:S(2)}) collective-permute-start(bf16[256,1024]{1,0:T(8,128)(2,1)S(1)} %fusion.82), channel_id=1, source_target_pairs={{2,0},{4,2},{6,4},{7,6},{5,7},{3,5},{1,3},{0,1},{10,8},{12,10},{14... | collective-permute-start | bytes 1572872 | tf_op jit(solution)/shard_map/ppermute | solution.py:399
  137.7 21.7 %collective-permute-start.24 = (bf16[256,1024]{1,0:T(8,128)(2,1)S(1)}, bf16[256,1024]{1,0:T(8,128)(2,1)S(1)}, u32[]{:S(2)}, u32[]{:S(2)}) collective-permute-start(bf16[256,1024]{1,0:T(8,128)(2,1)S(1)} %fusion.67), channel_id=1, source_target_pairs={{0,2},{2,4},{4,6},{6,7},{7,5},{5,3},{3,1},{1,0},{8,10},{10,12},{12... | collective-permute-start | bytes 1572872 | tf_op jit(solution)/shard_map/ppermute | solution.py:399
  148.1 21.7 %collective-permute-start.21 = (bf16[256,1024]{1,0:T(8,128)(2,1)S(1)}, bf16[256,1024]{1,0:T(8,128)(2,1)S(1)}, u32[]{:S(2)}, u32[]{:S(2)}) collective-permute-start(bf16[256,1024]{1,0:T(8,128)(2,1)S(1)} %fusion.76), channel_id=1, source_target_pairs={{0,2},{2,4},{4,6},{6,7},{7,5},{5,3},{3,1},{1,0},{8,10},{10,12},{12... | collective-permute-start | bytes 1572872 | tf_op jit(solution)/shard_map/ppermute | solution.py:399
  150.5 20.0 %collective-permute-start.18 = (bf16[256,1024]{1,0:T(8,128)(2,1)S(1)}, bf16[256,1024]{1,0:T(8,128)(2,1)S(1)}, u32[]{:S(2)}, u32[]{:S(2)}) collective-permute-start(bf16[256,1024]{1,0:T(8,128)(2,1)S(1)} %fusion.91), channel_id=1, source_target_pairs={{2,0},{4,2},{6,4},{7,6},{5,7},{3,5},{1,3},{0,1},{10,8},{12,10},{14... | collective-permute-start | bytes 1572872 | tf_op jit(solution)/shard_map/ppermute | solution.py:399
  158.8 20.9 %collective-permute-start.29 = (bf16[256,1024]{1,0:T(8,128)(2,1)S(1)}, bf16[256,1024]{1,0:T(8,128)(2,1)S(1)}, u32[]{:S(2)}, u32[]{:S(2)}) collective-permute-start(bf16[256,1024]{1,0:T(8,128)(2,1)S(1)} %fusion.88), channel_id=1, source_target_pairs={{2,0},{4,2},{6,4},{7,6},{5,7},{3,5},{1,3},{0,1},{10,8},{12,10},{14... | collective-permute-start | bytes 1572872 | tf_op jit(solution)/shard_map/ppermute | solution.py:399
  160.1 19.7 %collective-permute-start.25 = (bf16[256,1024]{1,0:T(8,128)(2,1)S(1)}, bf16[256,1024]{1,0:T(8,128)(2,1)S(1)}, u32[]{:S(2)}, u32[]{:S(2)}) collective-permute-start(bf16[256,1024]{1,0:T(8,128)(2,1)S(1)} %fusion.73), channel_id=1, source_target_pairs={{0,2},{2,4},{4,6},{6,7},{7,5},{5,3},{3,1},{1,0},{8,10},{10,12},{12... | collective-permute-start | bytes 1572872 | tf_op jit(solution)/shard_map/ppermute | solution.py:399

commit v5 on v4

--- a/solution.py
+++ b/solution.py
@@ -290,7 +290,7 @@
     half = row_count // 2
     count = lax.axis_size("tp")
     reach = count // 2
-    order = ring_order(count)
+    order = ring_order(count)[::-1]
     forward = [(order[i], order[(i + 1) % count]) for i in range(count)]
     backward = [(b, a) for a, b in forward]
     index = lax.axis_index("tp")

time: 181 us -> 181 us (level)
  no operation moved by 1% of the time
where the time goes in v5:
time: 181 us
  waiting for transfers between devices  91.8 us (51%)
  Pallas kernels  39.3 us (22%)
  starting transfers between devices  34 us (19%)
  matrix products  14.2 us (8%)
    ppermute x12, waiting for transfers between devices, local(): held[rows] = lax.ppermute(value.astype(BF16), 'tp', hops)  46.2 us
    pallas_call x11, Pallas kernels, kernel(): pl.pallas_call(body, in_specs=[pl.BlockSpec(memory_space=space) for _, sp...  38.2 us
    ppermute x7, waiting for transfers between devices, send(): ahead[level + 1, second] = lax.ppermute(ahead[up], 'tp', forward)  24.5 us
    dot_general x14, matrix products, dot(): return jnp.dot(a, b, preferred_element_type=F32)  14.2 us
    ppermute x7, waiting for transfers between devices, send(): behind[level + 1, 1 - second] = lax.ppermute(behind[down], 'tp', backward)  13.4 us
    ppermute x12, starting transfers between devices, local(): held[rows] = lax.ppermute(value.astype(BF16), 'tp', hops)  12.9 us
    ppermute x7, starting transfers between devices, send(): ahead[level + 1, second] = lax.ppermute(ahead[up], 'tp', forward)  12.7 us
    ppermute x1, waiting for transfers between devices, local(): down = [None, lax.ppermute(bottom, 'tp', backward)]  6.17 us
  transfers between devices with their start and end apart: 30, of which 23 were waited for; matrix products, arithmetic and copies ran while one was open for 8% of the time, Pallas kernels for 19%

profile of v5, /device:TPU:0, one launch (start us, length us, event | category | flops | bytes accessed | tf_op | source)
XLA Modules:
  0.0 181.1 jit_solution(14028167458201473014)
XLA Ops:
  0.1 1.3 fusion.114
  1.4 3.0 %collective-permute-start = (bf16[256,1024]{1,0:T(8,128)(2,1)S(1)}, bf16[256,1024]{1,0:T(8,128)(2,1)S(1)}, u32[]{:S(2)}, u32[]{:S(2)}) collective-permute-start(bf16[256,1024]{1,0:T(8,128)(2,1)S(1)} %get-tuple-element.272.refs_1_), channel_id=1, source_target_pairs={{1,3},{3,5},{5,7},{7,6},{6,4},{4,2},{2,0},{0,1},{9,11},{11,13},{13... | collective-permute-start | bytes 1572872 | tf_op jit(solution)/shard_map/ppermute | solution.py:338
  4.5 1.9 %collective-permute-start.4 = (bf16[256,1024]{1,0:T(8,128)(2,1)S(1)}, bf16[256,1024]{1,0:T(8,128)(2,1)S(1)}, u32[]{:S(2)}, u32[]{:S(2)}) collective-permute-start(bf16[256,1024]{1,0:T(8,128)(2,1)S(1)} %get-tuple-element.271.refs_2_), channel_id=1, source_target_pairs={{1,3},{3,5},{5,7},{7,6},{6,4},{4,2},{2,0},{0,1},{9,11},{11,13},{13... | collective-permute-start | bytes 1572872 | tf_op jit(solution)/shard_map/ppermute | solution.py:338
  6.5 8.2 %shard_map.64 = (f32[512,768]{1,0:T(8,128)S(1)}, f32[512,768]{1,0:T(8,128)S(1)}, f32[512,768]{1,0:T(8,128)S(1)}, bf16[1024,768]{1,0:T(8,128)(2,1)S(1)}, bf16[102...) custom-call(s32[8]{0:T(128)S(1)} %stack.44.refs_0_.refs_7_, ...), custom_call_target="tpu_custom_call" | custom-call | bytes 1048576 | tf_op jit(solution)/shard_map/pallas_call | solution.py:57
  14.8 2.4 %collective-permute-done.refs_1_ = bf16[256,1024]{1,0:T(8,128)(2,1)S(1)} collective-permute-done((bf16[256,1024]{1,0:T(8,128)(2,1)S(1)}, bf16[256,1024]{1,0:T(8,128)(2,1)S(1)}, u32[]{:S(2)}, u32[]{:S(2)}) %collective-permute-start) | collective-permute-done | bytes 524320 | tf_op jit(solution)/shard_map/ppermute | solution.py:338
  17.2 2.0 %collective-permute-done.1.refs_2_ = bf16[256,1024]{1,0:T(8,128)(2,1)S(1)} collective-permute-done((bf16[256,1024]{1,0:T(8,128)(2,1)S(1)}, bf16[256,1024]{1,0:T(8,128)(2,1)S(1)}, u32[]{:S(2)}, u32[]{:S(2)}) %collective-permute-start.1) | collective-permute-done | bytes 524320 | tf_op jit(solution)/shard_map/ppermute | solution.py:339
  19.2 1.6 collective-permute-start.2
  21.2 7.2 %collective-permute-done.4.refs_2_ = bf16[256,1024]{1,0:T(8,128)(2,1)S(1)} collective-permute-done((bf16[256,1024]{1,0:T(8,128)(2,1)S(1)}, bf16[256,1024]{1,0:T(8,128)(2,1)S(1)}, u32[]{:S(2)}, u32[]{:S(2)}) %collective-permute-start.4) | collective-permute-done | bytes 524320 | tf_op jit(solution)/shard_map/ppermute | solution.py:338
  28.4 2.0 %collective-permute-done.5.refs_1_ = bf16[256,1024]{1,0:T(8,128)(2,1)S(1)} collective-permute-done((bf16[256,1024]{1,0:T(8,128)(2,1)S(1)}, bf16[256,1024]{1,0:T(8,128)(2,1)S(1)}, u32[]{:S(2)}, u32[]{:S(2)}) %collective-permute-start.5) | collective-permute-done | bytes 524320 | tf_op jit(solution)/shard_map/ppermute | solution.py:339
  30.4 1.6 collective-permute-start.8
  32.5 3.7 %shard_map.65 = (f32[512,768]{1,0:T(8,128)S(1)}, f32[512,768]{1,0:T(8,128)S(1)}, f32[512,768]{1,0:T(8,128)S(1)}, bf16[1024,768]{1,0:T(8,128)(2,1)S(1)}, bf16[102...) custom-call(s32[8]{0:T(128)S(1)} %stack.44.refs_0_.refs_7_, ...), custom_call_target="tpu_custom_call", output_to_operand_aliasing={{0}: (9, {}), {1}: (10, {}), {2}: (11, {})} | custom-call | bytes 1048576 | tf_op jit(solution)/shard_map/pallas_call | solution.py:57
  36.2 3.5 %collective-permute-done.2.refs_1_ = bf16[256,1024]{1,0:T(8,128)(2,1)S(1)} collective-permute-done((bf16[256,1024]{1,0:T(8,128)(2,1)S(1)}, bf16[256,1024]{1,0:T(8,128)(2,1)S(1)}, u32[]{:S(2)}, u32[]{:S(2)}) %collective-permute-start.2) | collective-permute-done | bytes 524320 | tf_op jit(solution)/shard_map/ppermute | solution.py:338
  39.7 2.0 %collective-permute-done.3.refs_2_ = bf16[256,1024]{1,0:T(8,128)(2,1)S(1)} collective-permute-done((bf16[256,1024]{1,0:T(8,128)(2,1)S(1)}, bf16[256,1024]{1,0:T(8,128)(2,1)S(1)}, u32[]{:S(2)}, u32[]{:S(2)}) %collective-permute-start.3) | collective-permute-done | bytes 524320 | tf_op jit(solution)/shard_map/ppermute | solution.py:339
  41.7 1.6 collective-permute-start.6
  43.7 3.7 %shard_map.66 = (f32[512,768]{1,0:T(8,128)S(1)}, f32[512,768]{1,0:T(8,128)S(1)}, f32[512,768]{1,0:T(8,128)S(1)}, bf16[1024,768]{1,0:T(8,128)(2,1)S(1)}, bf16[102...) custom-call(s32[8]{0:T(128)S(1)} %stack.44.refs_0_.refs_7_, ...), custom_call_target="tpu_custom_call", output_to_operand_aliasing={{0}: (9, {}), {1}: (10, {}), {2}: (11, {})} | custom-call | bytes 1048576 | tf_op jit(solution)/shard_map/pallas_call | solution.py:57
  47.4 3.5 %collective-permute-done.8.refs_2_ = bf16[256,1024]{1,0:T(8,128)(2,1)S(1)} collective-permute-done((bf16[256,1024]{1,0:T(8,128)(2,1)S(1)}, bf16[256,1024]{1,0:T(8,128)(2,1)S(1)}, u32[]{:S(2)}, u32[]{:S(2)}) %collective-permute-start.8) | collective-permute-done | bytes 524320 | tf_op jit(solution)/shard_map/ppermute | solution.py:338
  50.9 2.0 %collective-permute-done.9.refs_1_ = bf16[256,1024]{1,0:T(8,128)(2,1)S(1)} collective-permute-done((bf16[256,1024]{1,0:T(8,128)(2,1)S(1)}, bf16[256,1024]{1,0:T(8,128)(2,1)S(1)}, u32[]{:S(2)}, u32[]{:S(2)}) %collective-permute-start.9) | collective-permute-done | bytes 524320 | tf_op jit(solution)/shard_map/ppermute | solution.py:339
  52.9 1.6 collective-permute-start.12
  54.9 3.7 %shard_map.67 = (f32[512,768]{1,0:T(8,128)S(1)}, f32[512,768]{1,0:T(8,128)S(1)}, f32[512,768]{1,0:T(8,128)S(1)}, bf16[1024,768]{1,0:T(8,128)(2,1)S(1)}, bf16[102...) custom-call(s32[8]{0:T(128)S(1)} %stack.44.refs_0_.refs_7_, ...), custom_call_target="tpu_custom_call", output_to_operand_aliasing={{0}: (9, {}), {1}: (10, {}), {2}: (11, {})} | custom-call | bytes 1048576 | tf_op jit(solution)/shard_map/pallas_call | solution.py:57
  58.6 3.5 %collective-permute-done.6.refs_1_ = bf16[256,1024]{1,0:T(8,128)(2,1)S(1)} collective-permute-done((bf16[256,1024]{1,0:T(8,128)(2,1)S(1)}, bf16[256,1024]{1,0:T(8,128)(2,1)S(1)}, u32[]{:S(2)}, u32[]{:S(2)}) %collective-permute-start.6) | collective-permute-done | bytes 524320 | tf_op jit(solution)/shard_map/ppermute | solution.py:338
  62.1 2.0 %collective-permute-done.7.refs_2_ = bf16[256,1024]{1,0:T(8,128)(2,1)S(1)} collective-permute-done((bf16[256,1024]{1,0:T(8,128)(2,1)S(1)}, bf16[256,1024]{1,0:T(8,128)(2,1)S(1)}, u32[]{:S(2)}, u32[]{:S(2)}) %collective-permute-start.7) | collective-permute-done | bytes 524320 | tf_op jit(solution)/shard_map/ppermute | solution.py:339
  64.1 1.6 collective-permute-start.10
  66.2 3.7 %shard_map.68 = (f32[512,768]{1,0:T(8,128)S(1)}, f32[512,768]{1,0:T(8,128)S(1)}, f32[512,768]{1,0:T(8,128)S(1)}, bf16[1024,768]{1,0:T(8,128)(2,1)S(1)}, bf16[102...) custom-call(s32[8]{0:T(128)S(1)} %stack.44.refs_0_.refs_7_, ...), custom_call_target="tpu_custom_call", output_to_operand_aliasing={{0}: (9, {}), {1}: (10, {}), {2}: (11, {})} | custom-call | bytes 1048576 | tf_op jit(solution)/shard_map/pallas_call | solution.py:57
  69.9 3.5 %collective-permute-done.12.refs_2_ = bf16[256,1024]{1,0:T(8,128)(2,1)S(1)} collective-permute-done((bf16[256,1024]{1,0:T(8,128)(2,1)S(1)}, bf16[256,1024]{1,0:T(8,128)(2,1)S(1)}, u32[]{:S(2)}, u32[]{:S(2)}) %collective-permute-start.12) | collective-permute-done | bytes 524320 | tf_op jit(solution)/shard_map/ppermute | solution.py:338
  73.4 2.0 %collective-permute-done.13.refs_1_ = bf16[256,1024]{1,0:T(8,128)(2,1)S(1)} collective-permute-done((bf16[256,1024]{1,0:T(8,128)(2,1)S(1)}, bf16[256,1024]{1,0:T(8,128)(2,1)S(1)}, u32[]{:S(2)}, u32[]{:S(2)}) %collective-permute-start.13) | collective-permute-done | bytes 524320 | tf_op jit(solution)/shard_map/ppermute | solution.py:339
  75.4 3.7 %shard_map.69 = (f32[512,768]{1,0:T(8,128)S(1)}, f32[512,768]{1,0:T(8,128)S(1)}, f32[512,768]{1,0:T(8,128)S(1)}, bf16[1024,768]{1,0:T(8,128)(2,1)S(1)}, bf16[102...) custom-call(s32[8]{0:T(128)S(1)} %stack.44.refs_0_.refs_7_, ...), custom_call_target="tpu_custom_call", output_to_operand_aliasing={{0}: (11, {}), {1}: (12, {}), {2}: (13, {})} | custom-call | bytes 1048576 | tf_op jit(solution)/shard_map/pallas_call | solution.py:57
  79.1 3.7 %shard_map.70 = (f32[512,768]{1,0:T(8,128)S(1)}, f32[512,768]{1,0:T(8,128)S(1)}, f32[512,768]{1,0:T(8,128)S(1)}) custom-call(s32[8]{0:T(128)S(1)} %stack.44.refs_0_.refs_7_, bf16[256,1024]{1,0:T(8,128)(2,1)S(1)} %collective-permute-done.13.refs_1_, ...), custom_call_target="tpu_custom_call", output_to_operand_aliasing={{0}: (9, {}), {1}: (10, {}), {2}: (11, {})} | custom-call | bytes 1048576 | tf_op jit(solution)/shard_map/pallas_call | solution.py:57
  82.8 1.0 collective-permute-done.10.refs_0_
  83.8 1.4 collective-permute-done.11.refs_1_
  85.1 2.4 %shard_map.71 = (bf16[512,768]{1,0:T(8,128)(2,1)S(1)}, bf16[512,768]{1,0:T(8,128)(2,1)S(1)}, f32[6,128,128]{2,1,0:T(8,128)S(1)}, bf16[6,128,128]{2,1,0:T(8,128)(2,1)S(1)}) custom-call(bf16[256,1024]{1,0:T(8,128)(2,1)S(1)} %collective-permute-done.10.refs_0_, bf16[256,1024]{1,0:T(8,128)(2,1)S(1)} %collective-permute-done.11.refs_1_, ...), custom_call_target="tpu_custom_call" | custom-call | bytes 1048576 | tf_op jit(solution)/shard_map/pallas_call | solution.py:57
  87.6 3.6 %collective-permute-start.14 = (bf16[6,128,128]{2,1,0:T(8,128)(2,1)S(1)}, bf16[6,128,128]{2,1,0:T(8,128)(2,1)S(1)}, u32[]{:S(2)}, u32[]{:S(2)}) collective-permute-start(bf16[6,128,128]{2,1,0:T(8,128)(2,1)S(1)} %get-tuple-element.247), channel_id=1, source_target_pairs={{0,16},{8,24},{1,17},{9,25},{2,18},{10,26},{3,19},{11,27},{4,20},{... | collective-permute-start | bytes 589832 | tf_op jit(solution)/shard_map/ppermute | solution.py:373
  91.2 3.9 %shard_map.72 = (bf16[512,768]{1,0:T(8,128)(2,1)S(1)}, f32[512,768]{1,0:T(8,128)S(1)}) custom-call(bf16[256,1024]{1,0:T(8,128)(2,1)S(1)} %collective-permute-done.10.refs_0_, bf16[256,1024]{1,0:T(8,128)(2,1)S(1)} %collective-permute-done.11.refs_1_, bf16[1024,768]{1,0:T(8,128)(2,1)S(1)} %get-tuple-element.248.refs_2_, ...), custom_call_target="tpu_custom_call" | custom-call | bytes 1048576 | tf_op jit(solution)/shard_map/pallas_call | solution.py:57
  95.3 1.4 collective-permute-done.15.refs_1_
  96.7 1.4 shard_map.74
  98.7 1.5 collective-permute-start.22
  100.2 2.2 %fusion.97 = bf16[256,1024]{1,0:T(8,128)(2,1)S(1)} fusion(bf16[256,768]{1,0:T(8,128)(2,1)S(1)} %get-tuple-element.265, bf16[768,8192]{1,0:T(8,128)(2,1)} %refs_6_.1, s32[]{:T(128)} %mul.38), kind=kOutput, calls=%fused_computation.51 | convolution fusion | flops 402915328 | bytes 2490880 | tf_op jit(solution)/shard_map/dot_general | solution.py:45
  102.5 1.6 collective-permute-start.19
  104.1 2.2 %fusion.94 = bf16[256,1024]{1,0:T(8,128)(2,1)S(1)} fusion(bf16[256,768]{1,0:T(8,128)(2,1)S(1)} %get-tuple-element.260, bf16[768,8192]{1,0:T(8,128)(2,1)} %refs_6_.1, s32[]{:T(128)} %mul.32), kind=kOutput, calls=%fused_computation.50 | convolution fusion | flops 402915328 | bytes 2490880 | tf_op jit(solution)/shard_map/dot_general | solution.py:45
  106.8 6.2 %collective-permute-done.26 = bf16[256,1024]{1,0:T(8,128)(2,1)S(1)} collective-permute-done((bf16[256,1024]{1,0:T(8,128)(2,1)S(1)}, bf16[256,1024]{1,0:T(8,128)(2,1)S(1)}, u32[]{:S(2)}, u32[]{:S(2)}) %collective-permute-start.26) | collective-permute-done | bytes 524320 | tf_op jit(solution)/shard_map/ppermute | solution.py:392
  113.0 0.8 fusion.79
  114.4 0.8 fusion.64
  115.2 1.5 collective-permute-start.23
  116.8 8.0 %collective-permute-done.19 = bf16[256,1024]{1,0:T(8,128)(2,1)S(1)} collective-permute-done((bf16[256,1024]{1,0:T(8,128)(2,1)S(1)}, bf16[256,1024]{1,0:T(8,128)(2,1)S(1)}, u32[]{:S(2)}, u32[]{:S(2)}) %collective-permute-start.19) | collective-permute-done | bytes 524320 | tf_op jit(solution)/shard_map/ppermute | solution.py:399
  124.8 0.8 fusion.70
  125.6 1.5 collective-permute-start.20
  127.2 0.8 fusion.85
  128.5 6.9 %collective-permute-done.27 = bf16[256,1024]{1,0:T(8,128)(2,1)S(1)} collective-permute-done((bf16[256,1024]{1,0:T(8,128)(2,1)S(1)}, bf16[256,1024]{1,0:T(8,128)(2,1)S(1)}, u32[]{:S(2)}, u32[]{:S(2)}) %collective-permute-start.27) | collective-permute-done | bytes 524320 | tf_op jit(solution)/shard_map/ppermute | solution.py:399
  135.5 0.8 fusion.82
  136.8 0.8 fusion.67
  137.7 1.8 collective-permute-start.24
  139.4 7.8 %collective-permute-done.20 = bf16[256,1024]{1,0:T(8,128)(2,1)S(1)} collective-permute-done((bf16[256,1024]{1,0:T(8,128)(2,1)S(1)}, bf16[256,1024]{1,0:T(8,128)(2,1)S(1)}, u32[]{:S(2)}, u32[]{:S(2)}) %collective-permute-start.20) | collective-permute-done | bytes 524320 | tf_op jit(solution)/shard_map/ppermute | solution.py:399
  147.3 0.8 fusion.76
  148.1 1.5 collective-permute-start.21
  149.6 0.8 fusion.91
  150.4 0.6 collective-permute-start.18
  151.0 6.9 %collective-permute-done.28 = bf16[256,1024]{1,0:T(8,128)(2,1)S(1)} collective-permute-done((bf16[256,1024]{1,0:T(8,128)(2,1)S(1)}, bf16[256,1024]{1,0:T(8,128)(2,1)S(1)}, u32[]{:S(2)}, u32[]{:S(2)}) %collective-permute-start.28) | collective-permute-done | bytes 524320 | tf_op jit(solution)/shard_map/ppermute | solution.py:399
  157.9 0.8 fusion.88
  159.3 0.8 fusion.73
  160.1 1.5 collective-permute-start.25
  161.7 8.1 %collective-permute-done.21 = bf16[256,1024]{1,0:T(8,128)(2,1)S(1)} collective-permute-done((bf16[256,1024]{1,0:T(8,128)(2,1)S(1)}, bf16[256,1024]{1,0:T(8,128)(2,1)S(1)}, u32[]{:S(2)}, u32[]{:S(2)}) %collective-permute-start.21) | collective-permute-done | bytes 524320 | tf_op jit(solution)/shard_map/ppermute | solution.py:399
  169.7 0.8 fusion.31.bottom_sum
  170.5 0.8 fusion.28.top_sum
  171.3 8.2 %collective-permute-done.29.bottom = bf16[256,1024]{1,0:T(8,128)(2,1)S(1)} collective-permute-done((bf16[256,1024]{1,0:T(8,128)(2,1)S(1)}, bf16[256,1024]{1,0:T(8,128)(2,1)S(1)}, u32[]{:S(2)}, u32[]{:S(2)}) %collective-permute-start.29) | collective-permute-done | bytes 524320 | tf_op jit(solution)/shard_map/ppermute | solution.py:399
  179.8 1.0 shard_map.75
  (33 shorter events, 6.5 us)
Async XLA Ops:
  1.4 15.8 %collective-permute-start = (bf16[256,1024]{1,0:T(8,128)(2,1)S(1)}, bf16[256,1024]{1,0:T(8,128)(2,1)S(1)}, u32[]{:S(2)}, u32[]{:S(2)}) collective-permute-start(bf16[256,1024]{1,0:T(8,128)(2,1)S(1)} %get-tuple-element.272.refs_1_), channel_id=1, source_target_pairs={{1,3},{3,5},{5,7},{7,6},{6,4},{4,2},{2,0},{0,1},{9,11},{11,13},{13... | collective-permute-start | bytes 1572872 | tf_op jit(solution)/shard_map/ppermute | solution.py:338
  4.4 14.8 %collective-permute-start.1 = (bf16[256,1024]{1,0:T(8,128)(2,1)S(1)}, bf16[256,1024]{1,0:T(8,128)(2,1)S(1)}, u32[]{:S(2)}, u32[]{:S(2)}) collective-permute-start(bf16[256,1024]{1,0:T(8,128)(2,1)S(1)} %get-tuple-element.271.refs_2_), channel_id=1, source_target_pairs={{3,1},{5,3},{7,5},{6,7},{4,6},{2,4},{0,2},{1,0},{11,9},{13,11},{15... | collective-permute-start | bytes 1572872 | tf_op jit(solution)/shard_map/ppermute | solution.py:339
  4.5 23.9 %collective-permute-start.4 = (bf16[256,1024]{1,0:T(8,128)(2,1)S(1)}, bf16[256,1024]{1,0:T(8,128)(2,1)S(1)}, u32[]{:S(2)}, u32[]{:S(2)}) collective-permute-start(bf16[256,1024]{1,0:T(8,128)(2,1)S(1)} %get-tuple-element.271.refs_2_), channel_id=1, source_target_pairs={{1,3},{3,5},{5,7},{7,6},{6,4},{4,2},{2,0},{0,1},{9,11},{11,13},{13... | collective-permute-start | bytes 1572872 | tf_op jit(solution)/shard_map/ppermute | solution.py:338
  6.4 24.1 %collective-permute-start.5 = (bf16[256,1024]{1,0:T(8,128)(2,1)S(1)}, bf16[256,1024]{1,0:T(8,128)(2,1)S(1)}, u32[]{:S(2)}, u32[]{:S(2)}) collective-permute-start(bf16[256,1024]{1,0:T(8,128)(2,1)S(1)} %get-tuple-element.272.refs_1_), channel_id=1, source_target_pairs={{3,1},{5,3},{7,5},{6,7},{4,6},{2,4},{0,2},{1,0},{11,9},{13,11},{15... | collective-permute-start | bytes 1572872 | tf_op jit(solution)/shard_map/ppermute | solution.py:339
  19.2 20.5 %collective-permute-start.2 = (bf16[256,1024]{1,0:T(8,128)(2,1)S(1)}, bf16[256,1024]{1,0:T(8,128)(2,1)S(1)}, u32[]{:S(2)}, u32[]{:S(2)}) collective-permute-start(bf16[256,1024]{1,0:T(8,128)(2,1)S(1)} %collective-permute-done.refs_1_), channel_id=1, source_target_pairs={{1,3},{3,5},{5,7},{7,6},{6,4},{4,2},{2,0},{0,1},{9,11},{11,13},{13... | collective-permute-start | bytes 1572872 | tf_op jit(solution)/shard_map/ppermute | solution.py:338
  20.8 20.9 %collective-permute-start.3 = (bf16[256,1024]{1,0:T(8,128)(2,1)S(1)}, bf16[256,1024]{1,0:T(8,128)(2,1)S(1)}, u32[]{:S(2)}, u32[]{:S(2)}) collective-permute-start(bf16[256,1024]{1,0:T(8,128)(2,1)S(1)} %collective-permute-done.1.refs_2_), channel_id=1, source_target_pairs={{3,1},{5,3},{7,5},{6,7},{4,6},{2,4},{0,2},{1,0},{11,9},{13,11},{15... | collective-permute-start | bytes 1572872 | tf_op jit(solution)/shard_map/ppermute | solution.py:339
  30.4 20.5 %collective-permute-start.8 = (bf16[256,1024]{1,0:T(8,128)(2,1)S(1)}, bf16[256,1024]{1,0:T(8,128)(2,1)S(1)}, u32[]{:S(2)}, u32[]{:S(2)}) collective-permute-start(bf16[256,1024]{1,0:T(8,128)(2,1)S(1)} %collective-permute-done.4.refs_2_), channel_id=1, source_target_pairs={{1,3},{3,5},{5,7},{7,6},{6,4},{4,2},{2,0},{0,1},{9,11},{11,13},{13... | collective-permute-start | bytes 1572872 | tf_op jit(solution)/shard_map/ppermute | solution.py:338
  32.0 20.9 %collective-permute-start.9 = (bf16[256,1024]{1,0:T(8,128)(2,1)S(1)}, bf16[256,1024]{1,0:T(8,128)(2,1)S(1)}, u32[]{:S(2)}, u32[]{:S(2)}) collective-permute-start(bf16[256,1024]{1,0:T(8,128)(2,1)S(1)} %collective-permute-done.5.refs_1_), channel_id=1, source_target_pairs={{3,1},{5,3},{7,5},{6,7},{4,6},{2,4},{0,2},{1,0},{11,9},{13,11},{15... | collective-permute-start | bytes 1572872 | tf_op jit(solution)/shard_map/ppermute | solution.py:339
  41.7 20.5 %collective-permute-start.6 = (bf16[256,1024]{1,0:T(8,128)(2,1)S(1)}, bf16[256,1024]{1,0:T(8,128)(2,1)S(1)}, u32[]{:S(2)}, u32[]{:S(2)}) collective-permute-start(bf16[256,1024]{1,0:T(8,128)(2,1)S(1)} %collective-permute-done.2.refs_1_), channel_id=1, source_target_pairs={{1,3},{3,5},{5,7},{7,6},{6,4},{4,2},{2,0},{0,1},{9,11},{11,13},{13... | collective-permute-start | bytes 1572872 | tf_op jit(solution)/shard_map/ppermute | solution.py:338
  43.2 20.9 %collective-permute-start.7 = (bf16[256,1024]{1,0:T(8,128)(2,1)S(1)}, bf16[256,1024]{1,0:T(8,128)(2,1)S(1)}, u32[]{:S(2)}, u32[]{:S(2)}) collective-permute-start(bf16[256,1024]{1,0:T(8,128)(2,1)S(1)} %collective-permute-done.3.refs_2_), channel_id=1, source_target_pairs={{3,1},{5,3},{7,5},{6,7},{4,6},{2,4},{0,2},{1,0},{11,9},{13,11},{15... | collective-permute-start | bytes 1572872 | tf_op jit(solution)/shard_map/ppermute | solution.py:339
  52.9 20.5 %collective-permute-start.12 = (bf16[256,1024]{1,0:T(8,128)(2,1)S(1)}, bf16[256,1024]{1,0:T(8,128)(2,1)S(1)}, u32[]{:S(2)}, u32[]{:S(2)}) collective-permute-start(bf16[256,1024]{1,0:T(8,128)(2,1)S(1)} %collective-permute-done.8.refs_2_), channel_id=1, source_target_pairs={{1,3},{3,5},{5,7},{7,6},{6,4},{4,2},{2,0},{0,1},{9,11},{11,13},{13... | collective-permute-start | bytes 1572872 | tf_op jit(solution)/shard_map/ppermute | solution.py:338
  54.5 20.9 %collective-permute-start.13 = (bf16[256,1024]{1,0:T(8,128)(2,1)S(1)}, bf16[256,1024]{1,0:T(8,128)(2,1)S(1)}, u32[]{:S(2)}, u32[]{:S(2)}) collective-permute-start(bf16[256,1024]{1,0:T(8,128)(2,1)S(1)} %collective-permute-done.9.refs_1_), channel_id=1, source_target_pairs={{3,1},{5,3},{7,5},{6,7},{4,6},{2,4},{0,2},{1,0},{11,9},{13,11},{15... | collective-permute-start | bytes 1572872 | tf_op jit(solution)/shard_map/ppermute | solution.py:339
  64.1 19.6 %collective-permute-start.10 = (bf16[256,1024]{1,0:T(8,128)(2,1)S(1)}, bf16[256,1024]{1,0:T(8,128)(2,1)S(1)}, u32[]{:S(2)}, u32[]{:S(2)}) collective-permute-start(bf16[256,1024]{1,0:T(8,128)(2,1)S(1)} %collective-permute-done.6.refs_1_), channel_id=1, source_target_pairs={{1,3},{3,5},{5,7},{7,6},{6,4},{4,2},{2,0},{0,1},{9,11},{11,13},{13... | collective-permute-start | bytes 1572872 | tf_op jit(solution)/shard_map/ppermute | solution.py:338
  65.7 19.4 %collective-permute-start.11 = (bf16[256,1024]{1,0:T(8,128)(2,1)S(1)}, bf16[256,1024]{1,0:T(8,128)(2,1)S(1)}, u32[]{:S(2)}, u32[]{:S(2)}) collective-permute-start(bf16[256,1024]{1,0:T(8,128)(2,1)S(1)} %collective-permute-done.7.refs_2_), channel_id=1, source_target_pairs={{3,1},{5,3},{7,5},{6,7},{4,6},{2,4},{0,2},{1,0},{11,9},{13,11},{15... | collective-permute-start | bytes 1572872 | tf_op jit(solution)/shard_map/ppermute | solution.py:339
  85.1 27.8 %slice-start = ((s8[12582912]{0:T(1024)(128)(4,1)}), s8[4194304]{0:T(1024)(128)(4,1)S(1)}, s32[]{:S(2)}) async-start(s8[12582912]{0:T(1024)(128)(4,1)} %bitcast.23), calls=%async_computation | async-start | bytes 8388608
  87.6 7.6 %collective-permute-start.14 = (bf16[6,128,128]{2,1,0:T(8,128)(2,1)S(1)}, bf16[6,128,128]{2,1,0:T(8,128)(2,1)S(1)}, u32[]{:S(2)}, u32[]{:S(2)}) collective-permute-start(bf16[6,128,128]{2,1,0:T(8,128)(2,1)S(1)} %get-tuple-element.247), channel_id=1, source_target_pairs={{0,16},{8,24},{1,17},{9,25},{2,18},{10,26},{3,19},{11,27},{4,20},{... | collective-permute-start | bytes 589832 | tf_op jit(solution)/shard_map/ppermute | solution.py:373
  91.2 5.5 %copy-start = (f32[6,128,128]{2,1,0:T(8,128)S(1)}, f32[6,128,128]{2,1,0:T(8,128)}, u32[]{:S(2)}) copy-start(f32[6,128,128]{2,1,0:T(8,128)} %carry.1) | copy-start | bytes 1179652
  91.2 21.8 %slice-start.1 = ((s8[12582912]{0:T(1024)(128)(4,1)}), s8[4194304]{0:T(1024)(128)(4,1)S(1)}, s32[]{:S(2)}) async-start(s8[12582912]{0:T(1024)(128)(4,1)} %bitcast.23), calls=%async_computation.1 | async-start | bytes 8388608
  95.2 1.5 collective-permute-start.15
  96.7 16.3 %slice-start.2 = ((s8[12582912]{0:T(1024)(128)(4,1)}), s8[4194304]{0:T(1024)(128)(4,1)S(1)}, s32[]{:S(2)}) async-start(s8[12582912]{0:T(1024)(128)(4,1)} %bitcast.23), calls=%async_computation.2 | async-start | bytes 8388608
  98.2 14.8 %collective-permute-start.26 = (bf16[256,1024]{1,0:T(8,128)(2,1)S(1)}, bf16[256,1024]{1,0:T(8,128)(2,1)S(1)}, u32[]{:S(2)}, u32[]{:S(2)}) collective-permute-start(bf16[256,1024]{1,0:T(8,128)(2,1)S(1)} %get-tuple-element.270), channel_id=1, source_target_pairs={{3,1},{5,3},{7,5},{6,7},{4,6},{2,4},{0,2},{1,0},{11,9},{13,11},{15... | collective-permute-start | bytes 1572872 | tf_op jit(solution)/shard_map/ppermute | solution.py:392
  98.7 15.7 %collective-permute-start.22 = (bf16[256,1024]{1,0:T(8,128)(2,1)S(1)}, bf16[256,1024]{1,0:T(8,128)(2,1)S(1)}, u32[]{:S(2)}, u32[]{:S(2)}) collective-permute-start(bf16[256,1024]{1,0:T(8,128)(2,1)S(1)} %get-tuple-element.269), channel_id=1, source_target_pairs={{1,3},{3,5},{5,7},{7,6},{6,4},{4,2},{2,0},{0,1},{9,11},{11,13},{13... | collective-permute-start | bytes 1572872 | tf_op jit(solution)/shard_map/ppermute | solution.py:391
  102.5 22.3 %collective-permute-start.19 = (bf16[256,1024]{1,0:T(8,128)(2,1)S(1)}, bf16[256,1024]{1,0:T(8,128)(2,1)S(1)}, u32[]{:S(2)}, u32[]{:S(2)}) collective-permute-start(bf16[256,1024]{1,0:T(8,128)(2,1)S(1)} %fusion.97), channel_id=1, source_target_pairs={{1,3},{3,5},{5,7},{7,6},{6,4},{4,2},{2,0},{0,1},{9,11},{11,13},{13... | collective-permute-start | bytes 1572872 | tf_op jit(solution)/shard_map/ppermute | solution.py:399
  106.3 20.8 %collective-permute-start.16 = (bf16[256,1024]{1,0:T(8,128)(2,1)S(1)}, bf16[256,1024]{1,0:T(8,128)(2,1)S(1)}, u32[]{:S(2)}, u32[]{:S(2)}) collective-permute-start(bf16[256,1024]{1,0:T(8,128)(2,1)S(1)} %fusion.94), channel_id=1, source_target_pairs={{3,1},{5,3},{7,5},{6,7},{4,6},{2,4},{0,2},{1,0},{11,9},{13,11},{15... | collective-permute-start | bytes 1572872 | tf_op jit(solution)/shard_map/ppermute | solution.py:399
  113.8 21.6 %collective-permute-start.27 = (bf16[256,1024]{1,0:T(8,128)(2,1)S(1)}, bf16[256,1024]{1,0:T(8,128)(2,1)S(1)}, u32[]{:S(2)}, u32[]{:S(2)}) collective-permute-start(bf16[256,1024]{1,0:T(8,128)(2,1)S(1)} %fusion.79), channel_id=1, source_target_pairs={{3,1},{5,3},{7,5},{6,7},{4,6},{2,4},{0,2},{1,0},{11,9},{13,11},{15... | collective-permute-start | bytes 1572872 | tf_op jit(solution)/shard_map/ppermute | solution.py:399
  115.2 21.6 %collective-permute-start.23 = (bf16[256,1024]{1,0:T(8,128)(2,1)S(1)}, bf16[256,1024]{1,0:T(8,128)(2,1)S(1)}, u32[]{:S(2)}, u32[]{:S(2)}) collective-permute-start(bf16[256,1024]{1,0:T(8,128)(2,1)S(1)} %fusion.64), channel_id=1, source_target_pairs={{1,3},{3,5},{5,7},{7,6},{6,4},{4,2},{2,0},{0,1},{9,11},{11,13},{13... | collective-permute-start | bytes 1572872 | tf_op jit(solution)/shard_map/ppermute | solution.py:399
  125.6 21.7 %collective-permute-start.20 = (bf16[256,1024]{1,0:T(8,128)(2,1)S(1)}, bf16[256,1024]{1,0:T(8,128)(2,1)S(1)}, u32[]{:S(2)}, u32[]{:S(2)}) collective-permute-start(bf16[256,1024]{1,0:T(8,128)(2,1)S(1)} %fusion.70), channel_id=1, source_target_pairs={{1,3},{3,5},{5,7},{7,6},{6,4},{4,2},{2,0},{0,1},{9,11},{11,13},{13... | collective-permute-start | bytes 1572872 | tf_op jit(solution)/shard_map/ppermute | solution.py:399
  128.0 21.7 %collective-permute-start.17 = (bf16[256,1024]{1,0:T(8,128)(2,1)S(1)}, bf16[256,1024]{1,0:T(8,128)(2,1)S(1)}, u32[]{:S(2)}, u32[]{:S(2)}) collective-permute-start(bf16[256,1024]{1,0:T(8,128)(2,1)S(1)} %fusion.85), channel_id=1, source_target_pairs={{3,1},{5,3},{7,5},{6,7},{4,6},{2,4},{0,2},{1,0},{11,9},{13,11},{15... | collective-permute-start | bytes 1572872 | tf_op jit(solution)/shard_map/ppermute | solution.py:399
  136.3 21.7 %collective-permute-start.28 = (bf16[256,1024]{1,0:T(8,128)(2,1)S(1)}, bf16[256,1024]{1,0:T(8,128)(2,1)S(1)}, u32[]{:S(2)}, u32[]{:S(2)}) collective-permute-start(bf16[256,1024]{1,0:T(8,128)(2,1)S(1)} %fusion.82), channel_id=1, source_target_pairs={{3,1},{5,3},{7,5},{6,7},{4,6},{2,4},{0,2},{1,0},{11,9},{13,11},{15... | collective-permute-start | bytes 1572872 | tf_op jit(solution)/shard_map/ppermute | solution.py:399
  137.7 21.7 %collective-permute-start.24 = (bf16[256,1024]{1,0:T(8,128)(2,1)S(1)}, bf16[256,1024]{1,0:T(8,128)(2,1)S(1)}, u32[]{:S(2)}, u32[]{:S(2)}) collective-permute-start(bf16[256,1024]{1,0:T(8,128)(2,1)S(1)} %fusion.67), channel_id=1, source_target_pairs={{1,3},{3,5},{5,7},{7,6},{6,4},{4,2},{2,0},{0,1},{9,11},{11,13},{13... | collective-permute-start | bytes 1572872 | tf_op jit(solution)/shard_map/ppermute | solution.py:399
  148.1 21.7 %collective-permute-start.21 = (bf16[256,1024]{1,0:T(8,128)(2,1)S(1)}, bf16[256,1024]{1,0:T(8,128)(2,1)S(1)}, u32[]{:S(2)}, u32[]{:S(2)}) collective-permute-start(bf16[256,1024]{1,0:T(8,128)(2,1)S(1)} %fusion.76), channel_id=1, source_target_pairs={{1,3},{3,5},{5,7},{7,6},{6,4},{4,2},{2,0},{0,1},{9,11},{11,13},{13... | collective-permute-start | bytes 1572872 | tf_op jit(solution)/shard_map/ppermute | solution.py:399
  150.4 20.1 %collective-permute-start.18 = (bf16[256,1024]{1,0:T(8,128)(2,1)S(1)}, bf16[256,1024]{1,0:T(8,128)(2,1)S(1)}, u32[]{:S(2)}, u32[]{:S(2)}) collective-permute-start(bf16[256,1024]{1,0:T(8,128)(2,1)S(1)} %fusion.91), channel_id=1, source_target_pairs={{3,1},{5,3},{7,5},{6,7},{4,6},{2,4},{0,2},{1,0},{11,9},{13,11},{15... | collective-permute-start | bytes 1572872 | tf_op jit(solution)/shard_map/ppermute | solution.py:399
  158.7 20.9 %collective-permute-start.29 = (bf16[256,1024]{1,0:T(8,128)(2,1)S(1)}, bf16[256,1024]{1,0:T(8,128)(2,1)S(1)}, u32[]{:S(2)}, u32[]{:S(2)}) collective-permute-start(bf16[256,1024]{1,0:T(8,128)(2,1)S(1)} %fusion.88), channel_id=1, source_target_pairs={{3,1},{5,3},{7,5},{6,7},{4,6},{2,4},{0,2},{1,0},{11,9},{13,11},{15... | collective-permute-start | bytes 1572872 | tf_op jit(solution)/shard_map/ppermute | solution.py:399
  160.1 19.7 %collective-permute-start.25 = (bf16[256,1024]{1,0:T(8,128)(2,1)S(1)}, bf16[256,1024]{1,0:T(8,128)(2,1)S(1)}, u32[]{:S(2)}, u32[]{:S(2)}) collective-permute-start(bf16[256,1024]{1,0:T(8,128)(2,1)S(1)} %fusion.73), channel_id=1, source_target_pairs={{1,3},{3,5},{5,7},{7,6},{6,4},{4,2},{2,0},{0,1},{9,11},{11,13},{13... | collective-permute-start | bytes 1572872 | tf_op jit(solution)/shard_map/ppermute | solution.py:399

commit v6 on v5

--- a/solution.py
+++ b/solution.py
@@ -152,36 +152,45 @@
     return out[:3], sets, out[3 + 3 * len(bring) :]
 
 
-def keys_body(pieces, size, block, *refs):
-    xs = refs[:pieces]
-    w_key, w_value, key_sum, value_sum, keys_out, values_out, state_out, sent_out = refs[pieces:]
+def keys_body(part, size, block, has_state, x, *refs):
+    w_key, w_value, key_sum, value_sum, *refs = refs
+    if has_state:
+        state_in, *refs = refs
+        keys_out, values_out, state_out, sent_out = refs
+    else:
+        keys_out, values_out, state_out = refs
+    rows = x.shape[0]
+    mine = slice(part * rows, (part + 1) * rows)
     heads = block // size
-    chunk = jnp.concatenate([x[...] for x in xs], 0)
     for j in range(keys_out.shape[1] // block):
         cut = slice(j * block, (j + 1) * block)
-        keys = (key_sum[:, cut] + dot(chunk, w_key[:, cut])).astype(BF16)
+        keys = (key_sum[mine, cut] + dot(x[...], w_key[:, cut])).astype(BF16)
         keys_out[:, cut] = keys
-        values = (value_sum[:, cut] + dot(chunk, w_value[:, cut])).astype(BF16)
+        values = (value_sum[mine, cut] + dot(x[...], w_value[:, cut])).astype(BF16)
         values_out[:, cut] = values
         states = dot_rows(keys, values)
         for h in range(heads):
             own = slice(h * size, (h + 1) * size)
-            state_out[j * heads + h] = states[own, own]
-            sent_out[j * heads + h] = states[own, own].astype(BF16)
-
-
-def finish_keys(chunk, w_key, w_value, key_sum, value_sum, block, size):
-    rows, width = key_sum.shape
-    arrays = (*chunk, w_key, w_value, key_sum, value_sum)
-    outputs = [((rows, width), BF16)] * 2
-    outputs += [((width // size, size, size), kind) for kind in (F32, BF16)]
-    body = functools.partial(keys_body, len(chunk), size, block)
+            state = states[own, own]
+            if has_state:
+                state = state + state_in[j * heads + h]
+                sent_out[j * heads + h] = state.astype(BF16)
+            state_out[j * heads + h] = state
+
+
+def finish_keys(x, part, w_key, w_value, key_sum, value_sum, state, block, size):
+    rows, width = x.shape[0], w_key.shape[1]
+    arrays = [x, w_key, w_value, key_sum, value_sum] + ([] if state is None else [state])
+    shape = (width // size, size, size)
+    outputs = [((rows, width), BF16)] * 2 + [(shape, F32)]
+    outputs += [] if state is None else [(shape, BF16)]
+    body = functools.partial(keys_body, part, size, block, state is not None)
     return kernel(body, [(array, pltpu.VMEM) for array in arrays], outputs)
 
 
 def within_body(pieces, size, block, *refs):
     xs = refs[:pieces]
-    w_query, query_sum, keys_in, values_in, query_out, within_out = refs[pieces:]
+    w_query, query_sum, *halves, query_out, within_out = refs[pieces:]
     rows, width = query_sum.shape
     chunk = jnp.concatenate([x[...] for x in xs], 0)
     tile = rows // 2
@@ -193,21 +202,23 @@
         cut = slice(j * block, (j + 1) * block)
         query = (query_sum[:, cut] + dot(chunk, w_query[:, cut])).astype(BF16)
         query_out[:, cut] = query
-        keys, values = keys_in[:, cut], values_in[:, cut]
+        (k_top, k_bottom), (v_top, v_bottom) = [
+            [half[:, cut] for half in pair] for pair in (halves[:2], halves[2:])
+        ]
         sums = []
         for h in range(block // size):
             own = slice(h * size, (h + 1) * size)
-            q, k, v = query[:, own], keys[:, own], values[:, own]
-            first = jnp.where(causal, dot_columns(q[:tile], k[:tile]), 0.0).astype(BF16)
-            lower = dot_columns(q[tile:], k[:tile]).astype(BF16)
-            second = jnp.where(causal, dot_columns(q[tile:], k[tile:]), 0.0).astype(BF16)
-            bottom = dot(lower, v[:tile]) + dot(second, v[tile:])
-            sums.append(jnp.concatenate([dot(first, v[:tile]), bottom], 0))
+            q = query[:, own]
+            first = jnp.where(causal, dot_columns(q[:tile], k_top[:, own]), 0.0).astype(BF16)
+            lower = dot_columns(q[tile:], k_top[:, own]).astype(BF16)
+            second = jnp.where(causal, dot_columns(q[tile:], k_bottom[:, own]), 0.0).astype(BF16)
+            bottom = dot(lower, v_top[:, own]) + dot(second, v_bottom[:, own])
+            sums.append(jnp.concatenate([dot(first, v_top[:, own]), bottom], 0))
         within_out[:, cut] = jnp.concatenate(sums, 1)
 
 
 def finish_query(chunk, w_query, query_sum, keys, values, block, size):
-    arrays = (*chunk, w_query, query_sum, keys, values)
+    arrays = (*chunk, w_query, query_sum, *keys, *values)
     outputs = [(query_sum.shape, BF16), (query_sum.shape, F32)]
     body = functools.partial(within_body, len(chunk), size, block)
     return kernel(body, [(array, pltpu.VMEM) for array in arrays], outputs)
@@ -364,9 +375,10 @@
     ahead, behind = ahead[reach, 0], behind[reach, 1]
     last = [ahead, behind]
     w_query_last, w_key_last, w_value_last, w_first = final
-    keys, values, state, sent = finish_keys(
-        last, w_key_last, w_value_last, sums[1], sums[2], block, size
-    )
+    keys, values = [None, None], [None, None]
+    key_arrays = (w_key_last, w_value_last, sums[1], sums[2])
+    keys[0], values[0], state = finish_keys(last[0], 0, *key_arrays, None, block, size)
+    keys[1], values[1], state, sent = finish_keys(last[1], 1, *key_arrays, state, block, size)
 
     members = lax.axis_size("seq")
     others = [

time: 181 us -> 182 us (level)
  matrix products: 14.2 us -> 11.2 us
  waiting for transfers between devices: 91.8 us -> 94.4 us
    dot_general x14, matrix products: 14.2 us -> 11.2 us  [dot(): return jnp.dot(a, b, preferred_element_type=F32)]
    ppermute x1, waiting for transfers between devices: 6.17 us -> 9.03 us  [local(): down = [None, lax.ppermute(bottom, 'tp', backward)]]
    pallas_call x11 -> x12, Pallas kernels: 38.2 us -> 39 us  [kernel(): pl.pallas_call(body, in_specs=[pl.BlockSpec(memory_space=space) for _, sp...]
  transfers between devices with their start and end apart: 30 -> 30, of which waited for: 23 -> 22; matrix products, arithmetic and copies ran while one was open for 8% -> 6% of each run, Pallas kernels for 19% -> 20%
where the time goes in v6:
time: 182 us
  waiting for transfers between devices  94.4 us (52%)
  Pallas kernels  40 us (22%)
  starting transfers between devices  34.2 us (19%)
  matrix products  11.2 us (6%)
    ppermute x12, waiting for transfers between devices, local(): held[rows] = lax.ppermute(value.astype(BF16), 'tp', hops)  47.3 us
    pallas_call x12, Pallas kernels, kernel(): pl.pallas_call(body, in_specs=[pl.BlockSpec(memory_space=space) for _, sp...  39 us
    ppermute x7, waiting for transfers between devices, send(): ahead[level + 1, second] = lax.ppermute(ahead[up], 'tp', forward)  24.5 us
    ppermute x12, starting transfers between devices, local(): held[rows] = lax.ppermute(value.astype(BF16), 'tp', hops)  13 us
    ppermute x7, starting transfers between devices, send(): ahead[level + 1, second] = lax.ppermute(ahead[up], 'tp', forward)  12.7 us
    ppermute x7, waiting for transfers between devices, send(): behind[level + 1, 1 - second] = lax.ppermute(behind[down], 'tp', backward)  12.1 us
    dot_general x14, matrix products, dot(): return jnp.dot(a, b, preferred_element_type=F32)  11.2 us
    ppermute x1, waiting for transfers between devices, local(): down = [None, lax.ppermute(bottom, 'tp', backward)]  9.03 us
  transfers between devices with their start and end apart: 30, of which 22 were waited for; matrix products, arithmetic and copies ran while one was open for 6% of the time, Pallas kernels for 20%

profile of v6, /device:TPU:0, one launch (start us, length us, event | category | flops | bytes accessed | tf_op | source)
XLA Modules:
  0.0 181.7 jit_solution(3735805114305819063)
XLA Ops:
  0.1 1.3 fusion.114
  1.4 3.0 %collective-permute-start = (bf16[256,1024]{1,0:T(8,128)(2,1)S(1)}, bf16[256,1024]{1,0:T(8,128)(2,1)S(1)}, u32[]{:S(2)}, u32[]{:S(2)}) collective-permute-start(bf16[256,1024]{1,0:T(8,128)(2,1)S(1)} %get-tuple-element.278.refs_1_), channel_id=1, source_target_pairs={{1,3},{3,5},{5,7},{7,6},{6,4},{4,2},{2,0},{0,1},{9,11},{11,13},{13... | collective-permute-start | bytes 1572872 | tf_op jit(solution)/shard_map/ppermute | solution.py:349
  4.5 1.9 %collective-permute-start.4 = (bf16[256,1024]{1,0:T(8,128)(2,1)S(1)}, bf16[256,1024]{1,0:T(8,128)(2,1)S(1)}, u32[]{:S(2)}, u32[]{:S(2)}) collective-permute-start(bf16[256,1024]{1,0:T(8,128)(2,1)S(1)} %get-tuple-element.277.refs_2_), channel_id=1, source_target_pairs={{1,3},{3,5},{5,7},{7,6},{6,4},{4,2},{2,0},{0,1},{9,11},{11,13},{13... | collective-permute-start | bytes 1572872 | tf_op jit(solution)/shard_map/ppermute | solution.py:349
  6.5 8.2 %shard_map.64 = (f32[512,768]{1,0:T(8,128)S(1)}, f32[512,768]{1,0:T(8,128)S(1)}, f32[512,768]{1,0:T(8,128)S(1)}, bf16[1024,768]{1,0:T(8,128)(2,1)S(1)}, bf16[102...) custom-call(s32[8]{0:T(128)S(1)} %stack.44.refs_0_.refs_7_, ...), custom_call_target="tpu_custom_call" | custom-call | bytes 1048576 | tf_op jit(solution)/shard_map/pallas_call | solution.py:57
  14.8 2.4 %collective-permute-done.refs_1_ = bf16[256,1024]{1,0:T(8,128)(2,1)S(1)} collective-permute-done((bf16[256,1024]{1,0:T(8,128)(2,1)S(1)}, bf16[256,1024]{1,0:T(8,128)(2,1)S(1)}, u32[]{:S(2)}, u32[]{:S(2)}) %collective-permute-start) | collective-permute-done | bytes 524320 | tf_op jit(solution)/shard_map/ppermute | solution.py:349
  17.2 2.0 %collective-permute-done.1.refs_2_ = bf16[256,1024]{1,0:T(8,128)(2,1)S(1)} collective-permute-done((bf16[256,1024]{1,0:T(8,128)(2,1)S(1)}, bf16[256,1024]{1,0:T(8,128)(2,1)S(1)}, u32[]{:S(2)}, u32[]{:S(2)}) %collective-permute-start.1) | collective-permute-done | bytes 524320 | tf_op jit(solution)/shard_map/ppermute | solution.py:350
  19.2 1.6 collective-permute-start.2
  21.2 7.2 %collective-permute-done.4.refs_2_ = bf16[256,1024]{1,0:T(8,128)(2,1)S(1)} collective-permute-done((bf16[256,1024]{1,0:T(8,128)(2,1)S(1)}, bf16[256,1024]{1,0:T(8,128)(2,1)S(1)}, u32[]{:S(2)}, u32[]{:S(2)}) %collective-permute-start.4) | collective-permute-done | bytes 524320 | tf_op jit(solution)/shard_map/ppermute | solution.py:349
  28.4 2.0 %collective-permute-done.5.refs_1_ = bf16[256,1024]{1,0:T(8,128)(2,1)S(1)} collective-permute-done((bf16[256,1024]{1,0:T(8,128)(2,1)S(1)}, bf16[256,1024]{1,0:T(8,128)(2,1)S(1)}, u32[]{:S(2)}, u32[]{:S(2)}) %collective-permute-start.5) | collective-permute-done | bytes 524320 | tf_op jit(solution)/shard_map/ppermute | solution.py:350
  30.4 1.6 collective-permute-start.8
  32.5 3.7 %shard_map.65 = (f32[512,768]{1,0:T(8,128)S(1)}, f32[512,768]{1,0:T(8,128)S(1)}, f32[512,768]{1,0:T(8,128)S(1)}, bf16[1024,768]{1,0:T(8,128)(2,1)S(1)}, bf16[102...) custom-call(s32[8]{0:T(128)S(1)} %stack.44.refs_0_.refs_7_, ...), custom_call_target="tpu_custom_call", output_to_operand_aliasing={{0}: (9, {}), {1}: (10, {}), {2}: (11, {})} | custom-call | bytes 1048576 | tf_op jit(solution)/shard_map/pallas_call | solution.py:57
  36.2 3.5 %collective-permute-done.2.refs_1_ = bf16[256,1024]{1,0:T(8,128)(2,1)S(1)} collective-permute-done((bf16[256,1024]{1,0:T(8,128)(2,1)S(1)}, bf16[256,1024]{1,0:T(8,128)(2,1)S(1)}, u32[]{:S(2)}, u32[]{:S(2)}) %collective-permute-start.2) | collective-permute-done | bytes 524320 | tf_op jit(solution)/shard_map/ppermute | solution.py:349
  39.7 2.0 %collective-permute-done.3.refs_2_ = bf16[256,1024]{1,0:T(8,128)(2,1)S(1)} collective-permute-done((bf16[256,1024]{1,0:T(8,128)(2,1)S(1)}, bf16[256,1024]{1,0:T(8,128)(2,1)S(1)}, u32[]{:S(2)}, u32[]{:S(2)}) %collective-permute-start.3) | collective-permute-done | bytes 524320 | tf_op jit(solution)/shard_map/ppermute | solution.py:350
  41.7 1.6 collective-permute-start.6
  43.7 3.7 %shard_map.66 = (f32[512,768]{1,0:T(8,128)S(1)}, f32[512,768]{1,0:T(8,128)S(1)}, f32[512,768]{1,0:T(8,128)S(1)}, bf16[1024,768]{1,0:T(8,128)(2,1)S(1)}, bf16[102...) custom-call(s32[8]{0:T(128)S(1)} %stack.44.refs_0_.refs_7_, ...), custom_call_target="tpu_custom_call", output_to_operand_aliasing={{0}: (9, {}), {1}: (10, {}), {2}: (11, {})} | custom-call | bytes 1048576 | tf_op jit(solution)/shard_map/pallas_call | solution.py:57
  47.4 3.5 %collective-permute-done.8.refs_2_ = bf16[256,1024]{1,0:T(8,128)(2,1)S(1)} collective-permute-done((bf16[256,1024]{1,0:T(8,128)(2,1)S(1)}, bf16[256,1024]{1,0:T(8,128)(2,1)S(1)}, u32[]{:S(2)}, u32[]{:S(2)}) %collective-permute-start.8) | collective-permute-done | bytes 524320 | tf_op jit(solution)/shard_map/ppermute | solution.py:349
  50.9 2.0 %collective-permute-done.9.refs_1_ = bf16[256,1024]{1,0:T(8,128)(2,1)S(1)} collective-permute-done((bf16[256,1024]{1,0:T(8,128)(2,1)S(1)}, bf16[256,1024]{1,0:T(8,128)(2,1)S(1)}, u32[]{:S(2)}, u32[]{:S(2)}) %collective-permute-start.9) | collective-permute-done | bytes 524320 | tf_op jit(solution)/shard_map/ppermute | solution.py:350
  52.9 1.6 collective-permute-start.11
  54.9 3.7 %shard_map.67 = (f32[512,768]{1,0:T(8,128)S(1)}, f32[512,768]{1,0:T(8,128)S(1)}, f32[512,768]{1,0:T(8,128)S(1)}, bf16[1024,768]{1,0:T(8,128)(2,1)S(1)}, bf16[102...) custom-call(s32[8]{0:T(128)S(1)} %stack.44.refs_0_.refs_7_, ...), custom_call_target="tpu_custom_call", output_to_operand_aliasing={{0}: (9, {}), {1}: (10, {}), {2}: (11, {})} | custom-call | bytes 1048576 | tf_op jit(solution)/shard_map/pallas_call | solution.py:57
  58.6 3.5 %collective-permute-done.6.refs_1_ = bf16[256,1024]{1,0:T(8,128)(2,1)S(1)} collective-permute-done((bf16[256,1024]{1,0:T(8,128)(2,1)S(1)}, bf16[256,1024]{1,0:T(8,128)(2,1)S(1)}, u32[]{:S(2)}, u32[]{:S(2)}) %collective-permute-start.6) | collective-permute-done | bytes 524320 | tf_op jit(solution)/shard_map/ppermute | solution.py:349
  62.1 2.0 %collective-permute-done.7.refs_2_ = bf16[256,1024]{1,0:T(8,128)(2,1)S(1)} collective-permute-done((bf16[256,1024]{1,0:T(8,128)(2,1)S(1)}, bf16[256,1024]{1,0:T(8,128)(2,1)S(1)}, u32[]{:S(2)}, u32[]{:S(2)}) %collective-permute-start.7) | collective-permute-done | bytes 524320 | tf_op jit(solution)/shard_map/ppermute | solution.py:350
  64.1 1.6 collective-permute-start.13
  66.2 3.7 %shard_map.68 = (f32[512,768]{1,0:T(8,128)S(1)}, f32[512,768]{1,0:T(8,128)S(1)}, f32[512,768]{1,0:T(8,128)S(1)}, bf16[1024,768]{1,0:T(8,128)(2,1)S(1)}, bf16[102...) custom-call(s32[8]{0:T(128)S(1)} %stack.44.refs_0_.refs_7_, ...), custom_call_target="tpu_custom_call", output_to_operand_aliasing={{0}: (9, {}), {1}: (10, {}), {2}: (11, {})} | custom-call | bytes 1048576 | tf_op jit(solution)/shard_map/pallas_call | solution.py:57
  69.9 3.5 %collective-permute-done.11.refs_2_ = bf16[256,1024]{1,0:T(8,128)(2,1)S(1)} collective-permute-done((bf16[256,1024]{1,0:T(8,128)(2,1)S(1)}, bf16[256,1024]{1,0:T(8,128)(2,1)S(1)}, u32[]{:S(2)}, u32[]{:S(2)}) %collective-permute-start.11) | collective-permute-done | bytes 524320 | tf_op jit(solution)/shard_map/ppermute | solution.py:349
  73.4 2.0 %collective-permute-done.12.refs_1_ = bf16[256,1024]{1,0:T(8,128)(2,1)S(1)} collective-permute-done((bf16[256,1024]{1,0:T(8,128)(2,1)S(1)}, bf16[256,1024]{1,0:T(8,128)(2,1)S(1)}, u32[]{:S(2)}, u32[]{:S(2)}) %collective-permute-start.12) | collective-permute-done | bytes 524320 | tf_op jit(solution)/shard_map/ppermute | solution.py:350
  75.4 3.7 %shard_map.69 = (f32[512,768]{1,0:T(8,128)S(1)}, f32[512,768]{1,0:T(8,128)S(1)}, f32[512,768]{1,0:T(8,128)S(1)}, bf16[1024,768]{1,0:T(8,128)(2,1)S(1)}, bf16[102...) custom-call(s32[8]{0:T(128)S(1)} %stack.44.refs_0_.refs_7_, ...), custom_call_target="tpu_custom_call", output_to_operand_aliasing={{0}: (11, {}), {1}: (12, {}), {2}: (13, {})} | custom-call | bytes 1048576 | tf_op jit(solution)/shard_map/pallas_call | solution.py:57
  79.1 3.7 %shard_map.70 = (f32[512,768]{1,0:T(8,128)S(1)}, f32[512,768]{1,0:T(8,128)S(1)}, f32[512,768]{1,0:T(8,128)S(1)}) custom-call(s32[8]{0:T(128)S(1)} %stack.44.refs_0_.refs_7_, bf16[256,1024]{1,0:T(8,128)(2,1)S(1)} %collective-permute-done.12.refs_1_, ...), custom_call_target="tpu_custom_call", output_to_operand_aliasing={{0}: (9, {}), {1}: (10, {}), {2}: (11, {})} | custom-call | bytes 1048576 | tf_op jit(solution)/shard_map/pallas_call | solution.py:57
  82.8 1.0 collective-permute-done.13.x.refs_0_
  83.8 1.6 shard_map.71
  85.4 1.6 shard_map.72
  87.0 3.8 %collective-permute-start.14 = (bf16[6,128,128]{2,1,0:T(8,128)(2,1)S(1)}, bf16[6,128,128]{2,1,0:T(8,128)(2,1)S(1)}, u32[]{:S(2)}, u32[]{:S(2)}) collective-permute-start(bf16[6,128,128]{2,1,0:T(8,128)(2,1)S(1)} %get-tuple-element.251), channel_id=1, source_target_pairs={{0,16},{8,24},{1,17},{9,25},{2,18},{10,26},{3,19},{11,27},{4,20},{... | collective-permute-start | bytes 589832 | tf_op jit(solution)/shard_map/ppermute | solution.py:385
  90.8 3.9 %shard_map.73 = (bf16[512,768]{1,0:T(8,128)(2,1)S(1)}, f32[512,768]{1,0:T(8,128)S(1)}) custom-call(bf16[256,1024]{1,0:T(8,128)(2,1)S(1)} %collective-permute-done.13.x.refs_0_, bf16[256,1024]{1,0:T(8,128)(2,1)S(1)} %collective-permute-done.10.x.refs_1_, bf16[1024,768]{1,0:T(8,128)(2,1)S(1)} %get-tuple-element.252.refs_2_, ...), custom_call_target="tpu_custom_call" | custom-call | bytes 1048576 | tf_op jit(solution)/shard_map/pallas_call | solution.py:57
  94.8 1.4 collective-permute-done.15.refs_1_
  96.3 1.4 shard_map.75
  97.7 1.6 collective-permute-start.26
  99.8 0.8 fusion.97
  100.6 1.5 collective-permute-start.19
  102.1 0.8 fusion.94
  103.5 9.0 %collective-permute-done.26 = bf16[256,1024]{1,0:T(8,128)(2,1)S(1)} collective-permute-done((bf16[256,1024]{1,0:T(8,128)(2,1)S(1)}, bf16[256,1024]{1,0:T(8,128)(2,1)S(1)}, u32[]{:S(2)}, u32[]{:S(2)}) %collective-permute-start.26) | collective-permute-done | bytes 524320 | tf_op jit(solution)/shard_map/ppermute | solution.py:404
  112.5 0.8 fusion.79
  113.3 1.6 collective-permute-start.27
  115.0 0.8 fusion.64
  116.3 9.1 %collective-permute-done.19 = bf16[256,1024]{1,0:T(8,128)(2,1)S(1)} collective-permute-done((bf16[256,1024]{1,0:T(8,128)(2,1)S(1)}, bf16[256,1024]{1,0:T(8,128)(2,1)S(1)}, u32[]{:S(2)}, u32[]{:S(2)}) %collective-permute-start.19) | collective-permute-done | bytes 524320 | tf_op jit(solution)/shard_map/ppermute | solution.py:411
  125.4 0.8 fusion.70
  126.7 0.8 fusion.85
  127.5 1.6 collective-permute-start.17
  129.1 5.9 %collective-permute-done.27 = bf16[256,1024]{1,0:T(8,128)(2,1)S(1)} collective-permute-done((bf16[256,1024]{1,0:T(8,128)(2,1)S(1)}, bf16[256,1024]{1,0:T(8,128)(2,1)S(1)}, u32[]{:S(2)}, u32[]{:S(2)}) %collective-permute-start.27) | collective-permute-done | bytes 524320 | tf_op jit(solution)/shard_map/ppermute | solution.py:411
  135.0 0.8 fusion.82
  135.8 1.6 collective-permute-start.28
  137.4 0.8 fusion.67
  139.0 8.9 %collective-permute-done.20 = bf16[256,1024]{1,0:T(8,128)(2,1)S(1)} collective-permute-done((bf16[256,1024]{1,0:T(8,128)(2,1)S(1)}, bf16[256,1024]{1,0:T(8,128)(2,1)S(1)}, u32[]{:S(2)}, u32[]{:S(2)}) %collective-permute-start.20) | collective-permute-done | bytes 524320 | tf_op jit(solution)/shard_map/ppermute | solution.py:411
  147.9 0.8 fusion.76
  149.2 0.8 fusion.91
  150.0 1.6 collective-permute-start.18
  151.6 5.9 %collective-permute-done.28 = bf16[256,1024]{1,0:T(8,128)(2,1)S(1)} collective-permute-done((bf16[256,1024]{1,0:T(8,128)(2,1)S(1)}, bf16[256,1024]{1,0:T(8,128)(2,1)S(1)}, u32[]{:S(2)}, u32[]{:S(2)}) %collective-permute-start.28) | collective-permute-done | bytes 524320 | tf_op jit(solution)/shard_map/ppermute | solution.py:411
  157.5 0.8 fusion.88
  158.3 1.6 collective-permute-start.29
  159.9 0.8 fusion.73
  161.2 9.1 %collective-permute-done.21 = bf16[256,1024]{1,0:T(8,128)(2,1)S(1)} collective-permute-done((bf16[256,1024]{1,0:T(8,128)(2,1)S(1)}, bf16[256,1024]{1,0:T(8,128)(2,1)S(1)}, u32[]{:S(2)}, u32[]{:S(2)}) %collective-permute-start.21) | collective-permute-done | bytes 524320 | tf_op jit(solution)/shard_map/ppermute | solution.py:411
  170.3 0.8 fusion.31.bottom_sum
  171.1 0.8 fusion.28.top_sum
  171.9 7.2 %collective-permute-done.29.bottom = bf16[256,1024]{1,0:T(8,128)(2,1)S(1)} collective-permute-done((bf16[256,1024]{1,0:T(8,128)(2,1)S(1)}, bf16[256,1024]{1,0:T(8,128)(2,1)S(1)}, u32[]{:S(2)}, u32[]{:S(2)}) %collective-permute-start.29) | collective-permute-done | bytes 524320 | tf_op jit(solution)/shard_map/ppermute | solution.py:411
  179.1 1.3 collective-permute-done.25.top
  180.4 1.0 shard_map.76
  (34 shorter events, 6.5 us)
Async XLA Ops:
  1.4 15.8 %collective-permute-start = (bf16[256,1024]{1,0:T(8,128)(2,1)S(1)}, bf16[256,1024]{1,0:T(8,128)(2,1)S(1)}, u32[]{:S(2)}, u32[]{:S(2)}) collective-permute-start(bf16[256,1024]{1,0:T(8,128)(2,1)S(1)} %get-tuple-element.278.refs_1_), channel_id=1, source_target_pairs={{1,3},{3,5},{5,7},{7,6},{6,4},{4,2},{2,0},{0,1},{9,11},{11,13},{13... | collective-permute-start | bytes 1572872 | tf_op jit(solution)/shard_map/ppermute | solution.py:349
  4.4 14.8 %collective-permute-start.1 = (bf16[256,1024]{1,0:T(8,128)(2,1)S(1)}, bf16[256,1024]{1,0:T(8,128)(2,1)S(1)}, u32[]{:S(2)}, u32[]{:S(2)}) collective-permute-start(bf16[256,1024]{1,0:T(8,128)(2,1)S(1)} %get-tuple-element.277.refs_2_), channel_id=1, source_target_pairs={{3,1},{5,3},{7,5},{6,7},{4,6},{2,4},{0,2},{1,0},{11,9},{13,11},{15... | collective-permute-start | bytes 1572872 | tf_op jit(solution)/shard_map/ppermute | solution.py:350
  4.5 23.9 %collective-permute-start.4 = (bf16[256,1024]{1,0:T(8,128)(2,1)S(1)}, bf16[256,1024]{1,0:T(8,128)(2,1)S(1)}, u32[]{:S(2)}, u32[]{:S(2)}) collective-permute-start(bf16[256,1024]{1,0:T(8,128)(2,1)S(1)} %get-tuple-element.277.refs_2_), channel_id=1, source_target_pairs={{1,3},{3,5},{5,7},{7,6},{6,4},{4,2},{2,0},{0,1},{9,11},{11,13},{13... | collective-permute-start | bytes 1572872 | tf_op jit(solution)/shard_map/ppermute | solution.py:349
  6.4 24.1 %collective-permute-start.5 = (bf16[256,1024]{1,0:T(8,128)(2,1)S(1)}, bf16[256,1024]{1,0:T(8,128)(2,1)S(1)}, u32[]{:S(2)}, u32[]{:S(2)}) collective-permute-start(bf16[256,1024]{1,0:T(8,128)(2,1)S(1)} %get-tuple-element.278.refs_1_), channel_id=1, source_target_pairs={{3,1},{5,3},{7,5},{6,7},{4,6},{2,4},{0,2},{1,0},{11,9},{13,11},{15... | collective-permute-start | bytes 1572872 | tf_op jit(solution)/shard_map/ppermute | solution.py:350
  19.2 20.5 %collective-permute-start.2 = (bf16[256,1024]{1,0:T(8,128)(2,1)S(1)}, bf16[256,1024]{1,0:T(8,128)(2,1)S(1)}, u32[]{:S(2)}, u32[]{:S(2)}) collective-permute-start(bf16[256,1024]{1,0:T(8,128)(2,1)S(1)} %collective-permute-done.refs_1_), channel_id=1, source_target_pairs={{1,3},{3,5},{5,7},{7,6},{6,4},{4,2},{2,0},{0,1},{9,11},{11,13},{13... | collective-permute-start | bytes 1572872 | tf_op jit(solution)/shard_map/ppermute | solution.py:349
  20.8 20.9 %collective-permute-start.3 = (bf16[256,1024]{1,0:T(8,128)(2,1)S(1)}, bf16[256,1024]{1,0:T(8,128)(2,1)S(1)}, u32[]{:S(2)}, u32[]{:S(2)}) collective-permute-start(bf16[256,1024]{1,0:T(8,128)(2,1)S(1)} %collective-permute-done.1.refs_2_), channel_id=1, source_target_pairs={{3,1},{5,3},{7,5},{6,7},{4,6},{2,4},{0,2},{1,0},{11,9},{13,11},{15... | collective-permute-start | bytes 1572872 | tf_op jit(solution)/shard_map/ppermute | solution.py:350
  30.4 20.5 %collective-permute-start.8 = (bf16[256,1024]{1,0:T(8,128)(2,1)S(1)}, bf16[256,1024]{1,0:T(8,128)(2,1)S(1)}, u32[]{:S(2)}, u32[]{:S(2)}) collective-permute-start(bf16[256,1024]{1,0:T(8,128)(2,1)S(1)} %collective-permute-done.4.refs_2_), channel_id=1, source_target_pairs={{1,3},{3,5},{5,7},{7,6},{6,4},{4,2},{2,0},{0,1},{9,11},{11,13},{13... | collective-permute-start | bytes 1572872 | tf_op jit(solution)/shard_map/ppermute | solution.py:349
  32.0 20.9 %collective-permute-start.9 = (bf16[256,1024]{1,0:T(8,128)(2,1)S(1)}, bf16[256,1024]{1,0:T(8,128)(2,1)S(1)}, u32[]{:S(2)}, u32[]{:S(2)}) collective-permute-start(bf16[256,1024]{1,0:T(8,128)(2,1)S(1)} %collective-permute-done.5.refs_1_), channel_id=1, source_target_pairs={{3,1},{5,3},{7,5},{6,7},{4,6},{2,4},{0,2},{1,0},{11,9},{13,11},{15... | collective-permute-start | bytes 1572872 | tf_op jit(solution)/shard_map/ppermute | solution.py:350
  41.7 20.5 %collective-permute-start.6 = (bf16[256,1024]{1,0:T(8,128)(2,1)S(1)}, bf16[256,1024]{1,0:T(8,128)(2,1)S(1)}, u32[]{:S(2)}, u32[]{:S(2)}) collective-permute-start(bf16[256,1024]{1,0:T(8,128)(2,1)S(1)} %collective-permute-done.2.refs_1_), channel_id=1, source_target_pairs={{1,3},{3,5},{5,7},{7,6},{6,4},{4,2},{2,0},{0,1},{9,11},{11,13},{13... | collective-permute-start | bytes 1572872 | tf_op jit(solution)/shard_map/ppermute | solution.py:349
  43.2 20.9 %collective-permute-start.7 = (bf16[256,1024]{1,0:T(8,128)(2,1)S(1)}, bf16[256,1024]{1,0:T(8,128)(2,1)S(1)}, u32[]{:S(2)}, u32[]{:S(2)}) collective-permute-start(bf16[256,1024]{1,0:T(8,128)(2,1)S(1)} %collective-permute-done.3.refs_2_), channel_id=1, source_target_pairs={{3,1},{5,3},{7,5},{6,7},{4,6},{2,4},{0,2},{1,0},{11,9},{13,11},{15... | collective-permute-start | bytes 1572872 | tf_op jit(solution)/shard_map/ppermute | solution.py:350
  52.9 20.5 %collective-permute-start.11 = (bf16[256,1024]{1,0:T(8,128)(2,1)S(1)}, bf16[256,1024]{1,0:T(8,128)(2,1)S(1)}, u32[]{:S(2)}, u32[]{:S(2)}) collective-permute-start(bf16[256,1024]{1,0:T(8,128)(2,1)S(1)} %collective-permute-done.8.refs_2_), channel_id=1, source_target_pairs={{1,3},{3,5},{5,7},{7,6},{6,4},{4,2},{2,0},{0,1},{9,11},{11,13},{13... | collective-permute-start | bytes 1572872 | tf_op jit(solution)/shard_map/ppermute | solution.py:349
  54.5 20.9 %collective-permute-start.12 = (bf16[256,1024]{1,0:T(8,128)(2,1)S(1)}, bf16[256,1024]{1,0:T(8,128)(2,1)S(1)}, u32[]{:S(2)}, u32[]{:S(2)}) collective-permute-start(bf16[256,1024]{1,0:T(8,128)(2,1)S(1)} %collective-permute-done.9.refs_1_), channel_id=1, source_target_pairs={{3,1},{5,3},{7,5},{6,7},{4,6},{2,4},{0,2},{1,0},{11,9},{13,11},{15... | collective-permute-start | bytes 1572872 | tf_op jit(solution)/shard_map/ppermute | solution.py:350
  64.1 19.6 %collective-permute-start.13 = (bf16[256,1024]{1,0:T(8,128)(2,1)S(1)}, bf16[256,1024]{1,0:T(8,128)(2,1)S(1)}, u32[]{:S(2)}, u32[]{:S(2)}) collective-permute-start(bf16[256,1024]{1,0:T(8,128)(2,1)S(1)} %collective-permute-done.6.refs_1_), channel_id=1, source_target_pairs={{1,3},{3,5},{5,7},{7,6},{6,4},{4,2},{2,0},{0,1},{9,11},{11,13},{13... | collective-permute-start | bytes 1572872 | tf_op jit(solution)/shard_map/ppermute | solution.py:349
  65.7 19.6 %collective-permute-start.10 = (bf16[256,1024]{1,0:T(8,128)(2,1)S(1)}, bf16[256,1024]{1,0:T(8,128)(2,1)S(1)}, u32[]{:S(2)}, u32[]{:S(2)}) collective-permute-start(bf16[256,1024]{1,0:T(8,128)(2,1)S(1)} %collective-permute-done.7.refs_2_), channel_id=1, source_target_pairs={{3,1},{5,3},{7,5},{6,7},{4,6},{2,4},{0,2},{1,0},{11,9},{13,11},{15... | collective-permute-start | bytes 1572872 | tf_op jit(solution)/shard_map/ppermute | solution.py:350
  83.8 16.0 %slice-start = ((s8[12582912]{0:T(1024)(128)(4,1)}), s8[4194304]{0:T(1024)(128)(4,1)S(1)}, s32[]{:S(2)}) async-start(s8[12582912]{0:T(1024)(128)(4,1)} %bitcast.23), calls=%async_computation | async-start | bytes 8388608
  85.4 14.4 %slice-start.1 = ((s8[12582912]{0:T(1024)(128)(4,1)}), s8[4194304]{0:T(1024)(128)(4,1)S(1)}, s32[]{:S(2)}) async-start(s8[12582912]{0:T(1024)(128)(4,1)} %bitcast.23), calls=%async_computation.1 | async-start | bytes 8388608
  87.0 7.7 %collective-permute-start.14 = (bf16[6,128,128]{2,1,0:T(8,128)(2,1)S(1)}, bf16[6,128,128]{2,1,0:T(8,128)(2,1)S(1)}, u32[]{:S(2)}, u32[]{:S(2)}) collective-permute-start(bf16[6,128,128]{2,1,0:T(8,128)(2,1)S(1)} %get-tuple-element.251), channel_id=1, source_target_pairs={{0,16},{8,24},{1,17},{9,25},{2,18},{10,26},{3,19},{11,27},{4,20},{... | collective-permute-start | bytes 589832 | tf_op jit(solution)/shard_map/ppermute | solution.py:385
  90.8 5.5 %copy-start = (f32[6,128,128]{2,1,0:T(8,128)S(1)}, f32[6,128,128]{2,1,0:T(8,128)}, u32[]{:S(2)}) copy-start(f32[6,128,128]{2,1,0:T(8,128)} %carry.1) | copy-start | bytes 1179652
  90.8 9.0 %slice-start.2 = ((s8[12582912]{0:T(1024)(128)(4,1)}), s8[4194304]{0:T(1024)(128)(4,1)S(1)}, s32[]{:S(2)}) async-start(s8[12582912]{0:T(1024)(128)(4,1)} %bitcast.23), calls=%async_computation.2 | async-start | bytes 8388608
  94.8 1.5 collective-permute-start.15
  97.7 14.8 %collective-permute-start.26 = (bf16[256,1024]{1,0:T(8,128)(2,1)S(1)}, bf16[256,1024]{1,0:T(8,128)(2,1)S(1)}, u32[]{:S(2)}, u32[]{:S(2)}) collective-permute-start(bf16[256,1024]{1,0:T(8,128)(2,1)S(1)} %get-tuple-element.276), channel_id=1, source_target_pairs={{3,1},{5,3},{7,5},{6,7},{4,6},{2,4},{0,2},{1,0},{11,9},{13,11},{15... | collective-permute-start | bytes 1572872 | tf_op jit(solution)/shard_map/ppermute | solution.py:404
  99.3 15.6 %collective-permute-start.22 = (bf16[256,1024]{1,0:T(8,128)(2,1)S(1)}, bf16[256,1024]{1,0:T(8,128)(2,1)S(1)}, u32[]{:S(2)}, u32[]{:S(2)}) collective-permute-start(bf16[256,1024]{1,0:T(8,128)(2,1)S(1)} %get-tuple-element.275), channel_id=1, source_target_pairs={{1,3},{3,5},{5,7},{7,6},{6,4},{4,2},{2,0},{0,1},{9,11},{11,13},{13... | collective-permute-start | bytes 1572872 | tf_op jit(solution)/shard_map/ppermute | solution.py:403
  100.6 24.8 %collective-permute-start.19 = (bf16[256,1024]{1,0:T(8,128)(2,1)S(1)}, bf16[256,1024]{1,0:T(8,128)(2,1)S(1)}, u32[]{:S(2)}, u32[]{:S(2)}) collective-permute-start(bf16[256,1024]{1,0:T(8,128)(2,1)S(1)} %fusion.97), channel_id=1, source_target_pairs={{1,3},{3,5},{5,7},{7,6},{6,4},{4,2},{2,0},{0,1},{9,11},{11,13},{13... | collective-permute-start | bytes 1572872 | tf_op jit(solution)/shard_map/ppermute | solution.py:411
  102.9 23.8 %collective-permute-start.16 = (bf16[256,1024]{1,0:T(8,128)(2,1)S(1)}, bf16[256,1024]{1,0:T(8,128)(2,1)S(1)}, u32[]{:S(2)}, u32[]{:S(2)}) collective-permute-start(bf16[256,1024]{1,0:T(8,128)(2,1)S(1)} %fusion.94), channel_id=1, source_target_pairs={{3,1},{5,3},{7,5},{6,7},{4,6},{2,4},{0,2},{1,0},{11,9},{13,11},{15... | collective-permute-start | bytes 1572872 | tf_op jit(solution)/shard_map/ppermute | solution.py:411
  113.3 21.7 %collective-permute-start.27 = (bf16[256,1024]{1,0:T(8,128)(2,1)S(1)}, bf16[256,1024]{1,0:T(8,128)(2,1)S(1)}, u32[]{:S(2)}, u32[]{:S(2)}) collective-permute-start(bf16[256,1024]{1,0:T(8,128)(2,1)S(1)} %fusion.79), channel_id=1, source_target_pairs={{3,1},{5,3},{7,5},{6,7},{4,6},{2,4},{0,2},{1,0},{11,9},{13,11},{15... | collective-permute-start | bytes 1572872 | tf_op jit(solution)/shard_map/ppermute | solution.py:411
  115.8 21.7 %collective-permute-start.23 = (bf16[256,1024]{1,0:T(8,128)(2,1)S(1)}, bf16[256,1024]{1,0:T(8,128)(2,1)S(1)}, u32[]{:S(2)}, u32[]{:S(2)}) collective-permute-start(bf16[256,1024]{1,0:T(8,128)(2,1)S(1)} %fusion.64), channel_id=1, source_target_pairs={{1,3},{3,5},{5,7},{7,6},{6,4},{4,2},{2,0},{0,1},{9,11},{11,13},{13... | collective-permute-start | bytes 1572872 | tf_op jit(solution)/shard_map/ppermute | solution.py:411
  126.2 21.7 %collective-permute-start.20 = (bf16[256,1024]{1,0:T(8,128)(2,1)S(1)}, bf16[256,1024]{1,0:T(8,128)(2,1)S(1)}, u32[]{:S(2)}, u32[]{:S(2)}) collective-permute-start(bf16[256,1024]{1,0:T(8,128)(2,1)S(1)} %fusion.70), channel_id=1, source_target_pairs={{1,3},{3,5},{5,7},{7,6},{6,4},{4,2},{2,0},{0,1},{9,11},{11,13},{13... | collective-permute-start | bytes 1572872 | tf_op jit(solution)/shard_map/ppermute | solution.py:411
  127.5 21.7 %collective-permute-start.17 = (bf16[256,1024]{1,0:T(8,128)(2,1)S(1)}, bf16[256,1024]{1,0:T(8,128)(2,1)S(1)}, u32[]{:S(2)}, u32[]{:S(2)}) collective-permute-start(bf16[256,1024]{1,0:T(8,128)(2,1)S(1)} %fusion.85), channel_id=1, source_target_pairs={{3,1},{5,3},{7,5},{6,7},{4,6},{2,4},{0,2},{1,0},{11,9},{13,11},{15... | collective-permute-start | bytes 1572872 | tf_op jit(solution)/shard_map/ppermute | solution.py:411
  135.8 21.7 %collective-permute-start.28 = (bf16[256,1024]{1,0:T(8,128)(2,1)S(1)}, bf16[256,1024]{1,0:T(8,128)(2,1)S(1)}, u32[]{:S(2)}, u32[]{:S(2)}) collective-permute-start(bf16[256,1024]{1,0:T(8,128)(2,1)S(1)} %fusion.82), channel_id=1, source_target_pairs={{3,1},{5,3},{7,5},{6,7},{4,6},{2,4},{0,2},{1,0},{11,9},{13,11},{15... | collective-permute-start | bytes 1572872 | tf_op jit(solution)/shard_map/ppermute | solution.py:411
  138.3 21.7 %collective-permute-start.24 = (bf16[256,1024]{1,0:T(8,128)(2,1)S(1)}, bf16[256,1024]{1,0:T(8,128)(2,1)S(1)}, u32[]{:S(2)}, u32[]{:S(2)}) collective-permute-start(bf16[256,1024]{1,0:T(8,128)(2,1)S(1)} %fusion.67), channel_id=1, source_target_pairs={{1,3},{3,5},{5,7},{7,6},{6,4},{4,2},{2,0},{0,1},{9,11},{11,13},{13... | collective-permute-start | bytes 1572872 | tf_op jit(solution)/shard_map/ppermute | solution.py:411
  148.7 21.7 %collective-permute-start.21 = (bf16[256,1024]{1,0:T(8,128)(2,1)S(1)}, bf16[256,1024]{1,0:T(8,128)(2,1)S(1)}, u32[]{:S(2)}, u32[]{:S(2)}) collective-permute-start(bf16[256,1024]{1,0:T(8,128)(2,1)S(1)} %fusion.76), channel_id=1, source_target_pairs={{1,3},{3,5},{5,7},{7,6},{6,4},{4,2},{2,0},{0,1},{9,11},{11,13},{13... | collective-permute-start | bytes 1572872 | tf_op jit(solution)/shard_map/ppermute | solution.py:411
  150.0 21.1 %collective-permute-start.18 = (bf16[256,1024]{1,0:T(8,128)(2,1)S(1)}, bf16[256,1024]{1,0:T(8,128)(2,1)S(1)}, u32[]{:S(2)}, u32[]{:S(2)}) collective-permute-start(bf16[256,1024]{1,0:T(8,128)(2,1)S(1)} %fusion.91), channel_id=1, source_target_pairs={{3,1},{5,3},{7,5},{6,7},{4,6},{2,4},{0,2},{1,0},{11,9},{13,11},{15... | collective-permute-start | bytes 1572872 | tf_op jit(solution)/shard_map/ppermute | solution.py:411
  158.3 20.9 %collective-permute-start.29 = (bf16[256,1024]{1,0:T(8,128)(2,1)S(1)}, bf16[256,1024]{1,0:T(8,128)(2,1)S(1)}, u32[]{:S(2)}, u32[]{:S(2)}) collective-permute-start(bf16[256,1024]{1,0:T(8,128)(2,1)S(1)} %fusion.88), channel_id=1, source_target_pairs={{3,1},{5,3},{7,5},{6,7},{4,6},{2,4},{0,2},{1,0},{11,9},{13,11},{15... | collective-permute-start | bytes 1572872 | tf_op jit(solution)/shard_map/ppermute | solution.py:411
  160.7 19.7 %collective-permute-start.25 = (bf16[256,1024]{1,0:T(8,128)(2,1)S(1)}, bf16[256,1024]{1,0:T(8,128)(2,1)S(1)}, u32[]{:S(2)}, u32[]{:S(2)}) collective-permute-start(bf16[256,1024]{1,0:T(8,128)(2,1)S(1)} %fusion.73), channel_id=1, source_target_pairs={{1,3},{3,5},{5,7},{7,6},{6,4},{4,2},{2,0},{0,1},{9,11},{11,13},{13... | collective-permute-start | bytes 1572872 | tf_op jit(solution)/shard_map/ppermute | solution.py:411
